TPU v7x, 256 devices: a whole 4x4x8 slice. The times are simulated.
256 devices in a mesh: dom: 64 (over z, y, core), rep: 4 (over x).
Axes of the slice: x: 4, y: 4, z: 8, core: 2. Of those that a mesh axis runs over, the one named last changes fastest.
Arguments:
- node_features: bfloat16 [262144, 128], P(('rep', 'dom')), parts along dimension 0, may hold values from -6 to 6
- edge_features: bfloat16 [688128, 128], P(('rep', 'dom')), parts along dimension 0, may hold values from -6 to 6
- node_cotangent: bfloat16 [262144, 128], P(('rep', 'dom')), parts along dimension 0, may hold values from -6 to 6
- edge_cotangent: bfloat16 [688128, 128], P(('rep', 'dom')), parts along dimension 0, may hold values from -6 to 6
- edge_in_weight: bfloat16 [384, 128], replicated, may hold values from -0.3125 to 0.3125
- edge_in_bias: float32 [128], replicated, may hold values from -3 to 3
- edge_out_weight: bfloat16 [128, 128], replicated, may hold values from -0.5 to 0.5
- edge_out_bias: float32 [128], replicated, may hold values from -3 to 3
- node_in_weight: bfloat16 [256, 128], replicated, may hold values from -0.375 to 0.375
- node_in_bias: float32 [128], replicated, may hold values from -3 to 3
- node_out_weight: bfloat16 [128, 128], replicated, may hold values from -0.5 to 0.5
- edge_ends: int32 [2, 1344], replicated, may hold values from 0 to 511, as said below
- live_elements: int32 [256], P(('rep', 'dom')), parts along dimension 0, may hold values from 1 to 2, as said below
- shared_nodes: int32 [256, 4, 128], P(('rep', 'dom')), parts along dimension 0, may hold values from 0 to 1023, as said below
- shared_counts: int32 [256, 4], P(('rep', 'dom')), parts along dimension 0, may hold values from 32 to 128, as said below
- multiplicity: int32 [262144], P(('rep', 'dom')), parts along dimension 0, may hold values from 1 to 515
Outputs:
- node_gradient: bfloat16 [262144, 128], P(('rep', 'dom')), parts along dimension 0
- edge_gradient: bfloat16 [688128, 128], P(('rep', 'dom')), parts along dimension 0
- edge_in_weight_gradient: float32 [1536, 128], P('rep'), parts along dimension 0
- edge_in_bias_gradient: float32 [512], P('rep'), parts along dimension 0
- edge_out_weight_gradient: float32 [512, 128], P('rep'), parts along dimension 0
- edge_out_bias_gradient: float32 [512], P('rep'), parts along dimension 0
- node_in_weight_gradient: float32 [1024, 128], P('rep'), parts along dimension 0
- node_in_bias_gradient: float32 [512], P('rep'), parts along dimension 0
- node_out_weight_gradient: float32 [512, 128], P('rep'), parts along dimension 0
- node_out_bias_gradient: float32 [512], P('rep'), parts along dimension 0
There are 4 independent parts, one for each index of `rep`. A program takes and returns all parts, laid end to end along the dimension named above; an argument that names none is the same for every part. Nothing has to cross between parts.
Inputs may be any that keep to these rules, and one draw needn't show every extreme that they name: `edge_ends`: each edge joins two nodes next to each other on the element's 8 x 8 x 8 lattice of nodes. `live_elements`: some partition has all 2 slots live. `shared_nodes`: entry s of a partition's list for neighbour k is the node paired with entry s of that neighbour's list for neighbour k xor 1; entries below the count name nodes of live slots; entries at or beyond it are 0. `shared_counts`: both lists of a pair have the same count; some pair has 128 entries.
All inputs are finite; a program needn't handle non-finite values.
Results may differ from a plain program's by a relative error of at most 0.0056.
Values sent between devices are 32-bit elements; how exact they have to be, the bound alone decides.
No kernel may reach another device: no remote copies, remote signals or barrier semaphores. Data moves between devices by JAX's collectives and lax.ppermute only.
A program may use at most 64 MiB of HBM per device.

v0:
```python
import math

import jax
import jax.numpy as jnp
from jax import lax
from jax.sharding import PartitionSpec as P

NPE = 512


def shifted(value, axis, steps):
    count = lax.axis_size(axis)
    pairs = [(source, (source + steps) % count) for source in range(count)]
    return lax.ppermute(value, axis, pairs)


def in_blocks(value, dim, count):
    lengths = value.shape
    tiles = value.reshape(*lengths[:dim], count, lengths[dim] // count, *lengths[dim + 1 :])
    return jnp.moveaxis(tiles, dim, 0)


def sent_and_summed(value, axis, dim):
    tiles = in_blocks(value, dim, lax.axis_size(axis))
    arrived = lax.all_to_all(tiles, axis, split_axis=0, concat_axis=0, tiled=True)
    return arrived.sum(axis=0)


def copy_for_each(value, axis):
    copies = jnp.broadcast_to(value, (lax.axis_size(axis), *value.shape))
    return lax.all_to_all(copies, axis, split_axis=0, concat_axis=0, tiled=True)


def joined_along(tiles, dim):
    tiles = jnp.moveaxis(tiles, 0, dim)
    lengths = tiles.shape
    return tiles.reshape(*lengths[:dim], lengths[dim] * lengths[dim + 1], *lengths[dim + 2 :])


def collect_2(value, axis, dim):
    tiles = copy_for_each(value, axis)
    return joined_along(tiles, dim)


def silu_slope(linear):
    squashed = jax.nn.sigmoid(linear)
    return squashed * (1.0 + linear * (1.0 - squashed))


def contract_rows(left, right):
    return lax.dot_general(
        left, right, (((0,), (0,)), ((), ())), preferred_element_type=jnp.float32
    )


def pick_rows(table, blocks):
    return jnp.einsum("jn,gnd->gjd", table, blocks, preferred_element_type=jnp.float32)


def pick_exact(table, blocks):
    return jnp.einsum(
        "jn,gnd->gjd",
        table,
        blocks,
        preferred_element_type=jnp.float32,
        precision=lax.Precision.HIGHEST,
    )


def spread_rows(table, grouped):
    return jnp.einsum(
        "jn,gjd->gnd",
        table,
        grouped,
        preferred_element_type=jnp.float32,
        precision=lax.Precision.HIGHEST,
    )


def edge_forward(
    blocks, edge_rows, tables, edge_in_weight, edge_in_bias, edge_out_weight, edge_out_bias
):
    feature_width = blocks.shape[2]
    source = pick_rows(tables[0], blocks).astype(jnp.bfloat16).reshape(-1, feature_width)
    target = pick_rows(tables[1], blocks).astype(jnp.bfloat16).reshape(-1, feature_width)
    joined = jnp.concatenate([source, target, edge_rows], axis=1)
    edge_linear = jnp.dot(joined, edge_in_weight, preferred_element_type=jnp.float32) + edge_in_bias
    edge_hidden = jax.nn.silu(edge_linear).astype(jnp.bfloat16)
    new_edges = (
        edge_rows.astype(jnp.float32)
        + jnp.dot(edge_hidden, edge_out_weight, preferred_element_type=jnp.float32)
        + edge_out_bias
    )
    return (joined, edge_linear, edge_hidden, new_edges)


def collect(new_edges, tables, slot_count):
    feature_width = new_edges.shape[1]
    grouped = new_edges.reshape(slot_count, -1, feature_width)
    return spread_rows(tables[3], grouped)


def edge_backward(
    joined, edge_linear, edge_hidden, edge_cot, tables, edge_in_weight, edge_out_weight, slot_count
):
    feature_width = edge_cot.shape[1]
    cot_half = edge_cot.astype(jnp.bfloat16)
    out_weight_term = contract_rows(edge_hidden, cot_half)
    out_bias_term = jnp.sum(cot_half.astype(jnp.float32), axis=0)
    hidden_back = jnp.dot(cot_half, edge_out_weight.T, preferred_element_type=jnp.float32)
    edge_back = (hidden_back * silu_slope(edge_linear)).astype(jnp.bfloat16)
    in_weight_term = contract_rows(joined, edge_back)
    in_bias_term = jnp.sum(edge_back.astype(jnp.float32), axis=0)
    joined_back = jnp.dot(edge_back, edge_in_weight.T, preferred_element_type=jnp.float32)
    from_source = joined_back[:, :feature_width].reshape(slot_count, -1, feature_width)
    from_target = joined_back[:, feature_width : 2 * feature_width].reshape(
        slot_count, -1, feature_width
    )
    block_back = spread_rows(tables[2], from_source) + spread_rows(tables[3], from_target)
    edge_result = (edge_cot + joined_back[:, 2 * feature_width :]).astype(jnp.bfloat16)
    return (block_back, edge_result, (in_weight_term, in_bias_term, out_weight_term, out_bias_term))


def body(
    node_features,
    edge_features,
    node_cotangent,
    edge_cotangent,
    edge_in_weight,
    edge_in_bias,
    edge_out_weight,
    edge_out_bias,
    node_in_weight,
    node_in_bias,
    node_out_weight,
    edge_ends,
    live_elements,
    shared_nodes,
    shared_counts,
    multiplicity,
):
    element_nodes = NPE
    feature_width = node_features.shape[1]
    slot_count = node_features.shape[0] // element_nodes
    element_edges = edge_ends.shape[1]
    devices = lax.axis_size("dom")
    quarter = devices // 4
    offsets = (1, -1, quarter, -quarter)
    node_iota = lax.iota(jnp.int32, element_nodes)[None, :]
    source_hit = edge_ends[0][:, None] == node_iota
    target_hit = edge_ends[1][:, None] == node_iota
    tables = (
        source_hit.astype(jnp.bfloat16),
        target_hit.astype(jnp.bfloat16),
        source_hit.astype(jnp.float32),
        target_hit.astype(jnp.float32),
    )
    live_count = live_elements[0]
    node_live = lax.iota(jnp.int32, node_features.shape[0]) // element_nodes < live_count
    edge_live = lax.iota(jnp.int32, edge_features.shape[0]) // element_edges < live_count
    node_cot = jnp.where(node_live[:, None], node_cotangent, jnp.zeros_like(node_cotangent))
    edge_given = jnp.where(
        edge_live[:, None],
        edge_cotangent.astype(jnp.float32),
        jnp.zeros((1, feature_width), jnp.float32),
    )
    share_lists = shared_nodes[0]
    entry_valid = lax.iota(jnp.int32, share_lists.shape[1])[None, :] < shared_counts[0][:, None]

    def partner_sum(values):
        outgoing = jnp.where(
            entry_valid[:, :, None],
            values[share_lists],
            jnp.zeros((1, 1, feature_width), jnp.float32),
        )
        running = values
        for neighbour in range(4):
            incoming = shifted(outgoing[neighbour ^ 1], "dom", -offsets[neighbour])
            masked = jnp.where(
                entry_valid[neighbour][:, None],
                incoming,
                jnp.zeros((1, feature_width), jnp.float32),
            )
            running = running.at[share_lists[neighbour]].add(masked)
        return running

    blocks = node_features.reshape(slot_count, element_nodes, feature_width)
    weight_args = (edge_in_weight, edge_in_bias, edge_out_weight, edge_out_bias)
    joined, edge_linear, edge_hidden, new_edges = edge_forward(
        blocks, edge_features, tables, *weight_args
    )
    aggregate = collect(new_edges, tables, slot_count).reshape(-1, feature_width)
    copies = multiplicity[:, None].astype(jnp.float32)
    consistent = partner_sum(aggregate) / copies
    node_input = jnp.concatenate([node_features, consistent.astype(jnp.bfloat16)], axis=1)
    node_linear = (
        jnp.dot(node_input, node_in_weight, preferred_element_type=jnp.float32) + node_in_bias
    )
    node_hidden = jax.nn.silu(node_linear).astype(jnp.bfloat16)
    node_out_term = contract_rows(node_hidden, node_cot)
    node_out_bias_term = jnp.sum(node_cot.astype(jnp.float32), axis=0)
    hidden_back = jnp.dot(node_cot, node_out_weight.T, preferred_element_type=jnp.float32)
    node_back = (hidden_back * silu_slope(node_linear)).astype(jnp.bfloat16)
    node_in_term = contract_rows(node_input, node_back)
    node_in_bias_term = jnp.sum(node_back.astype(jnp.float32), axis=0)
    node_input_back = jnp.dot(node_back, node_in_weight.T, preferred_element_type=jnp.float32)
    consistent_back = node_input_back[:, feature_width:] / copies
    aggregate_back = partner_sum(consistent_back)
    gathered_back = pick_exact(
        tables[3], aggregate_back.reshape(slot_count, element_nodes, feature_width)
    ).reshape(-1, feature_width)
    edge_cot = edge_given + gathered_back
    block_back, edge_result, edge_terms = edge_backward(
        joined,
        edge_linear,
        edge_hidden,
        edge_cot,
        tables,
        edge_in_weight,
        edge_out_weight,
        slot_count,
    )
    pieces = (
        edge_terms[0],
        edge_terms[1],
        edge_terms[2],
        edge_terms[3],
        node_in_term,
        node_in_bias_term,
        node_out_term,
        node_out_bias_term,
    )
    lengths = [piece.size for piece in pieces]
    total_length = sum(lengths)
    padded_length = -(-total_length // devices) * devices
    flat_terms = jnp.concatenate(
        [piece.reshape(-1) for piece in pieces]
        + [jnp.zeros((padded_length - total_length,), jnp.float32)]
    )
    share_sums = sent_and_summed(flat_terms, "dom", 0)
    flat_sums = collect_2(share_sums, "dom", 0)
    summed = []
    cursor = 0
    for piece, length in zip(pieces, lengths):
        summed.append(flat_sums[cursor : cursor + length].reshape(piece.shape))
        cursor = cursor + length
    edge_scale = 1.0 / math.sqrt(edge_features.shape[0] * devices)
    node_scale = 1.0 / math.sqrt(node_features.shape[0] * devices)
    node_result = (
        node_cot.astype(jnp.float32)
        + node_input_back[:, :feature_width]
        + block_back.reshape(-1, feature_width)
    ).astype(jnp.bfloat16)
    return (
        node_result,
        edge_result,
        summed[0] * edge_scale,
        summed[1] * edge_scale,
        summed[2] * edge_scale,
        summed[3] * edge_scale,
        summed[4] * node_scale,
        summed[5] * node_scale,
        summed[6] * node_scale,
        summed[7] * node_scale,
    )


def solution(mesh):
    in_specs = (
        P(("rep", "dom"), None),
        P(("rep", "dom"), None),
        P(("rep", "dom"), None),
        P(("rep", "dom"), None),
        P(),
        P(),
        P(),
        P(),
        P(),
        P(),
        P(),
        P(),
        P(("rep", "dom")),
        P(("rep", "dom"), None, None),
        P(("rep", "dom"), None),
        P(("rep", "dom")),
    )
    out_specs = (
        P(("rep", "dom"), None),
        P(("rep", "dom"), None),
        P("rep", None),
        P("rep"),
        P("rep", None),
        P("rep"),
        P("rep", None),
        P("rep"),
        P("rep", None),
        P("rep"),
    )
    return jax.shard_map(body, mesh=mesh, in_specs=in_specs, out_specs=out_specs, check_vma=False)
```

profile of v0, /device:TPU:1, one launch (start us, length us, event | category | flops | bytes accessed | tf_op | source)
XLA Modules:
  0.0 123.4 jit_solution(5282869609046977283)
XLA Ops:
  0.7 0.8 iota_compare_fusion.2
  1.4 0.7 fusion.83
  2.1 0.8 slice_reduce_fusion.1
  3.0 1.6 %fusion.20 = bf16[1344,2,128]{2,0,1:T(8,128)(2,1)S(1)} fusion(bf16[2,512,128]{2,1,0:T(8,128)(2,1)} %bitcast.133, s32[1344]{0:T(1024)S(1)} %get-tuple-element.10), kind=kOutput, calls=%fused_computation.29 | convolution fusion | flops 353353728 | bytes 955648 | tf_op jit(solution)/shard_map/jn,gnd->gjd/dot_general | solution.py:57
  4.6 0.6 fusion.17
  5.3 0.8 copy-done.17
  6.1 0.7 convolution_add_fusion
  6.9 0.5 fusion.1
  7.4 0.6 copy-done.19
  8.0 1.9 %fusion.36 = f32[2,512,128]{1,2,0:T(8,128)S(1)} fusion(f32[2,1344,128]{2,1,0:T(8,128)S(1)} %bitcast.136, s32[1344]{0:T(1024)S(1)} %get-tuple-element.11), kind=kOutput, calls=%fused_computation.48 | convolution fusion | flops 2114617344 | bytes 1905920 | tf_op jit(solution)/shard_map/jn,gjd->gnd/dot_general | solution.py:71
  9.9 0.2 copy.33
  10.1 1.0 gather_fusion
  11.3 3.9 %collective-permute-start.3 = (f32[128,128]{1,0:T(8,128)S(1)}, f32[128,128]{1,0:T(8,128)S(1)}, u32[]{:S(2)}, u32[]{:S(2)}) collective-permute-start(f32[128,128]{1,0:T(8,128)S(1)} %get-tuple-element.29), channel_id=1, source_target_pairs={{0,64},{4,68},{8,72},{12,76},{16,80},{20,84},{24,88},{28,92},{32,9... | collective-permute-start | bytes 196616 | tf_op jit(solution)/shard_map/ppermute | solution.py:14
  15.2 3.1 %collective-permute-start.2 = (f32[128,128]{1,0:T(8,128)S(1)}, f32[128,128]{1,0:T(8,128)S(1)}, u32[]{:S(2)}, u32[]{:S(2)}) collective-permute-start(f32[128,128]{1,0:T(8,128)S(1)} %get-tuple-element.30), channel_id=1, source_target_pairs={{0,192},{4,196},{8,200},{12,204},{16,208},{20,212},{24,216},{28,22... | collective-permute-start | bytes 196616 | tf_op jit(solution)/shard_map/ppermute | solution.py:14
  18.3 2.1 %collective-permute-start.1 = (f32[128,128]{1,0:T(8,128)S(1)}, f32[128,128]{1,0:T(8,128)S(1)}, u32[]{:S(2)}, u32[]{:S(2)}) collective-permute-start(f32[128,128]{1,0:T(8,128)S(1)} %get-tuple-element.31), channel_id=1, source_target_pairs={{0,4},{4,8},{8,12},{12,16},{16,20},{20,24},{24,28},{28,32},{32,36}... | collective-permute-start | bytes 196616 | tf_op jit(solution)/shard_map/ppermute | solution.py:14
  21.2 3.2 %collective-permute-done = f32[128,128]{1,0:T(8,128)S(1)} collective-permute-done((f32[128,128]{1,0:T(8,128)S(1)}, f32[128,128]{1,0:T(8,128)S(1)}, u32[]{:S(2)}, u32[]{:S(2)}) %collective-permute-start) | collective-permute-done | bytes 65568 | tf_op jit(solution)/shard_map/ppermute | solution.py:14
  24.5 1.6 %scatter_custom_fusion = f32[1024,128]{1,0:T(8,128)S(1)} fusion(f32[1024,128]{1,0:T(8,128)S(1)} %bitcast.127, s32[128]{0:T(128)S(1)} %get-tuple-element.35, f32[128,128]{1,0:T(8,128)S(1)} %collective-permute-done, f32[]{:T(128)} %constant.48.clone.1, pred[128]{0:T(512)(128)(4,1)S(1)} %get-tuple-element.40), kind=kCustom, calls=%fused_computation.92 | custom fusion | flops 32768 | bytes 590340 | tf_op jit(solution)/shard_map/scatter-add | solution.py:184
  26.1 1.7 %scatter_custom_fusion.1 = f32[1024,128]{1,0:T(8,128)S(1)} fusion(f32[1024,128]{1,0:T(8,128)S(1)} %scatter_custom_fusion, s32[128]{0:T(128)S(1)} %get-tuple-element.34, f32[128,128]{1,0:T(8,128)S(1)} %collective-permute-done.1, f32[]{:T(128)} %constant.48.clone.1, pred[128]{0:T(512)(128)(4,1)S(1)} %get-tuple-element.39), kind=kCustom, calls=%fused_computation.90 | custom fusion | flops 32768 | bytes 590340 | tf_op jit(solution)/shard_map/scatter-add | solution.py:184
  27.8 1.7 %scatter_custom_fusion.2 = f32[1024,128]{1,0:T(8,128)S(1)} fusion(f32[1024,128]{1,0:T(8,128)S(1)} %scatter_custom_fusion.1, s32[128]{0:T(128)S(1)} %get-tuple-element.36, f32[128,128]{1,0:T(8,128)S(1)} %collective-permute-done.2, f32[]{:T(128)} %constant.48.clone.1, pred[128]{0:T(512)(128)(4,1)S(1)} %get-tuple-element.38), kind=kCustom, calls=%fused_computation.88 | custom fusion | flops 32768 | bytes 590340 | tf_op jit(solution)/shard_map/scatter-add | solution.py:184
  29.5 1.8 %scatter_custom_fusion.3 = f32[1024,128]{1,0:T(8,128)S(1)} fusion(f32[1024,128]{1,0:T(8,128)S(1)} %scatter_custom_fusion.2, s32[128]{0:T(128)S(1)} %get-tuple-element.33, f32[128,128]{1,0:T(8,128)S(1)} %collective-permute-done.3, f32[]{:T(128)} %constant.48.clone.1, pred[128]{0:T(512)(128)(4,1)S(1)} %get-tuple-element.37), kind=kCustom, calls=%fused_computation.86 | custom fusion | flops 32768 | bytes 590340 | tf_op jit(solution)/shard_map/scatter-add | solution.py:184
  31.3 0.2 divide_convert_fusion
  31.5 0.3 convolution_add_fusion.2
  31.8 0.4 convolution_bitcast_fusion.2
  32.2 0.3 copy-done.9
  32.6 0.4 convert_reduce_fusion.3
  32.9 0.3 fusion.94
  33.2 0.2 slice_divide_fusion
  33.4 1.0 gather_fusion.1
  34.7 1.2 collective-permute-start.7
  35.9 2.4 %collective-permute-start.6 = (f32[128,128]{1,0:T(8,128)S(1)}, f32[128,128]{1,0:T(8,128)S(1)}, u32[]{:S(2)}, u32[]{:S(2)}) collective-permute-start(f32[128,128]{1,0:T(8,128)S(1)} %get-tuple-element.26), channel_id=1, source_target_pairs={{0,192},{4,196},{8,200},{12,204},{16,208},{20,212},{24,216},{28,22... | collective-permute-start | bytes 196616 | tf_op jit(solution)/shard_map/ppermute | solution.py:14
  38.3 2.4 %collective-permute-start.4 = (f32[128,128]{1,0:T(8,128)S(1)}, f32[128,128]{1,0:T(8,128)S(1)}, u32[]{:S(2)}, u32[]{:S(2)}) collective-permute-start(f32[128,128]{1,0:T(8,128)S(1)} %get-tuple-element.28), channel_id=1, source_target_pairs={{0,252},{4,0},{8,4},{12,8},{16,12},{20,16},{24,20},{28,24},{32,28}... | collective-permute-start | bytes 196616 | tf_op jit(solution)/shard_map/ppermute | solution.py:14
  40.7 0.3 convolution_bitcast_fusion.1
  41.1 1.3 %collective-permute-done.4 = f32[128,128]{1,0:T(8,128)S(1)} collective-permute-done((f32[128,128]{1,0:T(8,128)S(1)}, f32[128,128]{1,0:T(8,128)S(1)}, u32[]{:S(2)}, u32[]{:S(2)}) %collective-permute-start.4) | collective-permute-done | bytes 65568 | tf_op jit(solution)/shard_map/ppermute | solution.py:14
  42.3 1.6 %scatter_custom_fusion.4 = f32[1024,128]{1,0:T(8,128)S(1)} fusion(f32[1024,128]{1,0:T(8,128)S(1)} %slice_divide_fusion, s32[128]{0:T(128)S(1)} %get-tuple-element.35, f32[128,128]{1,0:T(8,128)S(1)} %collective-permute-done.4, f32[]{:T(128)} %constant.48.clone.1, pred[128]{0:T(512)(128)(4,1)S(1)} %get-tuple-element.40), kind=kCustom, calls=%fused_computation.84 | custom fusion | flops 32768 | bytes 590340 | tf_op jit(solution)/shard_map/scatter-add | solution.py:184
  43.9 1.7 %scatter_custom_fusion.5 = f32[1024,128]{1,0:T(8,128)S(1)} fusion(f32[1024,128]{1,0:T(8,128)S(1)} %scatter_custom_fusion.4, s32[128]{0:T(128)S(1)} %get-tuple-element.34, f32[128,128]{1,0:T(8,128)S(1)} %collective-permute-done.5, f32[]{:T(128)} %constant.48.clone.1, pred[128]{0:T(512)(128)(4,1)S(1)} %get-tuple-element.39), kind=kCustom, calls=%fused_computation.82 | custom fusion | flops 32768 | bytes 590340 | tf_op jit(solution)/shard_map/scatter-add | solution.py:184
  45.6 1.7 %scatter_custom_fusion.6 = f32[1024,128]{1,0:T(8,128)S(1)} fusion(f32[1024,128]{1,0:T(8,128)S(1)} %scatter_custom_fusion.5, s32[128]{0:T(128)S(1)} %get-tuple-element.36, f32[128,128]{1,0:T(8,128)S(1)} %collective-permute-done.6, f32[]{:T(128)} %constant.48.clone.1, pred[128]{0:T(512)(128)(4,1)S(1)} %get-tuple-element.38), kind=kCustom, calls=%fused_computation.80 | custom fusion | flops 32768 | bytes 590340 | tf_op jit(solution)/shard_map/scatter-add | solution.py:184
  47.3 1.8 %scatter_custom_fusion.7 = f32[1024,128]{1,0:T(8,128)S(1)} fusion(f32[1024,128]{1,0:T(8,128)S(1)} %scatter_custom_fusion.6, s32[128]{0:T(128)S(1)} %get-tuple-element.33, f32[128,128]{1,0:T(8,128)S(1)} %collective-permute-done.7, f32[]{:T(128)} %constant.48.clone.1, pred[128]{0:T(512)(128)(4,1)S(1)} %get-tuple-element.37), kind=kCustom, calls=%fused_computation.78 | custom fusion | flops 32768 | bytes 590340 | tf_op jit(solution)/shard_map/scatter-add | solution.py:184
  49.1 1.4 %fusion.11 = f32[2,128,1344]{1,2,0:T(8,128)S(1)} fusion(f32[2,512,128]{2,1,0:T(8,128)S(1)} %bitcast.128, s32[1344]{0:T(1024)S(1)} %get-tuple-element.11), kind=kOutput, calls=%fused_computation.25 | convolution fusion | flops 2114617344 | bytes 1905920 | tf_op jit(solution)/shard_map/jn,gnd->gjd/dot_general | solution.py:61
  50.6 1.5 %convert_reduce_fusion = (f32[128]{0:T(128)S(1)}, bf16[2688,128]{1,0:T(8,128)(2,1)S(1)}) fusion(f32[2,128,1344]{1,2,0:T(8,128)S(1)} %fusion.11, bf16[2688,128]{1,0:T(8,128)(2,1)S(1)} %copy-done.1, pred[2688]{0:T(1024)(128)(4,1)S(1)} %fusion.75), kind=kLoop, calls=%fused_computation.36 | loop fusion | flops 2064256 | bytes 2755712 | tf_op jit(solution)/shard_map/reduce_sum | solution.py:109
  52.0 0.6 convolution_bitcast_fusion.3
  52.6 0.2 copy-done.11
  52.8 0.6 convert_reduce_fusion.1
  53.4 0.5 copy-done.7
  53.9 0.2 copy-done.16
  54.1 0.2 copy-done.18
  54.3 0.7 fusion
  55.1 0.7 fusion.95
  55.8 2.3 %fusion.23 = (bf16[2688,128]{1,0:T(8,128)(2,1)}, f32[2688,128]{1,0:T(8,128)S(1)}, f32[2688,128]{1,0:T(8,128)S(1)}) fusion(f32[2688,384]{1,0:T(8,128)S(1)} %fusion.95, f32[2,128,1344]{1,2,0:T(8,128)S(1)} %fusion.11, bf16[2688,128]{1,0:T(8,128)(2,1)S(1)} %copy-done.1, pred[2688]{0:T(1024)(128)(4,1)S(1)} %fusion.75), kind=kLoop, calls=%fused_computation.34 | loop fusion | flops 1720320 | bytes 9636480 | tf_op jit(solution)/shard_map/convert_element_type | solution.py:120
  58.1 2.0 %fusion.4 = f32[2,128,512]{2,1,0:T(8,128)S(1)} fusion(f32[2,1344,128]{2,1,0:T(8,128)S(1)} %bitcast.130, s32[1344]{0:T(1024)S(1)} %get-tuple-element.10), kind=kOutput, calls=%fused_computation.21 | convolution fusion | flops 2114617344 | bytes 1905920 | tf_op jit(solution)/shard_map/jn,gjd->gnd/dot_general | solution.py:71
  60.0 2.0 %fusion.33 = f32[2,512,128]{1,2,0:T(8,128)S(1)} fusion(f32[2,128,512]{2,1,0:T(8,128)S(1)} %fusion.4, f32[2,1344,128]{2,1,0:T(8,128)S(1)} %bitcast.129, s32[1344]{0:T(1024)S(1)} %get-tuple-element.11), kind=kOutput, calls=%fused_computation.47 | convolution fusion | flops 2114748416 | bytes 2430208 | tf_op jit(solution)/shard_map/jn,gjd->gnd/dot_general | solution.py:71
  62.0 0.2 copy.34
  62.2 0.9 convert_reduce_fusion.2
  63.3 0.7 all_to_all.10
  64.0 31.5 %all_to_all.15 = f32[64,1,1800]{2,1,0:T(1,128)S(1)} all-to-all(f32[64,1,1800]{2,1,0:T(1,128)S(1)} %all_to_all.10), channel_id=1, replica_groups=mesh['dom'=64,'rep'=4] {'dom'}, dimensions={0} | all-to-all | bytes 921600 | tf_op jit(solution)/shard_map/all_to_all | solution.py:25
  95.5 0.3 reduce_sum.49
  95.9 0.3 broadcast_in_dim.159
  96.1 22.8 %all_to_all.16 = f32[64,1,1800]{2,1,0:T(1,128)S(1)} all-to-all(f32[64,1,1800]{2,1,0:T(1,128)S(1)} %broadcast_in_dim.159), channel_id=1, replica_groups=mesh['dom'=64,'rep'=4] {'dom'}, dimensions={0} | all-to-all | bytes 921600 | tf_op jit(solution)/shard_map/all_to_all | solution.py:31
  118.9 1.2 reduce.3
  120.1 0.3 slice.134
  120.5 0.3 reshape.311
  120.8 0.7 slice_multiply_fusion.1
  121.5 0.7 slice_multiply_fusion.2
  122.2 0.7 slice_multiply_fusion
  122.9 0.5 slice_multiply_fusion.4
  (60 shorter events, 0.6 us)
Async XLA Ops:
  0.6 5.5 %copy-start = (bf16[384,128]{1,0:T(8,128)(2,1)S(1)}, bf16[384,128]{1,0:T(8,128)(2,1)}, u32[]{:S(2)}) copy-start(bf16[384,128]{1,0:T(8,128)(2,1)} %param.20) | copy-start | bytes 294916
  0.7 3.9 %copy-start.8 = (bf16[1024,128]{1,0:T(8,128)(2,1)S(1)}, bf16[1024,128]{1,0:T(8,128)(2,1)}, u32[]{:S(2)}) copy-start(bf16[1024,128]{1,0:T(8,128)(2,1)} %param.16) | copy-start | bytes 786436
  4.6 2.3 %copy-start.15 = (bf16[1344,2,128]{2,0,1:T(8,128)(2,1)}, bf16[1344,2,128]{2,0,1:T(8,128)(2,1)S(1)}, u32[]{:S(2)}) copy-start(bf16[1344,2,128]{2,0,1:T(8,128)(2,1)S(1)} %fusion.20) | copy-start | bytes 2064388
  4.6 1.5 %copy-start.6 = (bf16[2688,128]{1,0:T(8,128)(2,1)S(1)}, bf16[2688,128]{1,0:T(8,128)(2,1)}, u32[]{:S(2)}) copy-start(bf16[2688,128]{1,0:T(8,128)(2,1)} %param.17) | copy-start | bytes 2064388
  4.6 1.5 %copy-start.12 = (f32[128]{0:T(128)S(1)}, f32[128]{0:T(128)}, u32[]{:S(2)}) copy-start(f32[128]{0:T(128)} %param.21) | copy-start | bytes 1540
  5.3 0.8 copy-start.17
  6.1 0.8 copy-start.10
  6.1 0.8 copy-start.13
  6.9 1.1 copy-start.19
  10.1 10.4 %copy-start.4 = (s32[1,4,128]{2,1,0:T(4,128)S(1)}, s32[1,4,128]{2,1,0:T(4,128)}, u32[]{:S(2)}) copy-start(s32[1,4,128]{2,1,0:T(4,128)} %param.29) | copy-start | bytes 6148
  10.1 11.1 %copy-start.5 = (s32[1024]{0:T(1024)S(1)}, s32[1024]{0:T(1024)}, u32[]{:S(2)}) copy-start(s32[1024]{0:T(1024)} %param.31) | copy-start | bytes 12292
  11.3 18.1 %collective-permute-start.3 = (f32[128,128]{1,0:T(8,128)S(1)}, f32[128,128]{1,0:T(8,128)S(1)}, u32[]{:S(2)}, u32[]{:S(2)}) collective-permute-start(f32[128,128]{1,0:T(8,128)S(1)} %get-tuple-element.29), channel_id=1, source_target_pairs={{0,64},{4,68},{8,72},{12,76},{16,80},{20,84},{24,88},{28,92},{32,9... | collective-permute-start | bytes 196616 | tf_op jit(solution)/shard_map/ppermute | solution.py:14
  15.2 12.5 %collective-permute-start.2 = (f32[128,128]{1,0:T(8,128)S(1)}, f32[128,128]{1,0:T(8,128)S(1)}, u32[]{:S(2)}, u32[]{:S(2)}) collective-permute-start(f32[128,128]{1,0:T(8,128)S(1)} %get-tuple-element.30), channel_id=1, source_target_pairs={{0,192},{4,196},{8,200},{12,204},{16,208},{20,212},{24,216},{28,22... | collective-permute-start | bytes 196616 | tf_op jit(solution)/shard_map/ppermute | solution.py:14
  18.3 7.7 %collective-permute-start.1 = (f32[128,128]{1,0:T(8,128)S(1)}, f32[128,128]{1,0:T(8,128)S(1)}, u32[]{:S(2)}, u32[]{:S(2)}) collective-permute-start(f32[128,128]{1,0:T(8,128)S(1)} %get-tuple-element.31), channel_id=1, source_target_pairs={{0,4},{4,8},{8,12},{12,16},{16,20},{20,24},{24,28},{28,32},{32,36}... | collective-permute-start | bytes 196616 | tf_op jit(solution)/shard_map/ppermute | solution.py:14
  20.5 4.0 %collective-permute-start = (f32[128,128]{1,0:T(8,128)S(1)}, f32[128,128]{1,0:T(8,128)S(1)}, u32[]{:S(2)}, u32[]{:S(2)}) collective-permute-start(f32[128,128]{1,0:T(8,128)S(1)} %get-tuple-element.32), channel_id=1, source_target_pairs={{0,252},{4,0},{8,4},{12,8},{16,12},{20,16},{24,20},{28,24},{32,28}... | collective-permute-start | bytes 196616 | tf_op jit(solution)/shard_map/ppermute | solution.py:14
  26.0 5.4 %copy-start.3 = (bf16[256,128]{1,0:T(8,128)(2,1)S(1)}, bf16[256,128]{1,0:T(8,128)(2,1)}, u32[]{:S(2)}) copy-start(bf16[256,128]{1,0:T(8,128)(2,1)} %param.24) | copy-start | bytes 196612
  26.0 5.4 %copy-start.14 = (f32[128]{0:T(128)S(1)}, f32[128]{0:T(128)}, u32[]{:S(2)}) copy-start(f32[128]{0:T(128)} %param.25) | copy-start | bytes 1540
  29.5 2.3 %copy-start.2 = (bf16[1024,128]{1,0:T(8,128)(2,1)S(1)}, bf16[1024,128]{1,0:T(8,128)(2,1)}, u32[]{:S(2)}) copy-start(bf16[1024,128]{1,0:T(8,128)(2,1)} %param.18) | copy-start | bytes 786436
  31.8 0.8 copy-start.9
  34.7 12.6 %collective-permute-start.7 = (f32[128,128]{1,0:T(8,128)S(1)}, f32[128,128]{1,0:T(8,128)S(1)}, u32[]{:S(2)}, u32[]{:S(2)}) collective-permute-start(f32[128,128]{1,0:T(8,128)S(1)} %get-tuple-element.25), channel_id=1, source_target_pairs={{0,64},{4,68},{8,72},{12,76},{16,80},{20,84},{24,88},{28,92},{32,9... | collective-permute-start | bytes 196616 | tf_op jit(solution)/shard_map/ppermute | solution.py:14
  35.9 9.7 %collective-permute-start.6 = (f32[128,128]{1,0:T(8,128)S(1)}, f32[128,128]{1,0:T(8,128)S(1)}, u32[]{:S(2)}, u32[]{:S(2)}) collective-permute-start(f32[128,128]{1,0:T(8,128)S(1)} %get-tuple-element.26), channel_id=1, source_target_pairs={{0,192},{4,196},{8,200},{12,204},{16,208},{20,212},{24,216},{28,22... | collective-permute-start | bytes 196616 | tf_op jit(solution)/shard_map/ppermute | solution.py:14
  38.3 5.6 %collective-permute-start.5 = (f32[128,128]{1,0:T(8,128)S(1)}, f32[128,128]{1,0:T(8,128)S(1)}, u32[]{:S(2)}, u32[]{:S(2)}) collective-permute-start(f32[128,128]{1,0:T(8,128)S(1)} %get-tuple-element.27), channel_id=1, source_target_pairs={{0,4},{4,8},{8,12},{12,16},{16,20},{20,24},{24,28},{28,32},{32,36}... | collective-permute-start | bytes 196616 | tf_op jit(solution)/shard_map/ppermute | solution.py:14
  38.3 4.0 %collective-permute-start.4 = (f32[128,128]{1,0:T(8,128)S(1)}, f32[128,128]{1,0:T(8,128)S(1)}, u32[]{:S(2)}, u32[]{:S(2)}) collective-permute-start(f32[128,128]{1,0:T(8,128)S(1)} %get-tuple-element.28), channel_id=1, source_target_pairs={{0,252},{4,0},{8,4},{12,8},{16,12},{20,16},{24,20},{28,24},{32,28}... | collective-permute-start | bytes 196616 | tf_op jit(solution)/shard_map/ppermute | solution.py:14
  47.3 3.3 %copy-start.1 = (bf16[2688,128]{1,0:T(8,128)(2,1)S(1)}, bf16[2688,128]{1,0:T(8,128)(2,1)}, u32[]{:S(2)}) copy-start(bf16[2688,128]{1,0:T(8,128)(2,1)} %param.19) | copy-start | bytes 2064388
  50.6 1.5 %copy-start.20 = (f32[2688,128]{1,0:T(8,128)S(1)}, f32[2688,128]{1,0:T(8,128)}, u32[]{:S(2)}) copy-start(f32[2688,128]{1,0:T(8,128)} %copy-done.19) | copy-start | bytes 4128772
  52.0 0.8 copy-start.11
  52.8 1.1 copy-start.7
  52.8 1.3 %copy-start.16 = (bf16[1344,2,128]{2,0,1:T(8,128)(2,1)S(1)}, bf16[1344,2,128]{2,0,1:T(8,128)(2,1)}, u32[]{:S(2)}) copy-start(bf16[1344,2,128]{2,0,1:T(8,128)(2,1)} %copy-done.15) | copy-start | bytes 2064388
  52.8 1.5 %copy-start.18 = (bf16[1344,2,128]{2,0,1:T(8,128)(2,1)S(1)}, bf16[1344,2,128]{2,0,1:T(8,128)(2,1)}, u32[]{:S(2)}) copy-start(bf16[1344,2,128]{2,0,1:T(8,128)(2,1)} %copy-done.17) | copy-start | bytes 2064388
where the time goes:
time: 124 us; the launch traced here: 123 us
  blocking collectives  54.3 us (44%)
  other arithmetic  24.4 us (20%)
  starting transfers between devices  15.2 us (12%)
  matrix products  15.1 us (12%)
  local copies, waits for them, and re-layouts  7.96 us (6%)
  waiting for transfers between devices  4.51 us (4%)
  between operations  1.92 us (2%)
    all_to_all x1, blocking collectives, sent_and_summed(): lax.all_to_all(tiles, axis, split_axis=0, concat_axis=0, tiled=True)  31.5 us
    all_to_all x1, blocking collectives, copy_for_each(): return lax.all_to_all(copies, axis, split_axis=0, concat_axis=0, tiled=True)  22.8 us
    ppermute x8, starting transfers between devices, shifted(): return lax.ppermute(value, axis, pairs)  15.2 us
    scatter-add x8, other arithmetic, partner_sum(): running = running.at[share_lists[neighbour]].add(masked)  13.4 us
    dot_general x3, matrix products, spread_rows(): jnp.einsum('jn,gjd->gnd', table, grouped, preferred_element_type=jnp.floa...  5.85 us
    ppermute x8, waiting for transfers between devices, shifted(): return lax.ppermute(value, axis, pairs)  4.51 us
    unnamed x48, local copies, waits for them, and re-layouts  2.97 us
  transfers between devices with their start and end apart: 8, of which 2 were waited for; matrix products, arithmetic and copies ran while one was open for 8% of the time, Pallas kernels for 0%

commit v1 on v0

v1 whole, which is shorter than its diff:
```python
import math

import jax
import jax.numpy as jnp
from jax import lax
from jax.experimental import pallas as pl
from jax.experimental.pallas import tpu as pltpu
from jax.sharding import Mesh, PartitionSpec as P

NPE = 512
LANES = 128
BLOCK = 256
F32 = jnp.float32
BF16 = jnp.bfloat16
AXES = ("z", "y", "c")
VMEM = pl.BlockSpec(memory_space=pltpu.VMEM)
SMEM = pl.BlockSpec(memory_space=pltpu.SMEM)


def padded(count):
    return -(-count // LANES) * LANES


def dot(left, right):
    return jnp.dot(left, right, preferred_element_type=F32)


def dot_t(left, right):
    return lax.dot_general(left, right, (((1,), (1,)), ((), ())), preferred_element_type=F32)


def dot_rows(left, right):
    return lax.dot_general(left, right, (((0,), (0,)), ((), ())), preferred_element_type=F32)


def split(value):
    high = value.astype(BF16)
    low = (value - high.astype(F32)).astype(BF16)
    return high, low


def as_column(row):
    return jnp.transpose(jnp.broadcast_to(row, (LANES, LANES)))


def hot(flags):
    return jnp.where(flags, 1.0, 0.0).astype(BF16)


def pick_table(row, width):
    column = as_column(row)
    lane = lax.broadcasted_iota(jnp.int32, (LANES, LANES), 1)
    tiles = [hot(column == lane + start) for start in range(0, width, LANES)]
    return jnp.concatenate(tiles, axis=1)


def spread_table(row, height):
    return hot(lax.broadcasted_iota(jnp.int32, (height, row.shape[1]), 0) == row)


def list_rows(lists_ref, counts_ref):
    core = lax.axis_index("c")
    odd = lax.rem(lax.div(lax.axis_index("z"), 2), 2)
    lane = lax.broadcasted_iota(jnp.int32, (1, LANES), 1)
    rows = [jnp.where(lane < counts_ref[0, k], lists_ref[k : k + 1, :], -1) for k in range(4)]

    def ordered(flag, first, second):
        chosen = jnp.full((1, LANES), flag, jnp.int32) == 0
        return jnp.where(chosen, first, second), jnp.where(chosen, second, first)

    return ordered(core, rows[0], rows[1]) + ordered(odd, rows[2], rows[3])


def outgoing(rows, values, refs):
    table = jnp.concatenate([pick_table(row, values.shape[0]) for row in rows], axis=0)
    both = dot(table, jnp.concatenate(split(values), axis=1))
    for k, ref in enumerate(refs):
        part = both[k * LANES : (k + 1) * LANES]
        ref[...] = part[:, :LANES] + part[:, LANES:]


def incoming(rows, refs, height):
    table = jnp.concatenate([spread_table(row, height) for row in rows], axis=1)
    arrived = jnp.concatenate([ref[...] for ref in refs], axis=0)
    both = dot(table, jnp.concatenate(split(arrived), axis=1))
    return both[:, :LANES] + both[:, LANES:]


def blocks_of(count):
    return [(start, min(BLOCK, count - start)) for start in range(0, count, BLOCK)]


def stage_ends(ends_ref, ends_sc):
    ends_sc[...] = jnp.full(ends_sc.shape, -1, jnp.int32)
    ends_sc[0:2, 0 : ends_ref.shape[1]] = ends_ref[...]


def edge_rows_table(ends_sc, side, start, size):
    parts = [
        pick_table(ends_sc[side : side + 1, first : first + LANES], NPE)
        for first in range(start, start + size, LANES)
    ]
    return jnp.concatenate(parts, axis=0)[:size]


def forward_kernel(
    counts_ref, ends_ref, lists_ref, nf_ref, ef_ref, wi_ref, bi_ref, wo_ref, bo_ref,
    agg_ref, out0, out1, out2, out3, hid_ref, slope_ref,
    ends_sc, rows_sc, spread_sc,
):
    edges = ends_ref.shape[1]
    width = padded(edges)
    stage_ends(ends_ref, ends_sc)
    nf = nf_ref[...]
    from_source = dot(nf, wi_ref[0:128, :]).astype(BF16)
    from_target = dot(nf, wi_ref[128:256, :]).astype(BF16)
    table_rows = jnp.concatenate(
        [
            jnp.concatenate([from_source[:NPE], from_source[NPE:]], axis=1),
            jnp.concatenate([from_target[:NPE], from_target[NPE:]], axis=1),
        ],
        axis=0,
    )
    for start, size in blocks_of(edges):
        table = jnp.concatenate(
            [
                edge_rows_table(ends_sc, 0, start, size),
                edge_rows_table(ends_sc, 1, start, size),
            ],
            axis=1,
        )
        ends_part = dot(table, table_rows)
        for slot in range(2):
            first = slot * edges + start
            own = ef_ref[first : first + size, :]
            linear = (
                ends_part[:, slot * LANES : (slot + 1) * LANES]
                + dot(own, wi_ref[256:384, :])
                + bi_ref[...]
            )
            squashed = jax.nn.sigmoid(linear)
            hidden = (linear * squashed).astype(BF16)
            hid_ref[first : first + size, :] = hidden
            slope_ref[first : first + size, :] = squashed * (1.0 + linear * (1.0 - squashed))
            rows_sc[start : start + size, slot * LANES : (slot + 1) * LANES] = own
            rows_sc[start : start + size, (2 + slot) * LANES : (3 + slot) * LANES] = hidden
    rows_sc[edges:width, :] = jnp.zeros((width - edges, 4 * LANES), BF16)
    degree = jnp.zeros((NPE, LANES), F32)
    for first in range(0, width, LANES):
        table = spread_table(ends_sc[1:2, first : first + LANES], NPE)
        spread_sc[:, first : first + LANES] = table
        degree = degree + table.astype(F32)
    degree = jnp.sum(degree, axis=1, keepdims=True)
    sums = dot(spread_sc[...], rows_sc[...])
    for slot in range(2):
        high, low = split(sums[:, (2 + slot) * LANES : (3 + slot) * LANES])
        agg_ref[slot * NPE : (slot + 1) * NPE, :] = (
            sums[:, slot * LANES : (slot + 1) * LANES]
            + (dot(high, wo_ref[...]) + dot(low, wo_ref[...]))
            + degree * bo_ref[...]
        )
    outgoing(list_rows(lists_ref, counts_ref), agg_ref[...], (out0, out1, out2, out3))


def node_kernel(
    counts_ref, live_ref, lists_ref, agg_ref, in0, in1, in2, in3, mult_ref,
    nf_ref, nc_ref, wn_ref, bn_ref, wo_ref,
    back_ref, out0, out1, out2, out3, part_ref, terms_ref,
):
    nodes = nf_ref.shape[0]
    rows = list_rows(lists_ref, counts_ref)
    copies = jnp.concatenate(
        [as_column(mult_ref[b : b + 1, :].astype(F32)) for b in range(nodes // LANES)], axis=0
    )
    total = agg_ref[...] + incoming(rows, (in0, in1, in2, in3), nodes)
    consistent = (total / copies).astype(BF16)
    node_input = jnp.concatenate([nf_ref[...], consistent], axis=1)
    linear = dot(node_input, wn_ref[...]) + bn_ref[...]
    squashed = jax.nn.sigmoid(linear)
    hidden = (linear * squashed).astype(BF16)
    live = lax.broadcasted_iota(jnp.int32, (nodes, LANES), 0) < NPE * live_ref[0]
    cot = jnp.where(live, nc_ref[...].astype(F32), 0.0)
    cot_half = cot.astype(BF16)
    slope = squashed * (1.0 + linear * (1.0 - squashed))
    back = (dot_t(cot_half, wo_ref[...]) * slope).astype(BF16)
    consistent_back = dot_t(back, wn_ref[128:256, :]) / copies
    back_ref[...] = consistent_back
    outgoing(rows, consistent_back, (out0, out1, out2, out3))
    part_ref[...] = cot + dot_t(back, wn_ref[0:128, :])
    terms_ref[0:256, :] = dot_rows(node_input, back)
    terms_ref[256:384, :] = dot_rows(hidden, cot_half)
    terms_ref[384:386, :] = jnp.zeros((2, LANES), F32)
    terms_ref[386:387, :] = jnp.sum(back.astype(F32), axis=0, keepdims=True)
    terms_ref[387:388, :] = jnp.sum(cot, axis=0, keepdims=True)
    terms_ref[388:512, :] = jnp.zeros((124, LANES), F32)


def backward_kernel(
    counts_ref, live_ref, ends_ref, lists_ref, back_ref, in0, in1, in2, in3,
    ec_ref, hid_ref, slope_ref, ef_ref, nf_ref, part_ref, terms_ref, wi_ref, wo_ref,
    node_ref, edge_ref, mine_ref, theirs_ref,
    ends_sc, rows_sc, spread_sc, half_sc, eback_sc, sums_sc,
):
    edges = ends_ref.shape[1]
    width = padded(edges)
    nodes = nf_ref.shape[0]
    stage_ends(ends_ref, ends_sc)
    rows = list_rows(lists_ref, counts_ref)
    agg_back = (back_ref[...] + incoming(rows, (in0, in1, in2, in3), nodes)).astype(BF16)
    table_rows = jnp.concatenate([agg_back[:NPE], agg_back[NPE:]], axis=1)
    in_bias = jnp.zeros((1, LANES), F32)
    out_bias = jnp.zeros((1, LANES), F32)
    for start, size in blocks_of(edges):
        gathered = dot(edge_rows_table(ends_sc, 1, start, size), table_rows)
        for slot in range(2):
            first = slot * edges + start
            given = ec_ref[first : first + size, :].astype(F32)
            given = jnp.where(
                jnp.full((size, LANES), live_ref[0], jnp.int32) > slot, given, 0.0
            )
            cot = given + gathered[:, slot * LANES : (slot + 1) * LANES]
            half = cot.astype(BF16)
            back = (
                dot_t(half, wo_ref[...]) * slope_ref[first : first + size, :]
            ).astype(BF16)
            edge_ref[first : first + size, :] = (
                cot + dot_t(back, wi_ref[256:384, :])
            ).astype(BF16)
            half_sc[first : first + size, :] = half
            eback_sc[first : first + size, :] = back
            rows_sc[start : start + size, slot * LANES : (slot + 1) * LANES] = back
            in_bias = in_bias + jnp.sum(back.astype(F32), axis=0, keepdims=True)
            out_bias = out_bias + jnp.sum(half.astype(F32), axis=0, keepdims=True)
    rows_sc[edges:width, :] = jnp.zeros((width - edges, 2 * LANES), BF16)
    for first in range(0, width, LANES):
        for side in range(2):
            spread_sc[side * NPE : (side + 1) * NPE, first : first + LANES] = spread_table(
                ends_sc[side : side + 1, first : first + LANES], NPE
            )
    sums = dot(spread_sc[...], rows_sc[...])
    by_source = jnp.concatenate([sums[:NPE, :LANES], sums[:NPE, LANES:]], axis=0)
    by_target = jnp.concatenate([sums[NPE:, :LANES], sums[NPE:, LANES:]], axis=0)
    source_high, source_low = split(by_source)
    target_high, target_low = split(by_target)
    node_ref[...] = (
        part_ref[...]
        + (dot_t(source_high, wi_ref[0:128, :]) + dot_t(source_low, wi_ref[0:128, :]))
        + (dot_t(target_high, wi_ref[128:256, :]) + dot_t(target_low, wi_ref[128:256, :]))
    ).astype(BF16)
    pieces = dot_rows(
        nf_ref[...],
        jnp.concatenate([source_high, target_high, source_low, target_low], axis=1),
    )
    sums_sc[0:128, :] = pieces[:, 0:128] + pieces[:, 256:384]
    sums_sc[128:256, :] = pieces[:, 128:256] + pieces[:, 384:512]
    sums_sc[256:384, :] = dot_rows(ef_ref[...], eback_sc[...])
    sums_sc[384:512, :] = dot_rows(hid_ref[...], half_sc[...])
    sums_sc[512:1024, :] = terms_ref[...]
    sums_sc[896:897, :] = in_bias
    sums_sc[897:898, :] = out_bias
    first_core = jnp.full((512, LANES), lax.axis_index("c"), jnp.int32) == 0
    edge_half = sums_sc[0:512, :]
    node_half = sums_sc[512:1024, :]
    mine_ref[...] = jnp.where(first_core, edge_half, node_half)
    theirs_ref[...] = jnp.where(first_core, node_half, edge_half)


def finish_kernel(edge_scale, node_scale, own_ref, other_ref, ei, eib, eo, eob, ni, nib, no, nob):
    first_core = jnp.full((512, LANES), lax.axis_index("c"), jnp.int32) == 0
    own = own_ref[...]
    other = other_ref[...]
    edge_half = jnp.where(first_core, own, other)
    node_half = jnp.where(first_core, other, own)
    ei[...] = edge_half[0:384] * edge_scale
    eo[...] = edge_half[384:512] * edge_scale
    ni[...] = node_half[0:256] * node_scale
    no[...] = node_half[256:384] * node_scale
    eib[...] = node_half[384:385] * edge_scale
    eob[...] = node_half[385:386] * edge_scale
    nib[...] = node_half[386:387] * node_scale
    nob[...] = node_half[387:388] * node_scale


def call(kernel, out_shapes, specs, scratch, args, flops, moved):
    return pl.pallas_call(
        kernel,
        out_shape=[jax.ShapeDtypeStruct(shape, dtype) for shape, dtype in out_shapes],
        in_specs=specs,
        out_specs=[VMEM] * len(out_shapes),
        scratch_shapes=scratch,
        compiler_params=pltpu.CompilerParams(vmem_limit_bytes=40 * 1024 * 1024),
        cost_estimate=pl.CostEstimate(flops=flops, bytes_accessed=moved, transcendentals=0),
    )(*args)


def exchanged(messages):
    def near(device):
        return device ^ 1

    def next_chip(device):
        return device + 1 if device % 2 else device - 1

    count = lax.axis_size(AXES)
    quarter = count // 4

    def far_up(device):
        return device + quarter if (device // quarter) % 2 == 0 else device - quarter

    def far_down(device):
        return device - quarter if (device // quarter) % 2 == 0 else device + quarter

    return [
        lax.ppermute(message, AXES, [(s, swap(s) % count) for s in range(count)])
        for message, swap in zip(messages, (near, next_chip, far_up, far_down))
    ]


def body(
    node_features,
    edge_features,
    node_cotangent,
    edge_cotangent,
    edge_in_weight,
    edge_in_bias,
    edge_out_weight,
    edge_out_bias,
    node_in_weight,
    node_in_bias,
    node_out_weight,
    edge_ends,
    live_elements,
    shared_nodes,
    shared_counts,
    multiplicity,
):
    nodes, width = node_features.shape
    edges = edge_features.shape[0]
    devices = lax.axis_size(AXES)
    element_edges = edge_ends.shape[1]
    lists = shared_nodes.reshape(shared_nodes.shape[1:])
    copies = multiplicity.reshape(nodes // LANES, LANES)
    message = ((LANES, width), F32)
    ends_scratch = pltpu.VMEM((8, padded(element_edges)), jnp.int32)
    rows_height = padded(element_edges)

    aggregate, *messages, edge_hidden, edge_slope = call(
        forward_kernel,
        [((nodes, width), F32)] + [message] * 4 + [((edges, width), BF16), ((edges, width), F32)],
        [SMEM] + [VMEM] * 8,
        [
            ends_scratch,
            pltpu.VMEM((rows_height, 4 * LANES), BF16),
            pltpu.VMEM((NPE, rows_height), BF16),
        ],
        (
            shared_counts,
            edge_ends,
            lists,
            node_features,
            edge_features,
            edge_in_weight,
            edge_in_bias.reshape(1, -1),
            edge_out_weight,
            edge_out_bias.reshape(1, -1),
        ),
        2_000_000_000,
        4_000_000,
    )
    arrived = exchanged(messages)
    consistent_back, *messages, node_part, node_terms = call(
        node_kernel,
        [((nodes, width), F32)] + [message] * 4 + [((nodes, width), F32), ((512, width), F32)],
        [SMEM, SMEM] + [VMEM] * 12,
        [],
        (
            shared_counts,
            live_elements,
            lists,
            aggregate,
            *arrived,
            copies,
            node_features,
            node_cotangent,
            node_in_weight,
            node_in_bias.reshape(1, -1),
            node_out_weight,
        ),
        800_000_000,
        2_000_000,
    )
    arrived = exchanged(messages)
    node_result, edge_result, mine, theirs = call(
        backward_kernel,
        [
            ((nodes, width), BF16),
            ((edges, width), BF16),
            ((512, width), F32),
            ((512, width), F32),
        ],
        [SMEM, SMEM] + [VMEM] * 16,
        [
            ends_scratch,
            pltpu.VMEM((rows_height, 2 * LANES), BF16),
            pltpu.VMEM((2 * NPE, rows_height), BF16),
            pltpu.VMEM((edges, LANES), BF16),
            pltpu.VMEM((edges, LANES), BF16),
            pltpu.VMEM((1024, LANES), F32),
        ],
        (
            shared_counts,
            live_elements,
            edge_ends,
            lists,
            consistent_back,
            *arrived,
            edge_cotangent,
            edge_hidden,
            edge_slope,
            edge_features,
            node_features,
            node_part,
            node_terms,
            edge_in_weight,
            edge_out_weight,
        ),
        2_000_000_000,
        6_000_000,
    )
    other_core = [(0, 1), (1, 0)]
    chips = devices // 2
    half = mine + lax.ppermute(theirs, "c", other_core)
    half = half.reshape(chips, 512 // chips, width)
    share = lax.all_to_all(half, ("z", "y"), 0, 0, tiled=True).sum(axis=0)
    own = lax.all_to_all(
        jnp.broadcast_to(share, (chips, *share.shape)), ("z", "y"), 0, 0, tiled=True
    ).reshape(512, width)
    other = lax.ppermute(own, "c", other_core)
    edge_scale = 1.0 / math.sqrt(edges * devices)
    node_scale = 1.0 / math.sqrt(nodes * devices)

    def finish(*refs):
        finish_kernel(edge_scale, node_scale, *refs)

    ei, eib, eo, eob, ni, nib, no, nob = call(
        finish,
        [
            ((384, width), F32),
            ((1, width), F32),
            ((128, width), F32),
            ((1, width), F32),
            ((256, width), F32),
            ((1, width), F32),
            ((128, width), F32),
            ((1, width), F32),
        ],
        [VMEM] * 2,
        [],
        (own, other),
        1_000_000,
        1_000_000,
    )
    return (
        node_result,
        edge_result,
        ei,
        eib.reshape(-1),
        eo,
        eob.reshape(-1),
        ni,
        nib.reshape(-1),
        no,
        nob.reshape(-1),
    )


def solution(mesh):
    grid = mesh.devices.reshape(8, 4, 2, 4)
    mesh = Mesh(grid, ("z", "y", "c", "rep"))
    rows = ("rep", "z", "y", "c")
    in_specs = (
        P(rows, None),
        P(rows, None),
        P(rows, None),
        P(rows, None),
        P(),
        P(),
        P(),
        P(),
        P(),
        P(),
        P(),
        P(),
        P(rows),
        P(rows, None, None),
        P(rows, None),
        P(rows),
    )
    out_specs = (
        P(rows, None),
        P(rows, None),
        P("rep", None),
        P("rep"),
        P("rep", None),
        P("rep"),
        P("rep", None),
        P("rep"),
        P("rep", None),
        P("rep"),
    )
    return jax.shard_map(body, mesh=mesh, in_specs=in_specs, out_specs=out_specs, check_vma=False)
```

time: 124 us -> 85.8 us (0.69)
  other arithmetic: 24.4 us -> 0.06 us
  blocking collectives: 54.3 us -> 32.4 us
  matrix products: 15.1 us -> 0 us
  Pallas kernels: 0 us -> 12.8 us
  starting transfers between devices: 15.2 us -> 22.2 us
  waiting for transfers between devices: 4.51 us -> 9.25 us
    all_to_all x2, blocking collectives: 54.3 us -> 32.4 us  [the longest x1 17.4 us: body(): share = lax.all_to_all(half, ('z', 'y'), 0, 0, tiled=True).sum(axis=0)]
    dot_general x17 -> x0, matrix products: 15.1 us -> none  [the longest x3 5.85 us: spread_rows(): jnp.einsum('jn,gjd->gnd', table, grouped, preferred_element_type=jnp.floa...]
    scatter-add x8 -> x0, other arithmetic: 13.4 us -> none  [partner_sum(): running = running.at[share_lists[neighbour]].add(masked)]
    pallas_call x0 -> x4, Pallas kernels: none -> 12.8 us  [call(): pl.pallas_call(kernel, out_shape=[jax.ShapeDtypeStruct(shape, dtype) for...]
    ppermute x8 -> x10, starting transfers between devices: 15.2 us -> 22.2 us  [the longest x8 18.1 us: exchanged(): lax.ppermute(message, AXES, [(s, swap(s) % count) for s in range(count)])]
    ppermute x8 -> x10, waiting for transfers between devices: 4.51 us -> 9.25 us  [the longest x8 6.92 us: exchanged(): lax.ppermute(message, AXES, [(s, swap(s) % count) for s in range(count)])]
    unnamed x48 -> x40, local copies, waits for them, and re-layouts: 2.97 us -> 7.1 us
    reduce_sum x3 -> x1, other arithmetic: 2.71 us -> 0.04 us  [body(): share = lax.all_to_all(half, ('z', 'y'), 0, 0, tiled=True).sum(axis=0)]
  transfers between devices with their start and end apart: 8 -> 10, of which waited for: 2 -> 5; matrix products, arithmetic and copies ran while one was open for 8% -> 0% of each run, Pallas kernels for 0% -> 0%
where the time goes in v1:
time: 85.8 us; the launch traced here: 85.4 us
  blocking collectives  32.4 us (38%)
  starting transfers between devices  22.2 us (26%)
  Pallas kernels  12.8 us (15%)
  waiting for transfers between devices  9.25 us (11%)
  local copies, waits for them, and re-layouts  7.12 us (8%)
  between operations  1.48 us (2%)
    ppermute x8, starting transfers between devices, exchanged(): lax.ppermute(message, AXES, [(s, swap(s) % count) for s in range(count)])  18.1 us
    all_to_all x1, blocking collectives, body(): share = lax.all_to_all(half, ('z', 'y'), 0, 0, tiled=True).sum(axis=0)  17.4 us
    all_to_all x1, blocking collectives, body(): lax.all_to_all(jnp.broadcast_to(share, (chips, *share.shape)), ('z', 'y')...  15 us
    pallas_call x4, Pallas kernels, call(): pl.pallas_call(kernel, out_shape=[jax.ShapeDtypeStruct(shape, dtype) for...  12.8 us
    unnamed x40, local copies, waits for them, and re-layouts  7.1 us
    ppermute x8, waiting for transfers between devices, exchanged(): lax.ppermute(message, AXES, [(s, swap(s) % count) for s in range(count)])  6.92 us
    ppermute x1, starting transfers between devices, body(): other = lax.ppermute(own, 'c', other_core)  3.29 us
  transfers between devices with their start and end apart: 10, of which 5 were waited for; matrix products, arithmetic and copies ran while one was open for 0% of the time, Pallas kernels for 0%

profile of v1, /device:TPU:1, one launch (start us, length us, event | category | flops | bytes accessed | tf_op | source)
XLA Modules:
  0.0 85.4 jit_solution(9691228961235838623)
XLA Ops:
  0.6 0.0 copy-start
  0.7 1.1 %copy-done = bf16[2688,128]{1,0:T(8,128)(2,1)S(1)} copy-done((bf16[2688,128]{1,0:T(8,128)(2,1)S(1)}, bf16[2688,128]{1,0:T(8,128)(2,1)}, u32[]{:S(2)}) %copy-start) | copy-done | bytes 688152
  1.7 0.0 copy-start.4
  1.8 0.9 %copy-done.4 = bf16[1024,128]{1,0:T(8,128)(2,1)S(1)} copy-done((bf16[1024,128]{1,0:T(8,128)(2,1)S(1)}, bf16[1024,128]{1,0:T(8,128)(2,1)}, u32[]{:S(2)}) %copy-start.4) | copy-done | bytes 262168
  2.7 0.0 copy-start.6
  2.7 0.9 %copy-done.6 = bf16[384,128]{1,0:T(8,128)(2,1)S(1)} copy-done((bf16[384,128]{1,0:T(8,128)(2,1)S(1)}, bf16[384,128]{1,0:T(8,128)(2,1)}, u32[]{:S(2)}) %copy-start.6) | copy-done | bytes 98328
  3.6 0.0 copy-start.10
  3.6 0.8 copy-done.10
  4.4 0.0 copy-start.12
  4.4 0.7 copy-done.12
  5.1 0.0 copy-start.15
  5.1 0.7 copy-done.15
  5.7 0.0 copy-start.16
  5.7 0.7 copy-done.16
  6.4 0.0 copy-start.17
  6.4 0.7 copy-done.17
  7.0 0.0 copy-start.19
  7.1 0.7 copy-done.19
  7.7 0.0 copy-start.3
  7.7 0.0 copy-start.5
  7.7 0.0 copy-start.14
  7.7 0.0 copy-start.18
  7.7 4.1 %shard_map.231 = (f32[1024,128]{1,0:T(8,128)S(1)}, f32[128,128]{1,0:T(8,128)S(1)}, f32[128,128]{1,0:T(8,128)S(1)}, f32[128,128]{1,0:T(8,128)S(1)}, f32[128,128]{...) custom-call(s32[1,4]{1,0:T(1,128)S(1)} %copy-done.19, s32[2,1344]{1,0:T(2,128)S(1)} %copy-done.12, ...), custom_call_target="tpu_custom_call" | custom-call | flops 2000000000 | bytes 4000000 | tf_op jit(solution)/shard_map/pallas_call | solution.py:285
  11.9 3.3 %collective-permute-start = (f32[128,128]{1,0:T(8,128)S(1)}, f32[128,128]{1,0:T(8,128)S(1)}, u32[]{:S(2)}, u32[]{:S(2)}) collective-permute-start(f32[128,128]{1,0:T(8,128)S(1)} %get-tuple-element.37), channel_id=1, source_target_pairs={{0,4},{4,0},{8,12},{12,8},{16,20},{20,16},{24,28},{28,24},{32,36},... | collective-permute-start | bytes 196616 | tf_op jit(solution)/shard_map/ppermute | solution.py:313
  15.2 0.0 collective-permute-start.1
  15.2 2.5 %collective-permute-start.2 = (f32[128,128]{1,0:T(8,128)S(1)}, f32[128,128]{1,0:T(8,128)S(1)}, u32[]{:S(2)}, u32[]{:S(2)}) collective-permute-start(f32[128,128]{1,0:T(8,128)S(1)} %get-tuple-element.39), channel_id=1, source_target_pairs={{0,64},{4,68},{8,72},{12,76},{16,80},{20,84},{24,88},{28,92},{32,9... | collective-permute-start | bytes 196616 | tf_op jit(solution)/shard_map/ppermute | solution.py:313
  17.7 4.2 %collective-permute-start.3 = (f32[128,128]{1,0:T(8,128)S(1)}, f32[128,128]{1,0:T(8,128)S(1)}, u32[]{:S(2)}, u32[]{:S(2)}) collective-permute-start(f32[128,128]{1,0:T(8,128)S(1)} %get-tuple-element.40), channel_id=1, source_target_pairs={{0,192},{4,196},{8,200},{12,204},{16,208},{20,212},{24,216},{28,22... | collective-permute-start | bytes 196616 | tf_op jit(solution)/shard_map/ppermute | solution.py:313
  22.6 0.0 collective-permute-done.in0
  22.6 0.0 collective-permute-done.1.in1
  22.6 0.0 collective-permute-done.2.in2
  22.6 1.7 %collective-permute-done.3.in3 = f32[128,128]{1,0:T(8,128)S(1)} collective-permute-done((f32[128,128]{1,0:T(8,128)S(1)}, f32[128,128]{1,0:T(8,128)S(1)}, u32[]{:S(2)}, u32[]{:S(2)}) %collective-permute-start.3) | collective-permute-done | bytes 65568 | tf_op jit(solution)/shard_map/ppermute | solution.py:313
  24.3 0.0 copy-done.3
  24.3 0.0 copy-done.5
  24.3 0.0 copy-done.8
  24.3 0.0 copy-done.9
  24.3 0.0 copy-done.14
  24.3 0.0 copy-done.18
  24.3 0.0 copy-start.1
  24.3 0.0 copy-start.2
  24.3 0.0 copy-start.7
  24.3 0.0 copy-start.11
  24.4 0.0 copy-start.13
  24.4 2.3 %shard_map.232 = (f32[1024,128]{1,0:T(8,128)S(1)}, f32[128,128]{1,0:T(8,128)S(1)}, f32[128,128]{1,0:T(8,128)S(1)}, f32[128,128]{1,0:T(8,128)S(1)}, f32[128,128]{...) custom-call(s32[1,4]{1,0:T(1,128)S(1)} %copy-done.19, s32[1]{0:T(128)S(6)} %copy.26.live_ref, ...), custom_call_target="tpu_custom_call" | custom-call | flops 800000000 | bytes 2000000 | tf_op jit(solution)/shard_map/pallas_call | solution.py:285
  26.6 4.2 %collective-permute-start.4 = (f32[128,128]{1,0:T(8,128)S(1)}, f32[128,128]{1,0:T(8,128)S(1)}, u32[]{:S(2)}, u32[]{:S(2)}) collective-permute-start(f32[128,128]{1,0:T(8,128)S(1)} %get-tuple-element.42), channel_id=1, source_target_pairs={{0,4},{4,0},{8,12},{12,8},{16,20},{20,16},{24,28},{28,24},{32,36},... | collective-permute-start | bytes 196616 | tf_op jit(solution)/shard_map/ppermute | solution.py:313
  30.8 0.0 collective-permute-start.5
  30.8 2.5 %collective-permute-start.6 = (f32[128,128]{1,0:T(8,128)S(1)}, f32[128,128]{1,0:T(8,128)S(1)}, u32[]{:S(2)}, u32[]{:S(2)}) collective-permute-start(f32[128,128]{1,0:T(8,128)S(1)} %get-tuple-element.44), channel_id=1, source_target_pairs={{0,64},{4,68},{8,72},{12,76},{16,80},{20,84},{24,88},{28,92},{32,9... | collective-permute-start | bytes 196616 | tf_op jit(solution)/shard_map/ppermute | solution.py:313
  33.4 1.3 %collective-permute-start.7 = (f32[128,128]{1,0:T(8,128)S(1)}, f32[128,128]{1,0:T(8,128)S(1)}, u32[]{:S(2)}, u32[]{:S(2)}) collective-permute-start(f32[128,128]{1,0:T(8,128)S(1)} %get-tuple-element.45), channel_id=1, source_target_pairs={{0,192},{4,196},{8,200},{12,204},{16,208},{20,212},{24,216},{28,22... | collective-permute-start | bytes 196616 | tf_op jit(solution)/shard_map/ppermute | solution.py:313
  34.6 0.0 collective-permute-done.4.in0
  34.6 0.0 collective-permute-done.5.in1
  34.6 2.3 %collective-permute-done.6.in2 = f32[128,128]{1,0:T(8,128)S(1)} collective-permute-done((f32[128,128]{1,0:T(8,128)S(1)}, f32[128,128]{1,0:T(8,128)S(1)}, u32[]{:S(2)}, u32[]{:S(2)}) %collective-permute-start.6) | collective-permute-done | bytes 65568 | tf_op jit(solution)/shard_map/ppermute | solution.py:313
  37.0 2.9 %collective-permute-done.7.in3 = f32[128,128]{1,0:T(8,128)S(1)} collective-permute-done((f32[128,128]{1,0:T(8,128)S(1)}, f32[128,128]{1,0:T(8,128)S(1)}, u32[]{:S(2)}, u32[]{:S(2)}) %collective-permute-start.7) | collective-permute-done | bytes 65568 | tf_op jit(solution)/shard_map/ppermute | solution.py:313
  39.9 0.0 copy-done.1
  39.9 0.0 copy-done.2
  39.9 0.0 copy-done.7
  39.9 0.0 copy-done.11
  39.9 0.0 copy-done.13
  39.9 5.6 %shard_map.233 = (bf16[1024,128]{1,0:T(8,128)(2,1)}, bf16[2688,128]{1,0:T(8,128)(2,1)}, f32[512,128]{1,0:T(8,128)S(1)}, f32[512,128]{1,0:T(8,128)S(1)}) custom-call(s32[1,4]{1,0:T(1,128)S(1)} %copy-done.19, s32[1]{0:T(128)S(6)} %copy.26.live_ref, s32[2,1344]{1,0:T(2,128)S(1)} %copy-done.13, s32[4,128]{1,0:T(4,128)S(1)} %bitcast.16, ...), custom_call_target="tpu_custom_call" | custom-call | flops 2000000000 | bytes 6000000 | tf_op jit(solution)/shard_map/pallas_call | solution.py:285
  45.6 0.9 %collective-permute-start.8 = (f32[512,128]{1,0:T(8,128)S(1)}, f32[512,128]{1,0:T(8,128)S(1)}, u32[]{:S(2)}, u32[]{:S(2)}) collective-permute-start(f32[512,128]{1,0:T(8,128)S(1)} %get-tuple-element.53), channel_id=1, source_target_pairs={{0,4},{4,0},{1,5},{5,1},{2,6},{6,2},{3,7},{7,3},{8,12},{12,8},{9,1... | collective-permute-start | bytes 786440 | tf_op jit(solution)/shard_map/ppermute | solution.py:431
  46.5 1.2 %collective-permute-done.8 = f32[512,128]{1,0:T(8,128)S(1)} collective-permute-done((f32[512,128]{1,0:T(8,128)S(1)}, f32[512,128]{1,0:T(8,128)S(1)}, u32[]{:S(2)}, u32[]{:S(2)}) %collective-permute-start.8) | collective-permute-done | bytes 262176 | tf_op jit(solution)/shard_map/ppermute | solution.py:431
  47.7 17.4 %all_to_all.10 = f32[32,16,128]{2,1,0:T(8,128)S(1)} all-to-all(f32[32,16,128]{2,1,0:T(8,128)S(1)} %bitcast.20), channel_id=1, replica_groups=mesh['z'=8,'y'=4,'c'=2,'rep'=4] {'z','y'}, dimensions={0} | all-to-all | bytes 524288 | tf_op jit(solution)/shard_map/all_to_all | solution.py:433
  65.1 15.0 %all_to_all.11 = f32[32,16,128]{2,1,0:T(8,128)S(1)} all-to-all(f32[32,16,128]{2,1,0:T(8,128)S(1)} %broadcast_in_dim.3), channel_id=1, replica_groups=mesh['z'=8,'y'=4,'c'=2,'rep'=4] {'z','y'}, dimensions={0} | all-to-all | bytes 524288 | tf_op jit(solution)/shard_map/all_to_all | solution.py:434
  80.1 3.3 %collective-permute-start.9 = (f32[512,128]{1,0:T(8,128)S(1)}, f32[512,128]{1,0:T(8,128)S(1)}, u32[]{:S(2)}, u32[]{:S(2)}) collective-permute-start(f32[512,128]{1,0:T(8,128)S(1)} %bitcast.11), channel_id=1, source_target_pairs={{0,4},{4,0},{1,5},{5,1},{2,6},{6,2},{3,7},{7,3},{8,12},{12,8},{9,1... | collective-permute-start | bytes 786440 | tf_op jit(solution)/shard_map/ppermute | solution.py:437
  83.4 1.2 %collective-permute-done.9.refs_1_ = f32[512,128]{1,0:T(8,128)S(1)} collective-permute-done((f32[512,128]{1,0:T(8,128)S(1)}, f32[512,128]{1,0:T(8,128)S(1)}, u32[]{:S(2)}, u32[]{:S(2)}) %collective-permute-start.9) | collective-permute-done | bytes 262176 | tf_op jit(solution)/shard_map/ppermute | solution.py:437
  84.6 0.8 shard_map.234
  (5 shorter events, 0.1 us)
Async XLA Ops:
  0.6 1.1 %copy-start = (bf16[2688,128]{1,0:T(8,128)(2,1)S(1)}, bf16[2688,128]{1,0:T(8,128)(2,1)}, u32[]{:S(2)}) copy-start(bf16[2688,128]{1,0:T(8,128)(2,1)} %ef_ref.3) | copy-start | bytes 2064388
  1.7 0.9 %copy-start.4 = (bf16[1024,128]{1,0:T(8,128)(2,1)S(1)}, bf16[1024,128]{1,0:T(8,128)(2,1)}, u32[]{:S(2)}) copy-start(bf16[1024,128]{1,0:T(8,128)(2,1)} %nf_ref.5) | copy-start | bytes 786436
  2.7 0.9 %copy-start.6 = (bf16[384,128]{1,0:T(8,128)(2,1)S(1)}, bf16[384,128]{1,0:T(8,128)(2,1)}, u32[]{:S(2)}) copy-start(bf16[384,128]{1,0:T(8,128)(2,1)} %wi_ref.3) | copy-start | bytes 294916
  3.6 0.8 copy-start.10
  4.4 0.7 copy-start.12
  5.1 0.7 copy-start.15
  5.7 0.7 copy-start.16
  6.4 0.7 copy-start.17
  7.0 0.7 copy-start.19
  7.7 16.6 %copy-start.3 = (bf16[1024,128]{1,0:T(8,128)(2,1)S(1)}, bf16[1024,128]{1,0:T(8,128)(2,1)}, u32[]{:S(2)}) copy-start(bf16[1024,128]{1,0:T(8,128)(2,1)} %nc_ref.1) | copy-start | bytes 786436
  7.7 16.6 %copy-start.5 = (bf16[1024,128]{1,0:T(8,128)(2,1)S(1)}, bf16[1024,128]{1,0:T(8,128)(2,1)}, u32[]{:S(2)}) copy-start(bf16[1024,128]{1,0:T(8,128)(2,1)} %nf_ref.5) | copy-start | bytes 786436
  7.7 16.6 %copy-start.8 = (bf16[256,128]{1,0:T(8,128)(2,1)S(1)}, bf16[256,128]{1,0:T(8,128)(2,1)}, u32[]{:S(2)}) copy-start(bf16[256,128]{1,0:T(8,128)(2,1)} %wn_ref.1) | copy-start | bytes 196612
  7.7 16.6 %copy-start.9 = (bf16[128,128]{1,0:T(8,128)(2,1)S(1)}, bf16[128,128]{1,0:T(8,128)(2,1)}, u32[]{:S(2)}) copy-start(bf16[128,128]{1,0:T(8,128)(2,1)} %wo_ref.4) | copy-start | bytes 98308
  7.7 16.6 %copy-start.14 = (s32[1024]{0:T(1024)S(1)}, s32[1024]{0:T(1024)}, u32[]{:S(2)}) copy-start(s32[1024]{0:T(1024)} %param.31) | copy-start | bytes 12292
  7.7 16.6 %copy-start.18 = (f32[128]{0:T(128)S(1)}, f32[128]{0:T(128)}, u32[]{:S(2)}) copy-start(f32[128]{0:T(128)} %param.25) | copy-start | bytes 1540
  11.9 10.7 %collective-permute-start = (f32[128,128]{1,0:T(8,128)S(1)}, f32[128,128]{1,0:T(8,128)S(1)}, u32[]{:S(2)}, u32[]{:S(2)}) collective-permute-start(f32[128,128]{1,0:T(8,128)S(1)} %get-tuple-element.37), channel_id=1, source_target_pairs={{0,4},{4,0},{8,12},{12,8},{16,20},{20,16},{24,28},{28,24},{32,36},... | collective-permute-start | bytes 196616 | tf_op jit(solution)/shard_map/ppermute | solution.py:313
  15.2 7.4 %collective-permute-start.1 = (f32[128,128]{1,0:T(8,128)S(1)}, f32[128,128]{1,0:T(8,128)S(1)}, u32[]{:S(2)}, u32[]{:S(2)}) collective-permute-start(f32[128,128]{1,0:T(8,128)S(1)} %get-tuple-element.38), channel_id=1, source_target_pairs={{0,252},{4,8},{8,4},{12,16},{16,12},{20,24},{24,20},{28,32},{32,28... | collective-permute-start | bytes 196616 | tf_op jit(solution)/shard_map/ppermute | solution.py:313
  15.2 7.4 %collective-permute-start.2 = (f32[128,128]{1,0:T(8,128)S(1)}, f32[128,128]{1,0:T(8,128)S(1)}, u32[]{:S(2)}, u32[]{:S(2)}) collective-permute-start(f32[128,128]{1,0:T(8,128)S(1)} %get-tuple-element.39), channel_id=1, source_target_pairs={{0,64},{4,68},{8,72},{12,76},{16,80},{20,84},{24,88},{28,92},{32,9... | collective-permute-start | bytes 196616 | tf_op jit(solution)/shard_map/ppermute | solution.py:313
  17.7 6.5 %collective-permute-start.3 = (f32[128,128]{1,0:T(8,128)S(1)}, f32[128,128]{1,0:T(8,128)S(1)}, u32[]{:S(2)}, u32[]{:S(2)}) collective-permute-start(f32[128,128]{1,0:T(8,128)S(1)} %get-tuple-element.40), channel_id=1, source_target_pairs={{0,192},{4,196},{8,200},{12,204},{16,208},{20,212},{24,216},{28,22... | collective-permute-start | bytes 196616 | tf_op jit(solution)/shard_map/ppermute | solution.py:313
  24.3 15.6 %copy-start.1 = (bf16[2688,128]{1,0:T(8,128)(2,1)S(1)}, bf16[2688,128]{1,0:T(8,128)(2,1)}, u32[]{:S(2)}) copy-start(bf16[2688,128]{1,0:T(8,128)(2,1)} %ef_ref.3) | copy-start | bytes 2064388
  24.3 15.6 %copy-start.2 = (bf16[2688,128]{1,0:T(8,128)(2,1)S(1)}, bf16[2688,128]{1,0:T(8,128)(2,1)}, u32[]{:S(2)}) copy-start(bf16[2688,128]{1,0:T(8,128)(2,1)} %ec_ref.1) | copy-start | bytes 2064388
  24.3 15.6 %copy-start.7 = (bf16[384,128]{1,0:T(8,128)(2,1)S(1)}, bf16[384,128]{1,0:T(8,128)(2,1)}, u32[]{:S(2)}) copy-start(bf16[384,128]{1,0:T(8,128)(2,1)} %wi_ref.3) | copy-start | bytes 294916
  24.3 15.6 %copy-start.11 = (bf16[128,128]{1,0:T(8,128)(2,1)S(1)}, bf16[128,128]{1,0:T(8,128)(2,1)}, u32[]{:S(2)}) copy-start(bf16[128,128]{1,0:T(8,128)(2,1)} %wo_ref.5) | copy-start | bytes 98308
  24.4 15.6 %copy-start.13 = (s32[2,1344]{1,0:T(2,128)S(1)}, s32[2,1344]{1,0:T(2,128)}, u32[]{:S(2)}) copy-start(s32[2,1344]{1,0:T(2,128)} %ends_ref.3) | copy-start | bytes 32260
  26.6 8.0 %collective-permute-start.4 = (f32[128,128]{1,0:T(8,128)S(1)}, f32[128,128]{1,0:T(8,128)S(1)}, u32[]{:S(2)}, u32[]{:S(2)}) collective-permute-start(f32[128,128]{1,0:T(8,128)S(1)} %get-tuple-element.42), channel_id=1, source_target_pairs={{0,4},{4,0},{8,12},{12,8},{16,20},{20,16},{24,28},{28,24},{32,36},... | collective-permute-start | bytes 196616 | tf_op jit(solution)/shard_map/ppermute | solution.py:313
  30.8 3.8 %collective-permute-start.5 = (f32[128,128]{1,0:T(8,128)S(1)}, f32[128,128]{1,0:T(8,128)S(1)}, u32[]{:S(2)}, u32[]{:S(2)}) collective-permute-start(f32[128,128]{1,0:T(8,128)S(1)} %get-tuple-element.43), channel_id=1, source_target_pairs={{0,252},{4,8},{8,4},{12,16},{16,12},{20,24},{24,20},{28,32},{32,28... | collective-permute-start | bytes 196616 | tf_op jit(solution)/shard_map/ppermute | solution.py:313
  30.8 6.1 %collective-permute-start.6 = (f32[128,128]{1,0:T(8,128)S(1)}, f32[128,128]{1,0:T(8,128)S(1)}, u32[]{:S(2)}, u32[]{:S(2)}) collective-permute-start(f32[128,128]{1,0:T(8,128)S(1)} %get-tuple-element.44), channel_id=1, source_target_pairs={{0,64},{4,68},{8,72},{12,76},{16,80},{20,84},{24,88},{28,92},{32,9... | collective-permute-start | bytes 196616 | tf_op jit(solution)/shard_map/ppermute | solution.py:313
  33.4 6.5 %collective-permute-start.7 = (f32[128,128]{1,0:T(8,128)S(1)}, f32[128,128]{1,0:T(8,128)S(1)}, u32[]{:S(2)}, u32[]{:S(2)}) collective-permute-start(f32[128,128]{1,0:T(8,128)S(1)} %get-tuple-element.45), channel_id=1, source_target_pairs={{0,192},{4,196},{8,200},{12,204},{16,208},{20,212},{24,216},{28,22... | collective-permute-start | bytes 196616 | tf_op jit(solution)/shard_map/ppermute | solution.py:313
  45.6 2.0 %collective-permute-start.8 = (f32[512,128]{1,0:T(8,128)S(1)}, f32[512,128]{1,0:T(8,128)S(1)}, u32[]{:S(2)}, u32[]{:S(2)}) collective-permute-start(f32[512,128]{1,0:T(8,128)S(1)} %get-tuple-element.53), channel_id=1, source_target_pairs={{0,4},{4,0},{1,5},{5,1},{2,6},{6,2},{3,7},{7,3},{8,12},{12,8},{9,1... | collective-permute-start | bytes 786440 | tf_op jit(solution)/shard_map/ppermute | solution.py:431
  80.1 4.5 %collective-permute-start.9 = (f32[512,128]{1,0:T(8,128)S(1)}, f32[512,128]{1,0:T(8,128)S(1)}, u32[]{:S(2)}, u32[]{:S(2)}) collective-permute-start(f32[512,128]{1,0:T(8,128)S(1)} %bitcast.11), channel_id=1, source_target_pairs={{0,4},{4,0},{1,5},{5,1},{2,6},{6,2},{3,7},{7,3},{8,12},{12,8},{9,1... | collective-permute-start | bytes 786440 | tf_op jit(solution)/shard_map/ppermute | solution.py:437

commit v2 on v1

v2 whole, which is shorter than its diff:
```python
import math

import jax
import jax.numpy as jnp
from jax import lax
from jax.experimental import pallas as pl
from jax.experimental.pallas import tpu as pltpu
from jax.sharding import Mesh, PartitionSpec as P

NPE = 512
LANES = 128
BLOCK = 256
F32 = jnp.float32
BF16 = jnp.bfloat16
AXES = ("z", "y", "c")
VMEM = pl.BlockSpec(memory_space=pltpu.VMEM)
SMEM = pl.BlockSpec(memory_space=pltpu.SMEM)
HBM = pl.BlockSpec(memory_space=pltpu.HBM)


def padded(count):
    return -(-count // LANES) * LANES


def dot(left, right):
    return jnp.dot(left, right, preferred_element_type=F32)


def dot_t(left, right):
    return lax.dot_general(left, right, (((1,), (1,)), ((), ())), preferred_element_type=F32)


def dot_rows(left, right):
    return lax.dot_general(left, right, (((0,), (0,)), ((), ())), preferred_element_type=F32)


def split(value):
    high = value.astype(BF16)
    low = (value - high.astype(F32)).astype(BF16)
    return high, low


def as_column(row):
    return jnp.transpose(jnp.broadcast_to(row, (LANES, LANES)))


def hot(flags):
    return jnp.where(flags, 1.0, 0.0).astype(BF16)


def pick_table(row, width):
    column = as_column(row)
    lane = lax.broadcasted_iota(jnp.int32, (LANES, LANES), 1)
    tiles = [hot(column == lane + start) for start in range(0, width, LANES)]
    return jnp.concatenate(tiles, axis=1)


def spread_table(row, height):
    return hot(lax.broadcasted_iota(jnp.int32, (height, row.shape[1]), 0) == row)


def list_rows(lists_ref, counts_ref):
    core = lax.axis_index("c")
    odd = lax.rem(lax.div(lax.axis_index("z"), 2), 2)
    lane = lax.broadcasted_iota(jnp.int32, (1, LANES), 1)
    rows = [jnp.where(lane < counts_ref[0, k], lists_ref[k : k + 1, :], -1) for k in range(4)]

    def ordered(flag, first, second):
        chosen = jnp.full((1, LANES), flag, jnp.int32) == 0
        return jnp.where(chosen, first, second), jnp.where(chosen, second, first)

    near, next_chip = ordered(core, rows[0], rows[1])
    return ordered(odd, rows[2], rows[3]) + (next_chip, near)


def outgoing(table_ref, values, refs):
    both = dot(table_ref[...], jnp.concatenate(split(values), axis=1))
    for k, ref in enumerate(refs):
        part = both[k * LANES : (k + 1) * LANES]
        ref[...] = part[:, :LANES] + part[:, LANES:]


def incoming(table_ref, refs):
    arrived = jnp.concatenate([ref[...] for ref in refs], axis=0)
    both = dot(table_ref[...], jnp.concatenate(split(arrived), axis=1))
    return both[:, :LANES] + both[:, LANES:]


def blocks_of(count):
    return [(start, min(BLOCK, count - start)) for start in range(0, count, BLOCK)]


def stage_ends(ends_ref, ends_sc):
    ends_sc[...] = jnp.full(ends_sc.shape, -1, jnp.int32)
    ends_sc[0:2, 0 : ends_ref.shape[1]] = ends_ref[...]


def edge_rows_table(ends_sc, side, start, size):
    parts = [
        pick_table(ends_sc[side : side + 1, first : first + LANES], NPE)
        for first in range(start, start + size, LANES)
    ]
    return jnp.concatenate(parts, axis=0)[:size]


def forward_kernel(
    counts_hbm, ends_hbm, lists_hbm, nf_hbm, ef_hbm, wi_hbm, bi_hbm, wo_hbm, bo_hbm,
    agg_ref, out0, out1, out2, out3, hid_ref, slope_ref, table_ref, spread_ref, pick_ref,
    counts_ref, ends_ref, lists_ref, nf_ref, ef_ref, wi_ref, bi_ref, wo_ref, bo_ref,
    sems, ends_sc, rows_sc,
):
    pairs = (
        (ends_hbm, ends_ref),
        (nf_hbm, nf_ref),
        (wi_hbm, wi_ref),
        (ef_hbm, ef_ref),
        (bi_hbm, bi_ref),
        (wo_hbm, wo_ref),
        (bo_hbm, bo_ref),
        (lists_hbm, lists_ref),
        (counts_hbm, counts_ref),
    )
    loads = [
        pltpu.make_async_copy(source, target, sems.at[k])
        for k, (source, target) in enumerate(pairs)
    ]
    for load in loads:
        load.start()
    edges = ends_ref.shape[1]
    width = padded(edges)
    loads[0].wait()
    stage_ends(ends_ref, ends_sc)
    degree = jnp.zeros((NPE, LANES), F32)
    for first in range(0, width, LANES):
        table = spread_table(ends_sc[1:2, first : first + LANES], NPE)
        spread_ref[:, first : first + LANES] = table
        degree = degree + table.astype(F32)
    degree = jnp.sum(degree, axis=1, keepdims=True)
    loads[1].wait()
    loads[2].wait()
    nf = nf_ref[...]
    from_source = dot(nf, wi_ref[0:128, :]).astype(BF16)
    from_target = dot(nf, wi_ref[128:256, :]).astype(BF16)
    table_rows = jnp.concatenate(
        [
            jnp.concatenate([from_source[:NPE], from_source[NPE:]], axis=1),
            jnp.concatenate([from_target[:NPE], from_target[NPE:]], axis=1),
        ],
        axis=0,
    )
    for load in loads[3:]:
        load.wait()
    for start, size in blocks_of(edges):
        by_target = edge_rows_table(ends_sc, 1, start, size)
        table_ref[start : start + size, :] = by_target
        table = jnp.concatenate([edge_rows_table(ends_sc, 0, start, size), by_target], axis=1)
        ends_part = dot(table, table_rows)
        for slot in range(2):
            first = slot * edges + start
            own = ef_ref[first : first + size, :]
            linear = (
                ends_part[:, slot * LANES : (slot + 1) * LANES]
                + dot(own, wi_ref[256:384, :])
                + bi_ref[...]
            )
            squashed = jax.nn.sigmoid(linear)
            hidden = (linear * squashed).astype(BF16)
            hid_ref[first : first + size, :] = hidden
            slope_ref[first : first + size, :] = squashed * (1.0 + linear * (1.0 - squashed))
            rows_sc[start : start + size, slot * LANES : (slot + 1) * LANES] = own
            rows_sc[start : start + size, (2 + slot) * LANES : (3 + slot) * LANES] = hidden
    rows_sc[edges:width, :] = jnp.zeros((width - edges, 4 * LANES), BF16)
    sums = dot(spread_ref[...], rows_sc[...])
    for slot in range(2):
        high, low = split(sums[:, (2 + slot) * LANES : (3 + slot) * LANES])
        agg_ref[slot * NPE : (slot + 1) * NPE, :] = (
            sums[:, slot * LANES : (slot + 1) * LANES]
            + (dot(high, wo_ref[...]) + dot(low, wo_ref[...]))
            + degree * bo_ref[...]
        )
    values = agg_ref[...]
    for k, row in enumerate(list_rows(lists_ref, counts_ref)):
        pick_ref[k * LANES : (k + 1) * LANES, :] = pick_table(row, values.shape[0])
    outgoing(pick_ref, values, (out0, out1, out2, out3))


def prepare_kernel(
    counts_ref, live_ref, ends_ref, lists_ref, mult_ref, nf_ref, nc_ref, wn_ref, bn_ref, wo_ref,
    spread_ref, arrive_ref, linear_ref, hback_ref, cot_ref, copies_ref,
    ends_sc,
):
    nodes = nf_ref.shape[0]
    stage_ends(ends_ref, ends_sc)
    for first in range(0, ends_sc.shape[1], LANES):
        spread_ref[:, first : first + LANES] = spread_table(
            ends_sc[0:1, first : first + LANES], NPE
        )
    for k, row in enumerate(list_rows(lists_ref, counts_ref)):
        arrive_ref[:, k * LANES : (k + 1) * LANES] = spread_table(row, nodes)
    live = lax.broadcasted_iota(jnp.int32, (nodes, LANES), 0) < NPE * live_ref[0]
    cot = jnp.where(live, nc_ref[...].astype(F32), 0.0).astype(BF16)
    cot_ref[...] = cot
    linear_ref[...] = dot(nf_ref[...], wn_ref[0:128, :]) + bn_ref[...]
    hback_ref[...] = dot_t(cot, wo_ref[...])
    for b in range(nodes // LANES):
        copies_ref[b * LANES : (b + 1) * LANES, :] = as_column(mult_ref[b : b + 1, :].astype(F32))


def node_kernel(
    agg_ref, in0, in1, in2, in3, arrive_ref, pick_ref, linear_ref, hback_ref, copies_ref, wn_ref,
    cback_ref, out0, out1, out2, out3, cons_ref, hid_ref, back_ref,
):
    copies = copies_ref[...]
    total = agg_ref[...] + incoming(arrive_ref, (in0, in1, in2, in3))
    consistent = (total / copies).astype(BF16)
    linear = linear_ref[...] + dot(consistent, wn_ref[128:256, :])
    squashed = jax.nn.sigmoid(linear)
    slope = squashed * (1.0 + linear * (1.0 - squashed))
    back = (hback_ref[...] * slope).astype(BF16)
    consistent_back = dot_t(back, wn_ref[128:256, :]) / copies
    cback_ref[...] = consistent_back
    outgoing(pick_ref, consistent_back, (out0, out1, out2, out3))
    cons_ref[...] = consistent
    hid_ref[...] = (linear * squashed).astype(BF16)
    back_ref[...] = back


def node_sums_kernel(
    nf_ref, cons_ref, hid_ref, back_ref, cot_ref, wn_ref,
    part_ref, terms_ref,
):
    back = back_ref[...]
    cot_half = cot_ref[...]
    cot = cot_half.astype(F32)
    part_ref[...] = cot + dot_t(back, wn_ref[0:128, :])
    terms_ref[0:128, :] = dot_rows(nf_ref[...], back)
    terms_ref[128:256, :] = dot_rows(cons_ref[...], back)
    terms_ref[256:384, :] = dot_rows(hid_ref[...], cot_half)
    terms_ref[384:386, :] = jnp.zeros((2, LANES), F32)
    terms_ref[386:387, :] = jnp.sum(back.astype(F32), axis=0, keepdims=True)
    terms_ref[387:388, :] = jnp.sum(cot, axis=0, keepdims=True)
    terms_ref[388:512, :] = jnp.zeros((124, LANES), F32)


def backward_kernel(
    live_ref, cback_ref, in0, in1, in2, in3, arrive_ref, table_ref, spread_s_ref, spread_t_ref,
    ec_ref, hid_ref, slope_ref, ef_ref, nf_ref, terms_ref, wo_ref,
    cot_ref, eback_ref, sums_ref, mine_ref, theirs_ref,
    rows_sc, half_sc, terms_sc,
):
    edges = table_ref.shape[0]
    width = padded(edges)
    agg_back = (cback_ref[...] + incoming(arrive_ref, (in0, in1, in2, in3))).astype(BF16)
    table_rows = jnp.concatenate([agg_back[:NPE], agg_back[NPE:]], axis=1)
    in_bias = jnp.zeros((1, LANES), F32)
    out_bias = jnp.zeros((1, LANES), F32)
    for start, size in blocks_of(edges):
        gathered = dot(table_ref[start : start + size, :], table_rows)
        for slot in range(2):
            first = slot * edges + start
            given = ec_ref[first : first + size, :].astype(F32)
            given = jnp.where(
                jnp.full((size, LANES), live_ref[0], jnp.int32) > slot, given, 0.0
            )
            cot = given + gathered[:, slot * LANES : (slot + 1) * LANES]
            half = cot.astype(BF16)
            back = (
                dot_t(half, wo_ref[...]) * slope_ref[first : first + size, :]
            ).astype(BF16)
            cot_ref[first : first + size, :] = cot
            half_sc[first : first + size, :] = half
            eback_ref[first : first + size, :] = back
            rows_sc[start : start + size, slot * LANES : (slot + 1) * LANES] = back
            in_bias = in_bias + jnp.sum(back.astype(F32), axis=0, keepdims=True)
            out_bias = out_bias + jnp.sum(half.astype(F32), axis=0, keepdims=True)
    rows_sc[edges:width, :] = jnp.zeros((width - edges, 2 * LANES), BF16)
    by_source = dot(spread_s_ref[...], rows_sc[...])
    by_target = dot(spread_t_ref[...], rows_sc[...])
    sums_ref[0:NPE, 0:LANES] = by_source[:, :LANES]
    sums_ref[NPE : 2 * NPE, 0:LANES] = by_source[:, LANES:]
    sums_ref[0:NPE, LANES:] = by_target[:, :LANES]
    sums_ref[NPE : 2 * NPE, LANES:] = by_target[:, LANES:]
    both = dot_rows(nf_ref[...], jnp.concatenate(split(sums_ref[...]), axis=1))
    terms_sc[0:128, :] = both[:, 0:128] + both[:, 256:384]
    terms_sc[128:256, :] = both[:, 128:256] + both[:, 384:512]
    terms_sc[256:384, :] = dot_rows(ef_ref[...], eback_ref[...])
    terms_sc[384:512, :] = dot_rows(hid_ref[...], half_sc[...])
    terms_sc[512:1024, :] = terms_ref[...]
    terms_sc[896:897, :] = in_bias
    terms_sc[897:898, :] = out_bias
    core = lax.axis_index("c")
    place = lax.axis_index("y")
    for k in range(4):
        block = lax.bitwise_xor(place, k) * LANES
        kept = pl.multiple_of(core * 512 + block, LANES)
        sent = pl.multiple_of((1 - core) * 512 + block, LANES)
        mine_ref[k * LANES : (k + 1) * LANES, :] = terms_sc[pl.ds(kept, LANES), :]
        theirs_ref[k * LANES : (k + 1) * LANES, :] = terms_sc[pl.ds(sent, LANES), :]


def results_kernel(cot_ref, eback_ref, sums_ref, part_ref, wi_ref, node_ref, edge_ref):
    high, low = split(sums_ref[...])
    node_ref[...] = (
        part_ref[...]
        + (dot_t(high[:, :LANES], wi_ref[0:128, :]) + dot_t(low[:, :LANES], wi_ref[0:128, :]))
        + (dot_t(high[:, LANES:], wi_ref[128:256, :]) + dot_t(low[:, LANES:], wi_ref[128:256, :]))
    ).astype(BF16)
    edge_ref[...] = (cot_ref[...] + dot_t(eback_ref[...], wi_ref[256:384, :])).astype(BF16)


def finish_kernel(
    edge_scale, node_scale, own_ref, other_ref, ei, eib, eo, eob, ni, nib, no, nob, sums_sc
):
    core = lax.axis_index("c")
    place = lax.axis_index("y")
    for k in range(4):
        block = lax.bitwise_xor(place, k) * LANES
        kept = pl.multiple_of(core * 512 + block, LANES)
        sent = pl.multiple_of((1 - core) * 512 + block, LANES)
        sums_sc[pl.ds(kept, LANES), :] = own_ref[k * LANES : (k + 1) * LANES, :]
        sums_sc[pl.ds(sent, LANES), :] = other_ref[k * LANES : (k + 1) * LANES, :]
    ei[...] = sums_sc[0:384, :] * edge_scale
    eo[...] = sums_sc[384:512, :] * edge_scale
    ni[...] = sums_sc[512:768, :] * node_scale
    no[...] = sums_sc[768:896, :] * node_scale
    eib[...] = sums_sc[896:897, :] * edge_scale
    eob[...] = sums_sc[897:898, :] * edge_scale
    nib[...] = sums_sc[898:899, :] * node_scale
    nob[...] = sums_sc[899:900, :] * node_scale


def call(kernel, out_shapes, specs, scratch, args, flops, moved):
    return pl.pallas_call(
        kernel,
        out_shape=[jax.ShapeDtypeStruct(shape, dtype) for shape, dtype in out_shapes],
        in_specs=specs,
        out_specs=[VMEM] * len(out_shapes),
        scratch_shapes=scratch,
        compiler_params=pltpu.CompilerParams(vmem_limit_bytes=40 * 1024 * 1024),
        cost_estimate=pl.CostEstimate(flops=flops, bytes_accessed=moved, transcendentals=0),
    )(*args)


def in_hbm(*values):
    return tuple(pltpu.with_memory_space_constraint(value, pltpu.HBM) for value in values)


def exchanged(messages):
    def near(device):
        return device ^ 1

    def next_chip(device):
        return device + 1 if device % 2 else device - 1

    count = lax.axis_size(AXES)
    quarter = count // 4

    def far_up(device):
        return device + quarter if (device // quarter) % 2 == 0 else device - quarter

    def far_down(device):
        return device - quarter if (device // quarter) % 2 == 0 else device + quarter

    def swapped(message, swap):
        return lax.ppermute(message, AXES, [(s, swap(s) % count) for s in range(count)])

    swaps = (far_up, far_down, next_chip, near)
    return [swapped(message, swap) for message, swap in zip(messages, swaps)]


def swapped_with(value, axis, partner):
    return lax.ppermute(value, axis, [(s, partner(s)) for s in range(lax.axis_size(axis))])


def summed_along_y(mine, theirs):
    half = mine + swapped_with(theirs, "c", lambda s: 1 - s)
    blocks = [half[k * LANES : (k + 1) * LANES] for k in range(4)]
    two = swapped_with(blocks[2], "y", lambda s: s ^ 2)
    three = swapped_with(blocks[3], "y", lambda s: s ^ 3)
    one = swapped_with(blocks[1], "y", lambda s: s ^ 1)
    return (blocks[0] + one) + (two + three)


def summed_along_z(total):
    three = swapped_with(total, "z", lambda s: s ^ 3)
    two = swapped_with(total, "z", lambda s: s ^ 2)
    one = swapped_with(total, "z", lambda s: s ^ 1)
    return (total + one) + (two + three)


def shared(total):
    two = swapped_with(total, "y", lambda s: s ^ 2)
    three = swapped_with(total, "y", lambda s: s ^ 3)
    one = swapped_with(total, "y", lambda s: s ^ 1)
    own = jnp.concatenate([total, one, two, three], axis=0)
    return own, swapped_with(own, "c", lambda s: 1 - s)


def body(
    node_features,
    edge_features,
    node_cotangent,
    edge_cotangent,
    edge_in_weight,
    edge_in_bias,
    edge_out_weight,
    edge_out_bias,
    node_in_weight,
    node_in_bias,
    node_out_weight,
    edge_ends,
    live_elements,
    shared_nodes,
    shared_counts,
    multiplicity,
):
    nodes, width = node_features.shape
    edges = edge_features.shape[0]
    devices = lax.axis_size(AXES)
    element_edges = edge_ends.shape[1]
    lists = shared_nodes.reshape(shared_nodes.shape[1:])
    copies = multiplicity.reshape(nodes // LANES, LANES)
    message = ((LANES, width), F32)
    node_f32 = ((nodes, width), F32)
    node_bf16 = ((nodes, width), BF16)
    edge_f32 = ((edges, width), F32)
    edge_bf16 = ((edges, width), BF16)
    rows_height = padded(element_edges)
    ends_scratch = pltpu.VMEM((8, rows_height), jnp.int32)
    listed = 4 * LANES

    forward_args = in_hbm(
        shared_counts,
        edge_ends,
        lists,
        node_features,
        edge_features,
        edge_in_weight,
        edge_in_bias.reshape(1, -1),
        edge_out_weight,
        edge_out_bias.reshape(1, -1),
    )
    aggregate, *messages, edge_hidden, edge_slope, table, spread_target, pick = call(
        forward_kernel,
        [node_f32]
        + [message] * 4
        + [
            edge_bf16,
            edge_f32,
            ((element_edges, NPE), BF16),
            ((NPE, rows_height), BF16),
            ((listed, nodes), BF16),
        ],
        [HBM] * 9,
        [pltpu.SMEM(shared_counts.shape, jnp.int32)]
        + [pltpu.VMEM(arg.shape, arg.dtype) for arg in forward_args[1:]]
        + [
            pltpu.SemaphoreType.DMA((9,)),
            ends_scratch,
            pltpu.VMEM((rows_height, 4 * LANES), BF16),
        ],
        forward_args,
        2_000_000_000,
        4_000_000,
    )
    arrived = exchanged(messages)
    spread_source, arrive, linear_part, hidden_back, node_cot, copies_wide = call(
        prepare_kernel,
        [
            ((NPE, rows_height), BF16),
            ((nodes, listed), BF16),
            node_f32,
            node_f32,
            node_bf16,
            node_f32,
        ],
        [SMEM, SMEM] + [VMEM] * 8,
        [ends_scratch],
        (
            shared_counts,
            live_elements,
            edge_ends,
            lists,
            copies,
            node_features,
            node_cotangent,
            node_in_weight,
            node_in_bias.reshape(1, -1),
            node_out_weight,
        ),
        1_000_000_000,
        4_000_000,
    )
    consistent_back, *messages, consistent, node_hidden, node_back = call(
        node_kernel,
        [node_f32] + [message] * 4 + [node_bf16] * 3,
        [VMEM] * 11,
        [],
        (
            aggregate,
            *arrived,
            arrive,
            pick,
            linear_part,
            hidden_back,
            copies_wide,
            node_in_weight,
        ),
        600_000_000,
        4_000_000,
    )
    arrived = exchanged(messages)
    node_part, node_terms = call(
        node_sums_kernel,
        [node_f32, ((512, width), F32)],
        [VMEM] * 6,
        [],
        (node_features, consistent, node_hidden, node_back, node_cot, node_in_weight),
        1_000_000_000,
        4_000_000,
    )
    edge_cot, edge_back, edge_sums, mine, theirs = call(
        backward_kernel,
        [
            edge_f32,
            edge_bf16,
            ((nodes, 2 * LANES), F32),
            ((512, width), F32),
            ((512, width), F32),
        ],
        [SMEM] + [VMEM] * 16,
        [
            pltpu.VMEM((rows_height, 2 * LANES), BF16),
            pltpu.VMEM((edges, LANES), BF16),
            pltpu.VMEM((1024, LANES), F32),
        ],
        (
            live_elements,
            consistent_back,
            *arrived,
            arrive,
            table,
            spread_source,
            spread_target,
            edge_cotangent,
            edge_hidden,
            edge_slope,
            edge_features,
            node_features,
            node_terms,
            edge_out_weight,
        ),
        2_000_000_000,
        6_000_000,
    )
    total = summed_along_y(mine, theirs)
    total = summed_along_z(total)
    total, edge_cot = lax.optimization_barrier((total, edge_cot))
    far = swapped_with(total, "z", lambda s: 7 - s)
    node_result, edge_result = call(
        results_kernel,
        [node_bf16, edge_bf16],
        [VMEM] * 5,
        [],
        (edge_cot, edge_back, edge_sums, node_part, edge_in_weight),
        2_000_000_000,
        6_000_000,
    )
    total, far, node_result = lax.optimization_barrier((total, far, node_result))
    own, other = shared(total + far)
    edge_scale = 1.0 / math.sqrt(edges * devices)
    node_scale = 1.0 / math.sqrt(nodes * devices)

    def finish(*refs):
        finish_kernel(edge_scale, node_scale, *refs)

    ei, eib, eo, eob, ni, nib, no, nob = call(
        finish,
        [
            ((384, width), F32),
            ((1, width), F32),
            ((128, width), F32),
            ((1, width), F32),
            ((256, width), F32),
            ((1, width), F32),
            ((128, width), F32),
            ((1, width), F32),
        ],
        [VMEM] * 2,
        [pltpu.VMEM((1024, LANES), F32)],
        (own, other),
        1_000_000,
        1_000_000,
    )
    return (
        node_result,
        edge_result,
        ei,
        eib.reshape(-1),
        eo,
        eob.reshape(-1),
        ni,
        nib.reshape(-1),
        no,
        nob.reshape(-1),
    )


def solution(mesh):
    grid = mesh.devices.reshape(8, 4, 2, 4)
    mesh = Mesh(grid, ("z", "y", "c", "rep"))
    rows = ("rep", "z", "y", "c")
    in_specs = (
        P(rows, None),
        P(rows, None),
        P(rows, None),
        P(rows, None),
        P(),
        P(),
        P(),
        P(),
        P(),
        P(),
        P(),
        P(),
        P(rows),
        P(rows, None, None),
        P(rows, None),
        P(rows),
    )
    out_specs = (
        P(rows, None),
        P(rows, None),
        P("rep", None),
        P("rep"),
        P("rep", None),
        P("rep"),
        P("rep", None),
        P("rep"),
        P("rep", None),
        P("rep"),
    )
    return jax.shard_map(body, mesh=mesh, in_specs=in_specs, out_specs=out_specs, check_vma=False)
```

time: 85.8 us -> 71.5 us (0.83)
  blocking collectives: 32.4 us -> 0 us
  starting transfers between devices: 22.2 us -> 41.6 us
  local copies, waits for them, and re-layouts: 7.12 us -> 0.47 us
  waiting for transfers between devices: 9.25 us -> 12.1 us
  Pallas kernels: 12.8 us -> 14.6 us
    all_to_all x2 -> x0, blocking collectives: 32.4 us -> none  [the longest x1 17.4 us: body(): share = lax.all_to_all(half, ('z', 'y'), 0, 0, tiled=True).sum(axis=0)]
    ppermute x10 -> x20, starting transfers between devices: 22.2 us -> 41.6 us  [the longest x12 21.3 us: swapped_with(): lax.ppermute(value, axis, [(s, partner(s)) for s in range(lax.axis_size(a...]
    unnamed x40 -> x26, local copies, waits for them, and re-layouts: 7.1 us -> 0.45 us
    ppermute x10 -> x20, waiting for transfers between devices: 9.25 us -> 12.1 us  [the longest x12 11.6 us: swapped_with(): lax.ppermute(value, axis, [(s, partner(s)) for s in range(lax.axis_size(a...]
    pallas_call x4 -> x7, Pallas kernels: 12.8 us -> 14.6 us  [call(): pl.pallas_call(kernel, out_shape=[jax.ShapeDtypeStruct(shape, dtype) for...]
  transfers between devices with their start and end apart: 10 -> 20, of which waited for: 5 -> 10; matrix products, arithmetic and copies ran while one was open for 0% -> 0% of each run, Pallas kernels for 0% -> 5%
where the time goes in v2:
time: 71.5 us; the launch traced here: 70.4 us
  starting transfers between devices  41.6 us (58%)
  Pallas kernels  14.6 us (20%)
  waiting for transfers between devices  12.1 us (17%)
  between operations  1.6 us (2%)
    ppermute x12, starting transfers between devices, swapped_with(): lax.ppermute(value, axis, [(s, partner(s)) for s in range(lax.axis_size(a...  21.3 us
    ppermute x8, starting transfers between devices, swapped(): lax.ppermute(message, AXES, [(s, swap(s) % count) for s in range(count)])  20.3 us
    pallas_call x7, Pallas kernels, call(): pl.pallas_call(kernel, out_shape=[jax.ShapeDtypeStruct(shape, dtype) for...  14.6 us
    ppermute x12, waiting for transfers between devices, swapped_with(): lax.ppermute(value, axis, [(s, partner(s)) for s in range(lax.axis_size(a...  11.6 us
  transfers between devices with their start and end apart: 20, of which 10 were waited for; matrix products, arithmetic and copies ran while one was open for 0% of the time, Pallas kernels for 5%

profile of v2, /device:TPU:1, one launch (start us, length us, event | category | flops | bytes accessed | tf_op | source)
XLA Modules:
  0.0 70.4 jit_solution(8212796269897195852)
XLA Ops:
  0.6 0.0 copy-start.2
  0.7 0.0 copy-start.3
  0.7 0.0 copy-start.5
  0.7 0.0 copy-start.7
  0.7 0.0 copy-start.8
  0.7 0.0 copy-start.9
  0.7 0.0 copy-start.10
  0.7 0.0 copy-start.11
  0.7 0.0 copy-start.12
  0.7 5.2 %shard_map.231 = (f32[1024,128]{1,0:T(8,128)S(1)}, f32[128,128]{1,0:T(8,128)S(1)}, f32[128,128]{1,0:T(8,128)S(1)}, f32[128,128]{1,0:T(8,128)S(1)}, f32[128,128]{...) custom-call(s32[1,4]{1,0:T(1,128)} %counts_ref.1, ...), custom_call_target="tpu_custom_call" | custom-call | flops 2000000000 | bytes 4000000 | tf_op jit(solution)/shard_map/pallas_call | solution.py:333
  5.9 3.9 %collective-permute-start = (f32[128,128]{1,0:T(8,128)S(1)}, f32[128,128]{1,0:T(8,128)S(1)}, u32[]{:S(2)}, u32[]{:S(2)}) collective-permute-start(f32[128,128]{1,0:T(8,128)S(1)} %get-tuple-element.57), channel_id=1, source_target_pairs={{0,64},{4,68},{8,72},{12,76},{16,80},{20,84},{24,88},{28,92},{32,9... | collective-permute-start | bytes 196616 | tf_op jit(solution)/shard_map/ppermute | solution.py:365
  9.8 4.2 %collective-permute-start.1 = (f32[128,128]{1,0:T(8,128)S(1)}, f32[128,128]{1,0:T(8,128)S(1)}, u32[]{:S(2)}, u32[]{:S(2)}) collective-permute-start(f32[128,128]{1,0:T(8,128)S(1)} %get-tuple-element.58), channel_id=1, source_target_pairs={{0,192},{4,196},{8,200},{12,204},{16,208},{20,212},{24,216},{28,22... | collective-permute-start | bytes 196616 | tf_op jit(solution)/shard_map/ppermute | solution.py:365
  14.0 2.4 %collective-permute-start.2 = (f32[128,128]{1,0:T(8,128)S(1)}, f32[128,128]{1,0:T(8,128)S(1)}, u32[]{:S(2)}, u32[]{:S(2)}) collective-permute-start(f32[128,128]{1,0:T(8,128)S(1)} %get-tuple-element.59), channel_id=1, source_target_pairs={{0,252},{4,8},{8,4},{12,16},{16,12},{20,24},{24,20},{28,32},{32,28... | collective-permute-start | bytes 196616 | tf_op jit(solution)/shard_map/ppermute | solution.py:365
  16.4 0.3 collective-permute-start.3
  17.4 0.0 copy-done.2
  17.4 0.0 copy-done.3
  17.4 0.0 copy-done.5
  17.4 0.0 copy-done.7
  17.4 0.0 copy-done.8
  17.4 1.3 %shard_map.232 = (bf16[512,1408]{1,0:T(8,128)(2,1)S(1)}, bf16[1024,512]{1,0:T(8,128)(2,1)S(1)}, f32[1024,128]{1,0:T(8,128)S(1)}, f32[1024,128]{1,0:T(8,128)S(1)}...) custom-call(s32[1,4]{1,0:T(1,128)S(1)} %copy-done.11, s32[1]{0:T(128)S(6)} %copy.26.live_ref, ...), custom_call_target="tpu_custom_call" | custom-call | flops 1000000000 | bytes 4000000 | tf_op jit(solution)/shard_map/pallas_call | solution.py:333
  18.7 0.0 collective-permute-done.in0
  18.7 0.0 collective-permute-done.1.in1
  18.7 0.0 collective-permute-done.2.in2
  18.8 0.0 collective-permute-done.3.in3
  18.8 1.4 %shard_map.233 = (f32[1024,128]{1,0:T(8,128)S(1)}, f32[128,128]{1,0:T(8,128)S(1)}, f32[128,128]{1,0:T(8,128)S(1)}, f32[128,128]{1,0:T(8,128)S(1)}, f32[128,128]{...) custom-call(f32[1024,128]{1,0:T(8,128)S(1)} %get-tuple-element.56.agg_, ...), custom_call_target="tpu_custom_call" | custom-call | flops 600000000 | bytes 4000000 | tf_op jit(solution)/shard_map/pallas_call | solution.py:333
  20.2 2.2 %collective-permute-start.4 = (f32[128,128]{1,0:T(8,128)S(1)}, f32[128,128]{1,0:T(8,128)S(1)}, u32[]{:S(2)}, u32[]{:S(2)}) collective-permute-start(f32[128,128]{1,0:T(8,128)S(1)} %get-tuple-element.67), channel_id=1, source_target_pairs={{0,64},{4,68},{8,72},{12,76},{16,80},{20,84},{24,88},{28,92},{32,9... | collective-permute-start | bytes 196616 | tf_op jit(solution)/shard_map/ppermute | solution.py:365
  22.3 2.4 %collective-permute-start.5 = (f32[128,128]{1,0:T(8,128)S(1)}, f32[128,128]{1,0:T(8,128)S(1)}, u32[]{:S(2)}, u32[]{:S(2)}) collective-permute-start(f32[128,128]{1,0:T(8,128)S(1)} %get-tuple-element.68), channel_id=1, source_target_pairs={{0,192},{4,196},{8,200},{12,204},{16,208},{20,212},{24,216},{28,22... | collective-permute-start | bytes 196616 | tf_op jit(solution)/shard_map/ppermute | solution.py:365
  24.7 1.0 %collective-permute-start.6 = (f32[128,128]{1,0:T(8,128)S(1)}, f32[128,128]{1,0:T(8,128)S(1)}, u32[]{:S(2)}, u32[]{:S(2)}) collective-permute-start(f32[128,128]{1,0:T(8,128)S(1)} %get-tuple-element.69), channel_id=1, source_target_pairs={{0,252},{4,8},{8,4},{12,16},{16,12},{20,24},{24,20},{28,32},{32,28... | collective-permute-start | bytes 196616 | tf_op jit(solution)/shard_map/ppermute | solution.py:365
  25.8 3.9 %collective-permute-start.7 = (f32[128,128]{1,0:T(8,128)S(1)}, f32[128,128]{1,0:T(8,128)S(1)}, u32[]{:S(2)}, u32[]{:S(2)}) collective-permute-start(f32[128,128]{1,0:T(8,128)S(1)} %get-tuple-element.70), channel_id=1, source_target_pairs={{0,4},{4,0},{8,12},{12,8},{16,20},{20,16},{24,28},{28,24},{32,36},... | collective-permute-start | bytes 196616 | tf_op jit(solution)/shard_map/ppermute | solution.py:365
  29.7 0.5 shard_map.234
  30.1 0.0 collective-permute-done.4.in0
  30.2 0.0 collective-permute-done.5.in1
  30.2 0.0 collective-permute-done.6.in2
  30.2 0.4 collective-permute-done.7.in3
  30.6 0.2 copy-done
  30.8 0.2 copy-done.1
  31.0 3.9 %shard_map.235 = (f32[2688,128]{1,0:T(8,128)S(1)}, bf16[2688,128]{1,0:T(8,128)(2,1)S(1)}, f32[1024,256]{1,0:T(8,128)S(1)}, f32[512,128]{1,0:T(8,128)S(1)}, f32[512,128]{1,0:T(8,128)S(1)}) custom-call(s32[1]{0:T(128)S(6)} %copy.26.live_ref, f32[1024,128]{1,0:T(8,128)S(1)} %get-tuple-element.66.cback_ref, f32[128,128]{1,0:T(8,128)S(1)} %collective-permute-done.4.in0, ...), custom_call_target="tpu_custom_call" | custom-call | flops 2000000000 | bytes 6000000 | tf_op jit(solution)/shard_map/pallas_call | solution.py:333
  34.9 0.0 copy-start.6
  34.9 4.1 %collective-permute-start.8 = (f32[512,128]{1,0:T(8,128)S(1)}, f32[512,128]{1,0:T(8,128)S(1)}, u32[]{:S(2)}, u32[]{:S(2)}) collective-permute-start(f32[512,128]{1,0:T(8,128)S(1)} %get-tuple-element.82), channel_id=1, source_target_pairs={{0,4},{4,0},{1,5},{5,1},{2,6},{6,2},{3,7},{7,3},{8,12},{12,8},{9,1... | collective-permute-start | bytes 786440 | tf_op jit(solution)/shard_map/ppermute | solution.py:372
  39.0 1.2 %collective-permute-done.8 = f32[512,128]{1,0:T(8,128)S(1)} collective-permute-done((f32[512,128]{1,0:T(8,128)S(1)}, f32[512,128]{1,0:T(8,128)S(1)}, u32[]{:S(2)}, u32[]{:S(2)}) %collective-permute-start.8) | collective-permute-done | bytes 262176 | tf_op jit(solution)/shard_map/ppermute | solution.py:372
  40.2 0.1 collective-permute-start.11
  40.3 0.1 collective-permute-start.10
  40.4 3.1 %collective-permute-start.9 = (f32[128,128]{1,0:T(8,128)S(1)}, f32[128,128]{1,0:T(8,128)S(1)}, u32[]{:S(2)}, u32[]{:S(2)}) collective-permute-start(f32[128,128]{1,0:T(8,128)S(1)} %get-tuple-element.104), channel_id=1, source_target_pairs={{0,8},{8,0},{16,24},{24,16},{1,9},{9,1},{17,25},{25,17},{2,10},{10... | collective-permute-start | bytes 196616 | tf_op jit(solution)/shard_map/ppermute | solution.py:372
  43.5 2.7 %collective-permute-done.11 = f32[128,128]{1,0:T(8,128)S(1)} collective-permute-done((f32[128,128]{1,0:T(8,128)S(1)}, f32[128,128]{1,0:T(8,128)S(1)}, u32[]{:S(2)}, u32[]{:S(2)}) %collective-permute-start.11) | collective-permute-done | bytes 65568 | tf_op jit(solution)/shard_map/ppermute | solution.py:372
  46.2 0.0 collective-permute-done.10
  46.2 0.2 collective-permute-done.9
  46.5 0.1 collective-permute-start.14
  46.6 0.1 collective-permute-start.13
  46.7 3.4 %collective-permute-start.12 = (f32[128,128]{1,0:T(8,128)S(1)}, f32[128,128]{1,0:T(8,128)S(1)}, u32[]{:S(2)}, u32[]{:S(2)}) collective-permute-start(f32[128,128]{1,0:T(8,128)S(1)} %fusion), channel_id=1, source_target_pairs={{0,32},{32,0},{64,96},{96,64},{128,160},{160,128},{192,224},{224,1... | collective-permute-start | bytes 196616 | tf_op jit(solution)/shard_map/ppermute | solution.py:372
  50.1 1.4 %collective-permute-done.14 = f32[128,128]{1,0:T(8,128)S(1)} collective-permute-done((f32[128,128]{1,0:T(8,128)S(1)}, f32[128,128]{1,0:T(8,128)S(1)}, u32[]{:S(2)}, u32[]{:S(2)}) %collective-permute-start.14) | collective-permute-done | bytes 65568 | tf_op jit(solution)/shard_map/ppermute | solution.py:372
  51.5 0.0 collective-permute-done.13
  51.5 0.7 collective-permute-done.12
  52.2 1.3 %collective-permute-start.15 = (f32[128,128]{1,0:T(8,128)S(1)}, f32[128,128]{1,0:T(8,128)S(1)}, u32[]{:S(2)}, u32[]{:S(2)}) collective-permute-start(f32[128,128]{1,0:T(8,128)S(1)} %add_add_fusion), channel_id=1, source_target_pairs={{0,224},{32,192},{64,160},{96,128},{128,96},{160,64},{192,32},{224... | collective-permute-start | bytes 196616 | tf_op jit(solution)/shard_map/ppermute | solution.py:372
  53.5 1.6 %shard_map.236 = (bf16[1024,128]{1,0:T(8,128)(2,1)}, bf16[2688,128]{1,0:T(8,128)(2,1)}) custom-call(f32[2688,128]{1,0:T(8,128)S(1)} %get-tuple-element.85.cot_ref, bf16[2688,128]{1,0:T(8,128)(2,1)S(1)} %get-tuple-element.86.eback_ref, f32[1024,256]{1,0:T(8,128)S(1)} %get-tuple-element.87.sums_ref, f32[1024,128]{1,0:T(8,128)S(1)} %get-tuple-element.88.part_ref, ...), custom_call_target="tpu_custom_call" | custom-call | flops 2000000000 | bytes 6000000 | tf_op jit(solution)/shard_map/pallas_call | solution.py:333
  55.0 1.6 %collective-permute-done.15 = f32[128,128]{1,0:T(8,128)S(1)} collective-permute-done((f32[128,128]{1,0:T(8,128)S(1)}, f32[128,128]{1,0:T(8,128)S(1)}, u32[]{:S(2)}, u32[]{:S(2)}) %collective-permute-start.15) | collective-permute-done | bytes 65568 | tf_op jit(solution)/shard_map/ppermute | solution.py:372
  56.6 1.5 %collective-permute-start.18 = (f32[128,128]{1,0:T(8,128)S(1)}, f32[128,128]{1,0:T(8,128)S(1)}, u32[]{:S(2)}, u32[]{:S(2)}) collective-permute-start(f32[128,128]{1,0:T(8,128)S(1)} %add.31), channel_id=1, source_target_pairs={{0,24},{8,16},{16,8},{24,0},{1,25},{9,17},{17,9},{25,1},{2,26},{10... | collective-permute-start | bytes 196616 | tf_op jit(solution)/shard_map/ppermute | solution.py:372
  58.1 0.8 %collective-permute-start.17 = (f32[128,128]{1,0:T(8,128)S(1)}, f32[128,128]{1,0:T(8,128)S(1)}, u32[]{:S(2)}, u32[]{:S(2)}) collective-permute-start(f32[128,128]{1,0:T(8,128)S(1)} %add.31), channel_id=1, source_target_pairs={{0,16},{8,24},{16,0},{24,8},{1,17},{9,25},{17,1},{25,9},{2,18},{10... | collective-permute-start | bytes 196616 | tf_op jit(solution)/shard_map/ppermute | solution.py:372
  58.9 1.0 %collective-permute-start.16 = (f32[128,128]{1,0:T(8,128)S(1)}, f32[128,128]{1,0:T(8,128)S(1)}, u32[]{:S(2)}, u32[]{:S(2)}) collective-permute-start(f32[128,128]{1,0:T(8,128)S(1)} %add.31), channel_id=1, source_target_pairs={{0,8},{8,0},{16,24},{24,16},{1,9},{9,1},{17,25},{25,17},{2,10},{10... | collective-permute-start | bytes 196616 | tf_op jit(solution)/shard_map/ppermute | solution.py:372
  60.0 1.1 %collective-permute-done.18 = f32[128,128]{1,0:T(8,128)S(1)} collective-permute-done((f32[128,128]{1,0:T(8,128)S(1)}, f32[128,128]{1,0:T(8,128)S(1)}, u32[]{:S(2)}, u32[]{:S(2)}) %collective-permute-start.18) | collective-permute-done | bytes 65568 | tf_op jit(solution)/shard_map/ppermute | solution.py:372
  61.0 1.7 %collective-permute-done.17 = f32[128,128]{1,0:T(8,128)S(1)} collective-permute-done((f32[128,128]{1,0:T(8,128)S(1)}, f32[128,128]{1,0:T(8,128)S(1)}, u32[]{:S(2)}, u32[]{:S(2)}) %collective-permute-start.17) | collective-permute-done | bytes 65568 | tf_op jit(solution)/shard_map/ppermute | solution.py:372
  62.7 0.0 collective-permute-done.16
  62.7 5.7 %collective-permute-start.19 = (f32[512,128]{1,0:T(8,128)S(1)}, f32[512,128]{1,0:T(8,128)S(1)}, u32[]{:S(2)}, u32[]{:S(2)}) collective-permute-start(f32[512,128]{1,0:T(8,128)S(1)} %pad_maximum_fusion.refs_0_), channel_id=1, source_target_pairs={{0,4},{4,0},{1,5},{5,1},{2,6},{6,2},{3,7},{7,3},{8,12},{12,8},{9,1... | collective-permute-start | bytes 786440 | tf_op jit(solution)/shard_map/ppermute | solution.py:372
  68.4 1.2 %collective-permute-done.19.refs_1_ = f32[512,128]{1,0:T(8,128)S(1)} collective-permute-done((f32[512,128]{1,0:T(8,128)S(1)}, f32[512,128]{1,0:T(8,128)S(1)}, u32[]{:S(2)}, u32[]{:S(2)}) %collective-permute-start.19) | collective-permute-done | bytes 262176 | tf_op jit(solution)/shard_map/ppermute | solution.py:372
  69.5 0.8 %shard_map.237 = (f32[384,128]{1,0:T(8,128)}, f32[1,128]{1,0:T(1,128)}, f32[128,128]{1,0:T(8,128)}, f32[1,128]{1,0:T(1,128)}, f32[256,128]{1,0:T(8,128)}, /*inde...) custom-call(f32[512,128]{1,0:T(8,128)S(1)} %pad_maximum_fusion.refs_0_, ...), custom_call_target="tpu_custom_call" | custom-call | flops 1000000 | bytes 1000000 | tf_op jit(solution)/shard_map/pallas_call | solution.py:333
  (15 shorter events, 0.1 us)
Async XLA Ops:
  0.6 16.7 %copy-start.2 = (bf16[1024,128]{1,0:T(8,128)(2,1)S(1)}, bf16[1024,128]{1,0:T(8,128)(2,1)}, u32[]{:S(2)}) copy-start(bf16[1024,128]{1,0:T(8,128)(2,1)} %nf_ref.5) | copy-start | bytes 786436
  0.7 16.7 %copy-start.3 = (bf16[256,128]{1,0:T(8,128)(2,1)S(1)}, bf16[256,128]{1,0:T(8,128)(2,1)}, u32[]{:S(2)}) copy-start(bf16[256,128]{1,0:T(8,128)(2,1)} %wn_ref.5) | copy-start | bytes 196612
  0.7 16.7 %copy-start.5 = (bf16[1024,128]{1,0:T(8,128)(2,1)S(1)}, bf16[1024,128]{1,0:T(8,128)(2,1)}, u32[]{:S(2)}) copy-start(bf16[1024,128]{1,0:T(8,128)(2,1)} %nc_ref.1) | copy-start | bytes 786436
  0.7 16.7 %copy-start.7 = (bf16[128,128]{1,0:T(8,128)(2,1)S(1)}, bf16[128,128]{1,0:T(8,128)(2,1)}, u32[]{:S(2)}) copy-start(bf16[128,128]{1,0:T(8,128)(2,1)} %wo_ref.2) | copy-start | bytes 98308
  0.7 16.7 %copy-start.8 = (s32[2,1344]{1,0:T(2,128)S(1)}, s32[2,1344]{1,0:T(2,128)}, u32[]{:S(2)}) copy-start(s32[2,1344]{1,0:T(2,128)} %ends_ref.1) | copy-start | bytes 32260
  0.7 16.7 %copy-start.9 = (s32[1024]{0:T(1024)S(1)}, s32[1024]{0:T(1024)}, u32[]{:S(2)}) copy-start(s32[1024]{0:T(1024)} %param.31) | copy-start | bytes 12292
  0.7 16.7 %copy-start.10 = (s32[1,4,128]{2,1,0:T(4,128)S(1)}, s32[1,4,128]{2,1,0:T(4,128)}, u32[]{:S(2)}) copy-start(s32[1,4,128]{2,1,0:T(4,128)} %param.29) | copy-start | bytes 6148
  0.7 16.7 %copy-start.11 = (s32[1,4]{1,0:T(1,128)S(1)}, s32[1,4]{1,0:T(1,128)}, u32[]{:S(2)}) copy-start(s32[1,4]{1,0:T(1,128)} %counts_ref.1) | copy-start | bytes 52
  0.7 16.7 %copy-start.12 = (f32[128]{0:T(128)S(1)}, f32[128]{0:T(128)}, u32[]{:S(2)}) copy-start(f32[128]{0:T(128)} %param.25) | copy-start | bytes 1540
  5.9 12.8 %collective-permute-start = (f32[128,128]{1,0:T(8,128)S(1)}, f32[128,128]{1,0:T(8,128)S(1)}, u32[]{:S(2)}, u32[]{:S(2)}) collective-permute-start(f32[128,128]{1,0:T(8,128)S(1)} %get-tuple-element.57), channel_id=1, source_target_pairs={{0,64},{4,68},{8,72},{12,76},{16,80},{20,84},{24,88},{28,92},{32,9... | collective-permute-start | bytes 196616 | tf_op jit(solution)/shard_map/ppermute | solution.py:365
  9.8 8.9 %collective-permute-start.1 = (f32[128,128]{1,0:T(8,128)S(1)}, f32[128,128]{1,0:T(8,128)S(1)}, u32[]{:S(2)}, u32[]{:S(2)}) collective-permute-start(f32[128,128]{1,0:T(8,128)S(1)} %get-tuple-element.58), channel_id=1, source_target_pairs={{0,192},{4,196},{8,200},{12,204},{16,208},{20,212},{24,216},{28,22... | collective-permute-start | bytes 196616 | tf_op jit(solution)/shard_map/ppermute | solution.py:365
  14.0 4.7 %collective-permute-start.2 = (f32[128,128]{1,0:T(8,128)S(1)}, f32[128,128]{1,0:T(8,128)S(1)}, u32[]{:S(2)}, u32[]{:S(2)}) collective-permute-start(f32[128,128]{1,0:T(8,128)S(1)} %get-tuple-element.59), channel_id=1, source_target_pairs={{0,252},{4,8},{8,4},{12,16},{16,12},{20,24},{24,20},{28,32},{32,28... | collective-permute-start | bytes 196616 | tf_op jit(solution)/shard_map/ppermute | solution.py:365
  16.4 2.3 %collective-permute-start.3 = (f32[128,128]{1,0:T(8,128)S(1)}, f32[128,128]{1,0:T(8,128)S(1)}, u32[]{:S(2)}, u32[]{:S(2)}) collective-permute-start(f32[128,128]{1,0:T(8,128)S(1)} %get-tuple-element.60), channel_id=1, source_target_pairs={{0,4},{4,0},{8,12},{12,8},{16,20},{20,16},{24,28},{28,24},{32,36},... | collective-permute-start | bytes 196616 | tf_op jit(solution)/shard_map/ppermute | solution.py:365
  20.2 10.0 %collective-permute-start.4 = (f32[128,128]{1,0:T(8,128)S(1)}, f32[128,128]{1,0:T(8,128)S(1)}, u32[]{:S(2)}, u32[]{:S(2)}) collective-permute-start(f32[128,128]{1,0:T(8,128)S(1)} %get-tuple-element.67), channel_id=1, source_target_pairs={{0,64},{4,68},{8,72},{12,76},{16,80},{20,84},{24,88},{28,92},{32,9... | collective-permute-start | bytes 196616 | tf_op jit(solution)/shard_map/ppermute | solution.py:365
  22.3 7.8 %collective-permute-start.5 = (f32[128,128]{1,0:T(8,128)S(1)}, f32[128,128]{1,0:T(8,128)S(1)}, u32[]{:S(2)}, u32[]{:S(2)}) collective-permute-start(f32[128,128]{1,0:T(8,128)S(1)} %get-tuple-element.68), channel_id=1, source_target_pairs={{0,192},{4,196},{8,200},{12,204},{16,208},{20,212},{24,216},{28,22... | collective-permute-start | bytes 196616 | tf_op jit(solution)/shard_map/ppermute | solution.py:365
  24.7 5.4 %collective-permute-start.6 = (f32[128,128]{1,0:T(8,128)S(1)}, f32[128,128]{1,0:T(8,128)S(1)}, u32[]{:S(2)}, u32[]{:S(2)}) collective-permute-start(f32[128,128]{1,0:T(8,128)S(1)} %get-tuple-element.69), channel_id=1, source_target_pairs={{0,252},{4,8},{8,4},{12,16},{16,12},{20,24},{24,20},{28,32},{32,28... | collective-permute-start | bytes 196616 | tf_op jit(solution)/shard_map/ppermute | solution.py:365
  25.8 4.8 %collective-permute-start.7 = (f32[128,128]{1,0:T(8,128)S(1)}, f32[128,128]{1,0:T(8,128)S(1)}, u32[]{:S(2)}, u32[]{:S(2)}) collective-permute-start(f32[128,128]{1,0:T(8,128)S(1)} %get-tuple-element.70), channel_id=1, source_target_pairs={{0,4},{4,0},{8,12},{12,8},{16,20},{20,16},{24,28},{28,24},{32,36},... | collective-permute-start | bytes 196616 | tf_op jit(solution)/shard_map/ppermute | solution.py:365
  29.7 1.1 %copy-start = (bf16[2688,128]{1,0:T(8,128)(2,1)S(1)}, bf16[2688,128]{1,0:T(8,128)(2,1)}, u32[]{:S(2)}) copy-start(bf16[2688,128]{1,0:T(8,128)(2,1)} %ef_ref.1) | copy-start | bytes 2064388
  29.7 1.3 %copy-start.1 = (bf16[2688,128]{1,0:T(8,128)(2,1)S(1)}, bf16[2688,128]{1,0:T(8,128)(2,1)}, u32[]{:S(2)}) copy-start(bf16[2688,128]{1,0:T(8,128)(2,1)} %ec_ref.1) | copy-start | bytes 2064388
  29.7 1.3 %copy-start.4 = (bf16[128,128]{1,0:T(8,128)(2,1)S(1)}, bf16[128,128]{1,0:T(8,128)(2,1)}, u32[]{:S(2)}) copy-start(bf16[128,128]{1,0:T(8,128)(2,1)} %wo_ref.3) | copy-start | bytes 98308
  34.9 18.6 %copy-start.6 = (bf16[384,128]{1,0:T(8,128)(2,1)S(1)}, bf16[384,128]{1,0:T(8,128)(2,1)}, u32[]{:S(2)}) copy-start(bf16[384,128]{1,0:T(8,128)(2,1)} %wi_ref.1) | copy-start | bytes 294916
  34.9 5.2 %collective-permute-start.8 = (f32[512,128]{1,0:T(8,128)S(1)}, f32[512,128]{1,0:T(8,128)S(1)}, u32[]{:S(2)}, u32[]{:S(2)}) collective-permute-start(f32[512,128]{1,0:T(8,128)S(1)} %get-tuple-element.82), channel_id=1, source_target_pairs={{0,4},{4,0},{1,5},{5,1},{2,6},{6,2},{3,7},{7,3},{8,12},{12,8},{9,1... | collective-permute-start | bytes 786440 | tf_op jit(solution)/shard_map/ppermute | solution.py:372
  40.2 6.1 %collective-permute-start.11 = (f32[128,128]{1,0:T(8,128)S(1)}, f32[128,128]{1,0:T(8,128)S(1)}, u32[]{:S(2)}, u32[]{:S(2)}) collective-permute-start(f32[128,128]{1,0:T(8,128)S(1)} %get-tuple-element.102), channel_id=1, source_target_pairs={{0,24},{8,16},{16,8},{24,0},{1,25},{9,17},{17,9},{25,1},{2,26},{10... | collective-permute-start | bytes 196616 | tf_op jit(solution)/shard_map/ppermute | solution.py:372
  40.3 6.0 %collective-permute-start.10 = (f32[128,128]{1,0:T(8,128)S(1)}, f32[128,128]{1,0:T(8,128)S(1)}, u32[]{:S(2)}, u32[]{:S(2)}) collective-permute-start(f32[128,128]{1,0:T(8,128)S(1)} %get-tuple-element.103), channel_id=1, source_target_pairs={{0,16},{8,24},{16,0},{24,8},{1,17},{9,25},{17,1},{25,9},{2,18},{10... | collective-permute-start | bytes 196616 | tf_op jit(solution)/shard_map/ppermute | solution.py:372
  40.4 6.1 %collective-permute-start.9 = (f32[128,128]{1,0:T(8,128)S(1)}, f32[128,128]{1,0:T(8,128)S(1)}, u32[]{:S(2)}, u32[]{:S(2)}) collective-permute-start(f32[128,128]{1,0:T(8,128)S(1)} %get-tuple-element.104), channel_id=1, source_target_pairs={{0,8},{8,0},{16,24},{24,16},{1,9},{9,1},{17,25},{25,17},{2,10},{10... | collective-permute-start | bytes 196616 | tf_op jit(solution)/shard_map/ppermute | solution.py:372
  46.5 5.0 %collective-permute-start.14 = (f32[128,128]{1,0:T(8,128)S(1)}, f32[128,128]{1,0:T(8,128)S(1)}, u32[]{:S(2)}, u32[]{:S(2)}) collective-permute-start(f32[128,128]{1,0:T(8,128)S(1)} %fusion), channel_id=1, source_target_pairs={{0,96},{32,64},{64,32},{96,0},{128,224},{160,192},{192,160},{224,1... | collective-permute-start | bytes 196616 | tf_op jit(solution)/shard_map/ppermute | solution.py:372
  46.6 4.9 %collective-permute-start.13 = (f32[128,128]{1,0:T(8,128)S(1)}, f32[128,128]{1,0:T(8,128)S(1)}, u32[]{:S(2)}, u32[]{:S(2)}) collective-permute-start(f32[128,128]{1,0:T(8,128)S(1)} %fusion), channel_id=1, source_target_pairs={{0,64},{32,96},{64,0},{96,32},{128,192},{160,224},{192,128},{224,1... | collective-permute-start | bytes 196616 | tf_op jit(solution)/shard_map/ppermute | solution.py:372
  46.7 5.5 %collective-permute-start.12 = (f32[128,128]{1,0:T(8,128)S(1)}, f32[128,128]{1,0:T(8,128)S(1)}, u32[]{:S(2)}, u32[]{:S(2)}) collective-permute-start(f32[128,128]{1,0:T(8,128)S(1)} %fusion), channel_id=1, source_target_pairs={{0,32},{32,0},{64,96},{96,64},{128,160},{160,128},{192,224},{224,1... | collective-permute-start | bytes 196616 | tf_op jit(solution)/shard_map/ppermute | solution.py:372
  52.2 4.4 %collective-permute-start.15 = (f32[128,128]{1,0:T(8,128)S(1)}, f32[128,128]{1,0:T(8,128)S(1)}, u32[]{:S(2)}, u32[]{:S(2)}) collective-permute-start(f32[128,128]{1,0:T(8,128)S(1)} %add_add_fusion), channel_id=1, source_target_pairs={{0,224},{32,192},{64,160},{96,128},{128,96},{160,64},{192,32},{224... | collective-permute-start | bytes 196616 | tf_op jit(solution)/shard_map/ppermute | solution.py:372
  56.6 4.4 %collective-permute-start.18 = (f32[128,128]{1,0:T(8,128)S(1)}, f32[128,128]{1,0:T(8,128)S(1)}, u32[]{:S(2)}, u32[]{:S(2)}) collective-permute-start(f32[128,128]{1,0:T(8,128)S(1)} %add.31), channel_id=1, source_target_pairs={{0,24},{8,16},{16,8},{24,0},{1,25},{9,17},{17,9},{25,1},{2,26},{10... | collective-permute-start | bytes 196616 | tf_op jit(solution)/shard_map/ppermute | solution.py:372
  58.1 4.6 %collective-permute-start.17 = (f32[128,128]{1,0:T(8,128)S(1)}, f32[128,128]{1,0:T(8,128)S(1)}, u32[]{:S(2)}, u32[]{:S(2)}) collective-permute-start(f32[128,128]{1,0:T(8,128)S(1)} %add.31), channel_id=1, source_target_pairs={{0,16},{8,24},{16,0},{24,8},{1,17},{9,25},{17,1},{25,9},{2,18},{10... | collective-permute-start | bytes 196616 | tf_op jit(solution)/shard_map/ppermute | solution.py:372
  58.9 3.8 %collective-permute-start.16 = (f32[128,128]{1,0:T(8,128)S(1)}, f32[128,128]{1,0:T(8,128)S(1)}, u32[]{:S(2)}, u32[]{:S(2)}) collective-permute-start(f32[128,128]{1,0:T(8,128)S(1)} %add.31), channel_id=1, source_target_pairs={{0,8},{8,0},{16,24},{24,16},{1,9},{9,1},{17,25},{25,17},{2,10},{10... | collective-permute-start | bytes 196616 | tf_op jit(solution)/shard_map/ppermute | solution.py:372
  62.7 6.8 %collective-permute-start.19 = (f32[512,128]{1,0:T(8,128)S(1)}, f32[512,128]{1,0:T(8,128)S(1)}, u32[]{:S(2)}, u32[]{:S(2)}) collective-permute-start(f32[512,128]{1,0:T(8,128)S(1)} %pad_maximum_fusion.refs_0_), channel_id=1, source_target_pairs={{0,4},{4,0},{1,5},{5,1},{2,6},{6,2},{3,7},{7,3},{8,12},{12,8},{9,1... | collective-permute-start | bytes 786440 | tf_op jit(solution)/shard_map/ppermute | solution.py:372

commit v3 on v2

--- a/solution.py
+++ b/solution.py
@@ -10,6 +10,9 @@
 NPE = 512
 LANES = 128
 BLOCK = 256
+FORWARD_BLOCK = 1344
+BACKWARD_BLOCK = 1344
+QUARTER = 120
 F32 = jnp.float32
 BF16 = jnp.bfloat16
 AXES = ("z", "y", "c")
@@ -45,18 +48,21 @@
 
 
 def hot(flags):
-    return jnp.where(flags, 1.0, 0.0).astype(BF16)
+    return jnp.where(flags, jnp.ones(flags.shape, BF16), jnp.zeros(flags.shape, BF16))
 
 
 def pick_table(row, width):
-    column = as_column(row)
+    column = as_column(row).astype(jnp.int16)
     lane = lax.broadcasted_iota(jnp.int32, (LANES, LANES), 1)
-    tiles = [hot(column == lane + start) for start in range(0, width, LANES)]
+    tiles = [hot(column == (lane + start).astype(jnp.int16)) for start in range(0, width, LANES)]
     return jnp.concatenate(tiles, axis=1)
 
 
 def spread_table(row, height):
-    return hot(lax.broadcasted_iota(jnp.int32, (height, row.shape[1]), 0) == row)
+    named = jnp.broadcast_to(row, (16, LANES)).astype(jnp.int16)
+    named = jnp.concatenate([named] * (height // 16), axis=0)
+    place = lax.broadcasted_iota(jnp.int32, (height, LANES), 0).astype(jnp.int16)
+    return hot(place == named)
 
 
 def list_rows(lists_ref, counts_ref):
@@ -70,7 +76,8 @@
         return jnp.where(chosen, first, second), jnp.where(chosen, second, first)
 
     near, next_chip = ordered(core, rows[0], rows[1])
-    return ordered(odd, rows[2], rows[3]) + (next_chip, near)
+    up, down = ordered(odd, rows[2], rows[3])
+    return (next_chip, up, down, near)
 
 
 def outgoing(table_ref, values, refs):
@@ -86,8 +93,25 @@
     return both[:, :LANES] + both[:, LANES:]
 
 
+def spans(count, block):
+    return [(start, min(block, count - start)) for start in range(0, count, block)]
+
+
 def blocks_of(count):
-    return [(start, min(BLOCK, count - start)) for start in range(0, count, BLOCK)]
+    return spans(count, BLOCK)
+
+
+def twice(block):
+    zero = jnp.zeros_like(block)
+    return jnp.concatenate(
+        [jnp.concatenate([block, zero], axis=1), jnp.concatenate([zero, block], axis=1)], axis=0
+    )
+
+
+def beside(ref, start, size, edges):
+    return jnp.concatenate(
+        [ref[start : start + size, :], ref[edges + start : edges + start + size, :]], axis=1
+    )
 
 
 def stage_ends(ends_ref, ends_sc):
@@ -107,7 +131,7 @@
     counts_hbm, ends_hbm, lists_hbm, nf_hbm, ef_hbm, wi_hbm, bi_hbm, wo_hbm, bo_hbm,
     agg_ref, out0, out1, out2, out3, hid_ref, slope_ref, table_ref, spread_ref, pick_ref,
     counts_ref, ends_ref, lists_ref, nf_ref, ef_ref, wi_ref, bi_ref, wo_ref, bo_ref,
-    sems, ends_sc, rows_sc,
+    sems, ends_sc, rows_sc, source_sc,
 ):
     pairs = (
         (ends_hbm, ends_ref),
@@ -130,58 +154,58 @@
     width = padded(edges)
     loads[0].wait()
     stage_ends(ends_ref, ends_sc)
-    degree = jnp.zeros((NPE, LANES), F32)
     for first in range(0, width, LANES):
-        table = spread_table(ends_sc[1:2, first : first + LANES], NPE)
-        spread_ref[:, first : first + LANES] = table
-        degree = degree + table.astype(F32)
-    degree = jnp.sum(degree, axis=1, keepdims=True)
-    loads[1].wait()
-    loads[2].wait()
-    nf = nf_ref[...]
-    from_source = dot(nf, wi_ref[0:128, :]).astype(BF16)
-    from_target = dot(nf, wi_ref[128:256, :]).astype(BF16)
-    table_rows = jnp.concatenate(
-        [
-            jnp.concatenate([from_source[:NPE], from_source[NPE:]], axis=1),
-            jnp.concatenate([from_target[:NPE], from_target[NPE:]], axis=1),
-        ],
-        axis=0,
-    )
-    for load in loads[3:]:
+        spread_ref[:, first : first + LANES] = spread_table(
+            ends_sc[1:2, first : first + LANES], NPE
+        )
+    for start, size in blocks_of(edges):
+        source_sc[start : start + size, :] = edge_rows_table(ends_sc, 0, start, size)
+        table_ref[start : start + size, :] = edge_rows_table(ends_sc, 1, start, size)
+    rows_sc[edges:width, :] = jnp.zeros((width - edges, 2 * LANES), BF16)
+    for load in loads[1:]:
         load.wait()
-    for start, size in blocks_of(edges):
-        by_target = edge_rows_table(ends_sc, 1, start, size)
-        table_ref[start : start + size, :] = by_target
-        table = jnp.concatenate([edge_rows_table(ends_sc, 0, start, size), by_target], axis=1)
-        ends_part = dot(table, table_rows)
-        for slot in range(2):
-            first = slot * edges + start
-            own = ef_ref[first : first + size, :]
-            linear = (
-                ends_part[:, slot * LANES : (slot + 1) * LANES]
-                + dot(own, wi_ref[256:384, :])
-                + bi_ref[...]
-            )
-            squashed = jax.nn.sigmoid(linear)
-            hidden = (linear * squashed).astype(BF16)
-            hid_ref[first : first + size, :] = hidden
-            slope_ref[first : first + size, :] = squashed * (1.0 + linear * (1.0 - squashed))
-            rows_sc[start : start + size, slot * LANES : (slot + 1) * LANES] = own
-            rows_sc[start : start + size, (2 + slot) * LANES : (3 + slot) * LANES] = hidden
-    rows_sc[edges:width, :] = jnp.zeros((width - edges, 4 * LANES), BF16)
+    values_rows = list_rows(lists_ref, counts_ref)
+    for k, row in enumerate(values_rows):
+        pick_ref[k * LANES : (k + 1) * LANES, :] = pick_table(row, nf_ref.shape[0])
+    in_weights = jnp.concatenate([wi_ref[0:128, :], wi_ref[128:256, :]], axis=1)
+    ends_rows = dot(nf_ref[...], in_weights).astype(BF16)
+    source_rows = jnp.concatenate([ends_rows[:NPE, :LANES], ends_rows[NPE:, :LANES]], axis=1)
+    target_rows = jnp.concatenate([ends_rows[:NPE, LANES:], ends_rows[NPE:, LANES:]], axis=1)
+    own_weight = twice(wi_ref[256:384, :])
+    out_weight = twice(wo_ref[...])
+    in_bias = jnp.concatenate([bi_ref[...]] * 2, axis=1)
+    out_bias = jnp.concatenate([bo_ref[...]] * 2, axis=1)
+    for start, size in spans(edges, FORWARD_BLOCK):
+        own = beside(ef_ref, start, size, edges)
+        linear = (
+            dot(source_sc[start : start + size, :], source_rows)
+            + dot(table_ref[start : start + size, :], target_rows)
+            + dot(own, own_weight)
+            + in_bias
+        )
+        squashed = jax.nn.sigmoid(linear)
+        hidden = (linear * squashed).astype(BF16)
+        hid_ref[start : start + size, :] = hidden
+        slope_ref[start : start + size, :] = squashed * (1.0 + linear * (1.0 - squashed))
+        rows_sc[start : start + size, :] = (
+            own.astype(F32) + dot(hidden, out_weight) + out_bias
+        ).astype(BF16)
     sums = dot(spread_ref[...], rows_sc[...])
-    for slot in range(2):
-        high, low = split(sums[:, (2 + slot) * LANES : (3 + slot) * LANES])
-        agg_ref[slot * NPE : (slot + 1) * NPE, :] = (
-            sums[:, slot * LANES : (slot + 1) * LANES]
-            + (dot(high, wo_ref[...]) + dot(low, wo_ref[...]))
-            + degree * bo_ref[...]
-        )
-    values = agg_ref[...]
-    for k, row in enumerate(list_rows(lists_ref, counts_ref)):
-        pick_ref[k * LANES : (k + 1) * LANES, :] = pick_table(row, values.shape[0])
-    outgoing(pick_ref, values, (out0, out1, out2, out3))
+    agg_ref[0:NPE, :] = sums[:, :LANES]
+    agg_ref[NPE:, :] = sums[:, LANES:]
+    outgoing(pick_ref, agg_ref[...], (out0, out1, out2, out3))
+
+
+def block_starts():
+    core = lax.axis_index("c")
+    place = lax.axis_index("y")
+    starts = []
+    for k in range(4):
+        block = lax.bitwise_xor(place, k) * QUARTER
+        kept = pl.multiple_of(core * (4 * QUARTER) + block, 8)
+        sent = pl.multiple_of((1 - core) * (4 * QUARTER) + block, 8)
+        starts.append((kept, sent))
+    return starts
 
 
 def prepare_kernel(
@@ -225,9 +249,9 @@
     back_ref[...] = back
 
 
-def node_sums_kernel(
-    nf_ref, cons_ref, hid_ref, back_ref, cot_ref, wn_ref,
-    part_ref, terms_ref,
+def side_kernel(
+    live_ref, nf_ref, cons_ref, hid_ref, back_ref, cot_ref, wn_ref, ef_ref, ec_ref, ehid_ref,
+    spread_ref, wo_ref, part_ref, terms_ref, given_ref, eft_ref, nft_ref, hsumt_ref, outw_ref, wot_ref,
 ):
     back = back_ref[...]
     cot_half = cot_ref[...]
@@ -236,66 +260,73 @@
     terms_ref[0:128, :] = dot_rows(nf_ref[...], back)
     terms_ref[128:256, :] = dot_rows(cons_ref[...], back)
     terms_ref[256:384, :] = dot_rows(hid_ref[...], cot_half)
-    terms_ref[384:386, :] = jnp.zeros((2, LANES), F32)
+    terms_ref[384:448, :] = jnp.zeros((64, LANES), F32)
     terms_ref[386:387, :] = jnp.sum(back.astype(F32), axis=0, keepdims=True)
     terms_ref[387:388, :] = jnp.sum(cot, axis=0, keepdims=True)
-    terms_ref[388:512, :] = jnp.zeros((124, LANES), F32)
+    edges = ef_ref.shape[0] // 2
+    live = jnp.full((edges, LANES), live_ref[0], jnp.int32)
+    width = eft_ref.shape[1]
+    for slot in range(2):
+        rows = slice(slot * edges, (slot + 1) * edges)
+        lanes = slice(slot * LANES, (slot + 1) * LANES)
+        given_ref[:, lanes] = jnp.where(live > slot, ec_ref[rows, :].astype(F32), 0.0).astype(BF16)
+        eft_ref[lanes, 0:edges] = jnp.transpose(ef_ref[rows, :].astype(F32)).astype(BF16)
+    eft_ref[:, edges:] = jnp.zeros((2 * LANES, width - edges), BF16)
+    nft_ref[...] = jnp.transpose(nf_ref[...].astype(F32)).astype(BF16)
+    hidden = ehid_ref[...]
+    filler = jnp.zeros((width - edges, 2 * LANES), BF16)
+    sums = dot(spread_ref[...], jnp.concatenate([hidden, filler], axis=0))
+    for slot in range(2):
+        lanes = slice(slot * LANES, (slot + 1) * LANES)
+        high, low = split(jnp.transpose(sums[:, lanes]))
+        hsumt_ref[0:LANES, slot * NPE : (slot + 1) * NPE] = high
+        hsumt_ref[LANES:, slot * NPE : (slot + 1) * NPE] = low
+    both = dot_rows(hidden, given_ref[...])
+    outw_ref[...] = both[:LANES, :LANES] + both[LANES:, LANES:]
+    wot_ref[...] = twice(jnp.transpose(wo_ref[...].astype(F32)).astype(BF16))
 
 
 def backward_kernel(
-    live_ref, cback_ref, in0, in1, in2, in3, arrive_ref, table_ref, spread_s_ref, spread_t_ref,
-    ec_ref, hid_ref, slope_ref, ef_ref, nf_ref, terms_ref, wo_ref,
+    cback_ref, in0, in1, in2, in3, arrive_ref, table_ref, spread_s_ref, spread_t_ref,
+    given_ref, slope_ref, eft_ref, nft_ref, hsumt_ref, outw_ref, terms_ref, wot_ref,
     cot_ref, eback_ref, sums_ref, mine_ref, theirs_ref,
-    rows_sc, half_sc, terms_sc,
+    terms_sc,
 ):
     edges = table_ref.shape[0]
     width = padded(edges)
     agg_back = (cback_ref[...] + incoming(arrive_ref, (in0, in1, in2, in3))).astype(BF16)
     table_rows = jnp.concatenate([agg_back[:NPE], agg_back[NPE:]], axis=1)
-    in_bias = jnp.zeros((1, LANES), F32)
-    out_bias = jnp.zeros((1, LANES), F32)
-    for start, size in blocks_of(edges):
-        gathered = dot(table_ref[start : start + size, :], table_rows)
-        for slot in range(2):
-            first = slot * edges + start
-            given = ec_ref[first : first + size, :].astype(F32)
-            given = jnp.where(
-                jnp.full((size, LANES), live_ref[0], jnp.int32) > slot, given, 0.0
-            )
-            cot = given + gathered[:, slot * LANES : (slot + 1) * LANES]
-            half = cot.astype(BF16)
-            back = (
-                dot_t(half, wo_ref[...]) * slope_ref[first : first + size, :]
-            ).astype(BF16)
-            cot_ref[first : first + size, :] = cot
-            half_sc[first : first + size, :] = half
-            eback_ref[first : first + size, :] = back
-            rows_sc[start : start + size, slot * LANES : (slot + 1) * LANES] = back
-            in_bias = in_bias + jnp.sum(back.astype(F32), axis=0, keepdims=True)
-            out_bias = out_bias + jnp.sum(half.astype(F32), axis=0, keepdims=True)
-    rows_sc[edges:width, :] = jnp.zeros((width - edges, 2 * LANES), BF16)
-    by_source = dot(spread_s_ref[...], rows_sc[...])
-    by_target = dot(spread_t_ref[...], rows_sc[...])
+    in_bias = jnp.zeros((1, 2 * LANES), F32)
+    out_bias = jnp.zeros((1, 2 * LANES), F32)
+    for start, size in spans(edges, BACKWARD_BLOCK):
+        rows = slice(start, start + size)
+        cot = given_ref[rows, :].astype(F32) + dot(table_ref[rows, :], table_rows)
+        half = cot.astype(BF16)
+        back = (dot(half, wot_ref[...]) * slope_ref[rows, :]).astype(BF16)
+        cot_ref[rows, :] = cot
+        eback_ref[rows, :] = back
+        in_bias = in_bias + jnp.sum(back.astype(F32), axis=0, keepdims=True)
+        out_bias = out_bias + jnp.sum(half.astype(F32), axis=0, keepdims=True)
+    eback_ref[edges:width, :] = jnp.zeros((width - edges, 2 * LANES), BF16)
+    by_source = dot(spread_s_ref[...], eback_ref[...])
+    by_target = dot(spread_t_ref[...], eback_ref[...])
+    by_edge = dot(eft_ref[...], eback_ref[...])
     sums_ref[0:NPE, 0:LANES] = by_source[:, :LANES]
     sums_ref[NPE : 2 * NPE, 0:LANES] = by_source[:, LANES:]
     sums_ref[0:NPE, LANES:] = by_target[:, :LANES]
     sums_ref[NPE : 2 * NPE, LANES:] = by_target[:, LANES:]
-    both = dot_rows(nf_ref[...], jnp.concatenate(split(sums_ref[...]), axis=1))
+    both = dot(nft_ref[...], jnp.concatenate(split(sums_ref[...]), axis=1))
     terms_sc[0:128, :] = both[:, 0:128] + both[:, 256:384]
     terms_sc[128:256, :] = both[:, 128:256] + both[:, 384:512]
-    terms_sc[256:384, :] = dot_rows(ef_ref[...], eback_ref[...])
-    terms_sc[384:512, :] = dot_rows(hid_ref[...], half_sc[...])
-    terms_sc[512:1024, :] = terms_ref[...]
-    terms_sc[896:897, :] = in_bias
-    terms_sc[897:898, :] = out_bias
-    core = lax.axis_index("c")
-    place = lax.axis_index("y")
-    for k in range(4):
-        block = lax.bitwise_xor(place, k) * LANES
-        kept = pl.multiple_of(core * 512 + block, LANES)
-        sent = pl.multiple_of((1 - core) * 512 + block, LANES)
-        mine_ref[k * LANES : (k + 1) * LANES, :] = terms_sc[pl.ds(kept, LANES), :]
-        theirs_ref[k * LANES : (k + 1) * LANES, :] = terms_sc[pl.ds(sent, LANES), :]
+    terms_sc[256:384, :] = by_edge[:LANES, :LANES] + by_edge[LANES:, LANES:]
+    shared_part = dot(hsumt_ref[...], agg_back)
+    terms_sc[384:512, :] = outw_ref[...] + (shared_part[:LANES] + shared_part[LANES:])
+    terms_sc[512:960, :] = terms_ref[...]
+    terms_sc[896:897, :] = in_bias[:, :LANES] + in_bias[:, LANES:]
+    terms_sc[897:898, :] = out_bias[:, :LANES] + out_bias[:, LANES:]
+    for k, (kept, sent) in enumerate(block_starts()):
+        mine_ref[k * QUARTER : (k + 1) * QUARTER, :] = terms_sc[pl.ds(kept, QUARTER), :]
+        theirs_ref[k * QUARTER : (k + 1) * QUARTER, :] = terms_sc[pl.ds(sent, QUARTER), :]
 
 
 def results_kernel(cot_ref, eback_ref, sums_ref, part_ref, wi_ref, node_ref, edge_ref):
@@ -305,20 +336,19 @@
         + (dot_t(high[:, :LANES], wi_ref[0:128, :]) + dot_t(low[:, :LANES], wi_ref[0:128, :]))
         + (dot_t(high[:, LANES:], wi_ref[128:256, :]) + dot_t(low[:, LANES:], wi_ref[128:256, :]))
     ).astype(BF16)
-    edge_ref[...] = (cot_ref[...] + dot_t(eback_ref[...], wi_ref[256:384, :])).astype(BF16)
+    edges = cot_ref.shape[0]
+    own_weight = twice(jnp.transpose(wi_ref[256:384, :].astype(F32)).astype(BF16))
+    result = (cot_ref[...] + dot(eback_ref[0:edges, :], own_weight)).astype(BF16)
+    edge_ref[0:edges, :] = result[:, :LANES]
+    edge_ref[edges:, :] = result[:, LANES:]
 
 
 def finish_kernel(
     edge_scale, node_scale, own_ref, other_ref, ei, eib, eo, eob, ni, nib, no, nob, sums_sc
 ):
-    core = lax.axis_index("c")
-    place = lax.axis_index("y")
-    for k in range(4):
-        block = lax.bitwise_xor(place, k) * LANES
-        kept = pl.multiple_of(core * 512 + block, LANES)
-        sent = pl.multiple_of((1 - core) * 512 + block, LANES)
-        sums_sc[pl.ds(kept, LANES), :] = own_ref[k * LANES : (k + 1) * LANES, :]
-        sums_sc[pl.ds(sent, LANES), :] = other_ref[k * LANES : (k + 1) * LANES, :]
+    for k, (kept, sent) in enumerate(block_starts()):
+        sums_sc[pl.ds(kept, QUARTER), :] = own_ref[k * QUARTER : (k + 1) * QUARTER, :]
+        sums_sc[pl.ds(sent, QUARTER), :] = other_ref[k * QUARTER : (k + 1) * QUARTER, :]
     ei[...] = sums_sc[0:384, :] * edge_scale
     eo[...] = sums_sc[384:512, :] * edge_scale
     ni[...] = sums_sc[512:768, :] * node_scale
@@ -364,7 +394,7 @@
     def swapped(message, swap):
         return lax.ppermute(message, AXES, [(s, swap(s) % count) for s in range(count)])
 
-    swaps = (far_up, far_down, next_chip, near)
+    swaps = (next_chip, far_up, far_down, near)
     return [swapped(message, swap) for message, swap in zip(messages, swaps)]
 
 
@@ -374,7 +404,7 @@
 
 def summed_along_y(mine, theirs):
     half = mine + swapped_with(theirs, "c", lambda s: 1 - s)
-    blocks = [half[k * LANES : (k + 1) * LANES] for k in range(4)]
+    blocks = [half[k * QUARTER : (k + 1) * QUARTER] for k in range(4)]
     two = swapped_with(blocks[2], "y", lambda s: s ^ 2)
     three = swapped_with(blocks[3], "y", lambda s: s ^ 3)
     one = swapped_with(blocks[1], "y", lambda s: s ^ 1)
@@ -423,7 +453,8 @@
     message = ((LANES, width), F32)
     node_f32 = ((nodes, width), F32)
     node_bf16 = ((nodes, width), BF16)
-    edge_f32 = ((edges, width), F32)
+    both_f32 = ((element_edges, 2 * LANES), F32)
+    both_bf16 = ((element_edges, 2 * LANES), BF16)
     edge_bf16 = ((edges, width), BF16)
     rows_height = padded(element_edges)
     ends_scratch = pltpu.VMEM((8, rows_height), jnp.int32)
@@ -445,8 +476,8 @@
         [node_f32]
         + [message] * 4
         + [
-            edge_bf16,
-            edge_f32,
+            both_bf16,
+            both_f32,
             ((element_edges, NPE), BF16),
             ((NPE, rows_height), BF16),
             ((listed, nodes), BF16),
@@ -457,7 +488,8 @@
         + [
             pltpu.SemaphoreType.DMA((9,)),
             ends_scratch,
-            pltpu.VMEM((rows_height, 4 * LANES), BF16),
+            pltpu.VMEM((rows_height, 2 * LANES), BF16),
+            pltpu.VMEM((element_edges, NPE), BF16),
         ],
         forward_args,
         2_000_000_000,
@@ -510,45 +542,64 @@
         4_000_000,
     )
     arrived = exchanged(messages)
-    node_part, node_terms = call(
-        node_sums_kernel,
-        [node_f32, ((512, width), F32)],
-        [VMEM] * 6,
+    node_part, node_terms, given, edges_across, nodes_across, sums_across, out_part, out_across = call(
+        side_kernel,
+        [
+            node_f32,
+            ((448, width), F32),
+            both_bf16,
+            ((2 * LANES, rows_height), BF16),
+            ((width, nodes), BF16),
+            ((2 * width, nodes), BF16),
+            message,
+            ((2 * LANES, 2 * LANES), BF16),
+        ],
+        [SMEM] + [VMEM] * 11,
         [],
-        (node_features, consistent, node_hidden, node_back, node_cot, node_in_weight),
+        (
+            live_elements,
+            node_features,
+            consistent,
+            node_hidden,
+            node_back,
+            node_cot,
+            node_in_weight,
+            edge_features,
+            edge_cotangent,
+            edge_hidden,
+            spread_target,
+            edge_out_weight,
+        ),
         1_000_000_000,
         4_000_000,
     )
+    half_terms = ((4 * QUARTER, width), F32)
     edge_cot, edge_back, edge_sums, mine, theirs = call(
         backward_kernel,
         [
-            edge_f32,
-            edge_bf16,
+            both_f32,
+            ((rows_height, 2 * LANES), BF16),
             ((nodes, 2 * LANES), F32),
-            ((512, width), F32),
-            ((512, width), F32),
+            half_terms,
+            half_terms,
         ],
-        [SMEM] + [VMEM] * 16,
-        [
-            pltpu.VMEM((rows_height, 2 * LANES), BF16),
-            pltpu.VMEM((edges, LANES), BF16),
-            pltpu.VMEM((1024, LANES), F32),
-        ],
+        [VMEM] * 17,
+        [pltpu.VMEM((8 * QUARTER, LANES), F32)],
         (
-            live_elements,
             consistent_back,
             *arrived,
             arrive,
             table,
             spread_source,
             spread_target,
-            edge_cotangent,
-            edge_hidden,
+            given,
             edge_slope,
-            edge_features,
-            node_features,
+            edges_across,
+            nodes_across,
+            sums_across,
+            out_part,
             node_terms,
-            edge_out_weight,
+            out_across,
         ),
         2_000_000_000,
         6_000_000,
@@ -587,7 +638,7 @@
             ((1, width), F32),
         ],
         [VMEM] * 2,
-        [pltpu.VMEM((1024, LANES), F32)],
+        [pltpu.VMEM((8 * QUARTER, LANES), F32)],
         (own, other),
         1_000_000,
         1_000_000,

time: 71.5 us -> 68.8 us (0.962); the launches traced: 70.4 us -> 68.7 us
  starting transfers between devices: 41.6 us -> 38.9 us
  waiting for transfers between devices: 12.1 us -> 13.5 us
    ppermute x8, starting transfers between devices: 20.3 us -> 18.4 us  [swapped(): lax.ppermute(message, AXES, [(s, swap(s) % count) for s in range(count)])]
    ppermute x12, waiting for transfers between devices: 11.6 us -> 13.5 us  [swapped_with(): lax.ppermute(value, axis, [(s, partner(s)) for s in range(lax.axis_size(a...]
    ppermute x12, starting transfers between devices: 21.3 us -> 20.5 us  [swapped_with(): lax.ppermute(value, axis, [(s, partner(s)) for s in range(lax.axis_size(a...]
  transfers between devices with their start and end apart: 20 -> 20, of which waited for: 10 -> 10; matrix products, arithmetic and copies ran while one was open for 0% -> 0% of each run, Pallas kernels for 5% -> 6%
where the time goes in v3:
time: 68.8 us; the launch traced here: 68.7 us
  starting transfers between devices  38.9 us (57%)
  Pallas kernels  14.6 us (21%)
  waiting for transfers between devices  13.5 us (20%)
  between operations  1.6 us (2%)
    ppermute x12, starting transfers between devices, swapped_with(): lax.ppermute(value, axis, [(s, partner(s)) for s in range(lax.axis_size(a...  20.5 us
    ppermute x8, starting transfers between devices, swapped(): lax.ppermute(message, AXES, [(s, swap(s) % count) for s in range(count)])  18.4 us
    pallas_call x7, Pallas kernels, call(): pl.pallas_call(kernel, out_shape=[jax.ShapeDtypeStruct(shape, dtype) for...  14.6 us
    ppermute x12, waiting for transfers between devices, swapped_with(): lax.ppermute(value, axis, [(s, partner(s)) for s in range(lax.axis_size(a...  13.5 us
  transfers between devices with their start and end apart: 20, of which 10 were waited for; matrix products, arithmetic and copies ran while one was open for 0% of the time, Pallas kernels for 6%

profile of v3, /device:TPU:1, one launch (start us, length us, event | category | flops | bytes accessed | tf_op | source)
XLA Modules:
  0.0 68.7 jit_solution(11325645300577639891)
XLA Ops:
  0.6 0.0 copy-start.2
  0.7 0.0 copy-start.3
  0.7 0.0 copy-start.5
  0.7 0.0 copy-start.7
  0.7 0.0 copy-start.8
  0.7 0.0 copy-start.9
  0.7 0.0 copy-start.10
  0.7 0.0 copy-start.11
  0.7 0.0 copy-start.12
  0.7 5.3 %shard_map.231 = (f32[1024,128]{1,0:T(8,128)S(1)}, f32[128,128]{1,0:T(8,128)S(1)}, f32[128,128]{1,0:T(8,128)S(1)}, f32[128,128]{1,0:T(8,128)S(1)}, f32[128,128]{...) custom-call(s32[1,4]{1,0:T(1,128)} %counts_ref.1, ...), custom_call_target="tpu_custom_call" | custom-call | flops 2000000000 | bytes 4000000 | tf_op jit(solution)/shard_map/pallas_call | solution.py:363
  6.1 2.8 %collective-permute-start = (f32[128,128]{1,0:T(8,128)S(1)}, f32[128,128]{1,0:T(8,128)S(1)}, u32[]{:S(2)}, u32[]{:S(2)}) collective-permute-start(f32[128,128]{1,0:T(8,128)S(1)} %get-tuple-element.63), channel_id=1, source_target_pairs={{0,252},{4,8},{8,4},{12,16},{16,12},{20,24},{24,20},{28,32},{32,28... | collective-permute-start | bytes 196616 | tf_op jit(solution)/shard_map/ppermute | solution.py:395
  8.8 3.0 %collective-permute-start.1 = (f32[128,128]{1,0:T(8,128)S(1)}, f32[128,128]{1,0:T(8,128)S(1)}, u32[]{:S(2)}, u32[]{:S(2)}) collective-permute-start(f32[128,128]{1,0:T(8,128)S(1)} %get-tuple-element.64), channel_id=1, source_target_pairs={{0,64},{4,68},{8,72},{12,76},{16,80},{20,84},{24,88},{28,92},{32,9... | collective-permute-start | bytes 196616 | tf_op jit(solution)/shard_map/ppermute | solution.py:395
  11.8 4.2 %collective-permute-start.2 = (f32[128,128]{1,0:T(8,128)S(1)}, f32[128,128]{1,0:T(8,128)S(1)}, u32[]{:S(2)}, u32[]{:S(2)}) collective-permute-start(f32[128,128]{1,0:T(8,128)S(1)} %get-tuple-element.65), channel_id=1, source_target_pairs={{0,192},{4,196},{8,200},{12,204},{16,208},{20,212},{24,216},{28,22... | collective-permute-start | bytes 196616 | tf_op jit(solution)/shard_map/ppermute | solution.py:395
  16.0 1.4 %collective-permute-start.3 = (f32[128,128]{1,0:T(8,128)S(1)}, f32[128,128]{1,0:T(8,128)S(1)}, u32[]{:S(2)}, u32[]{:S(2)}) collective-permute-start(f32[128,128]{1,0:T(8,128)S(1)} %get-tuple-element.66), channel_id=1, source_target_pairs={{0,4},{4,0},{8,12},{12,8},{16,20},{20,16},{24,28},{28,24},{32,36},... | collective-permute-start | bytes 196616 | tf_op jit(solution)/shard_map/ppermute | solution.py:395
  18.0 0.0 copy-done.2
  18.1 0.0 copy-done.3
  18.1 0.0 copy-done.5
  18.1 1.1 %shard_map.232 = (bf16[512,1408]{1,0:T(8,128)(2,1)S(1)}, bf16[1024,512]{1,0:T(8,128)(2,1)S(1)}, f32[1024,128]{1,0:T(8,128)S(1)}, f32[1024,128]{1,0:T(8,128)S(1)}...) custom-call(s32[1,4]{1,0:T(1,128)S(1)} %copy-done.11, s32[1]{0:T(128)S(6)} %copy.26.live_ref, ...), custom_call_target="tpu_custom_call" | custom-call | flops 1000000000 | bytes 4000000 | tf_op jit(solution)/shard_map/pallas_call | solution.py:363
  19.3 0.0 collective-permute-done.in0
  19.3 0.0 collective-permute-done.1.in1
  19.3 0.0 collective-permute-done.2.in2
  19.3 0.0 collective-permute-done.3.in3
  19.3 0.0 copy-start
  19.3 0.0 copy-start.1
  19.3 0.0 copy-start.4
  19.4 1.4 %shard_map.233 = (f32[1024,128]{1,0:T(8,128)S(1)}, f32[128,128]{1,0:T(8,128)S(1)}, f32[128,128]{1,0:T(8,128)S(1)}, f32[128,128]{1,0:T(8,128)S(1)}, f32[128,128]{...) custom-call(f32[1024,128]{1,0:T(8,128)S(1)} %get-tuple-element.62.agg_, ...), custom_call_target="tpu_custom_call" | custom-call | flops 600000000 | bytes 4000000 | tf_op jit(solution)/shard_map/pallas_call | solution.py:363
  20.8 0.8 %collective-permute-start.4 = (f32[128,128]{1,0:T(8,128)S(1)}, f32[128,128]{1,0:T(8,128)S(1)}, u32[]{:S(2)}, u32[]{:S(2)}) collective-permute-start(f32[128,128]{1,0:T(8,128)S(1)} %get-tuple-element.73), channel_id=1, source_target_pairs={{0,252},{4,8},{8,4},{12,16},{16,12},{20,24},{24,20},{28,32},{32,28... | collective-permute-start | bytes 196616 | tf_op jit(solution)/shard_map/ppermute | solution.py:395
  21.6 1.5 %collective-permute-start.5 = (f32[128,128]{1,0:T(8,128)S(1)}, f32[128,128]{1,0:T(8,128)S(1)}, u32[]{:S(2)}, u32[]{:S(2)}) collective-permute-start(f32[128,128]{1,0:T(8,128)S(1)} %get-tuple-element.74), channel_id=1, source_target_pairs={{0,64},{4,68},{8,72},{12,76},{16,80},{20,84},{24,88},{28,92},{32,9... | collective-permute-start | bytes 196616 | tf_op jit(solution)/shard_map/ppermute | solution.py:395
  23.0 3.0 %collective-permute-start.6 = (f32[128,128]{1,0:T(8,128)S(1)}, f32[128,128]{1,0:T(8,128)S(1)}, u32[]{:S(2)}, u32[]{:S(2)}) collective-permute-start(f32[128,128]{1,0:T(8,128)S(1)} %get-tuple-element.75), channel_id=1, source_target_pairs={{0,192},{4,196},{8,200},{12,204},{16,208},{20,212},{24,216},{28,22... | collective-permute-start | bytes 196616 | tf_op jit(solution)/shard_map/ppermute | solution.py:395
  26.0 1.8 %collective-permute-start.7 = (f32[128,128]{1,0:T(8,128)S(1)}, f32[128,128]{1,0:T(8,128)S(1)}, u32[]{:S(2)}, u32[]{:S(2)}) collective-permute-start(f32[128,128]{1,0:T(8,128)S(1)} %get-tuple-element.76), channel_id=1, source_target_pairs={{0,4},{4,0},{8,12},{12,8},{16,20},{20,16},{24,28},{28,24},{32,36},... | collective-permute-start | bytes 196616 | tf_op jit(solution)/shard_map/ppermute | solution.py:395
  27.8 0.0 copy-done.1
  27.8 1.2 %shard_map.234 = (f32[1024,128]{1,0:T(8,128)S(1)}, f32[448,128]{1,0:T(8,128)S(1)}, bf16[1344,256]{1,0:T(8,128)(2,1)S(1)}, bf16[256,1408]{1,0:T(8,128)(2,1)S(1)},...) custom-call(s32[1]{0:T(128)S(6)} %copy.26.live_ref, ...), custom_call_target="tpu_custom_call" | custom-call | flops 1000000000 | bytes 4000000 | tf_op jit(solution)/shard_map/pallas_call | solution.py:363
  29.1 0.0 collective-permute-done.4.in0
  29.1 0.0 collective-permute-done.5.in1
  29.1 0.0 collective-permute-done.6.in2
  29.1 0.0 collective-permute-done.7.in3
  29.1 3.1 %shard_map.235 = (f32[1344,256]{1,0:T(8,128)S(1)}, bf16[1408,256]{1,0:T(8,128)(2,1)S(1)}, f32[1024,256]{1,0:T(8,128)S(1)}, f32[480,128]{1,0:T(8,128)S(1)}, f32[480,128]{1,0:T(8,128)S(1)}) custom-call(f32[1024,128]{1,0:T(8,128)S(1)} %get-tuple-element.72.cback_ref, f32[128,128]{1,0:T(8,128)S(1)} %collective-permute-done.4.in0, ...), custom_call_target="tpu_custom_call" | custom-call | flops 2000000000 | bytes 6000000 | tf_op jit(solution)/shard_map/pallas_call | solution.py:363
  32.2 0.0 copy-start.6
  32.2 3.6 %collective-permute-start.8 = (f32[480,128]{1,0:T(8,128)S(1)}, f32[480,128]{1,0:T(8,128)S(1)}, u32[]{:S(2)}, u32[]{:S(2)}) collective-permute-start(f32[480,128]{1,0:T(8,128)S(1)} %get-tuple-element.94), channel_id=1, source_target_pairs={{0,4},{4,0},{1,5},{5,1},{2,6},{6,2},{3,7},{7,3},{8,12},{12,8},{9,1... | collective-permute-start | bytes 737288 | tf_op jit(solution)/shard_map/ppermute | solution.py:402
  35.9 1.1 %collective-permute-done.8 = f32[480,128]{1,0:T(8,128)S(1)} collective-permute-done((f32[480,128]{1,0:T(8,128)S(1)}, f32[480,128]{1,0:T(8,128)S(1)}, u32[]{:S(2)}, u32[]{:S(2)}) %collective-permute-start.8) | collective-permute-done | bytes 245792 | tf_op jit(solution)/shard_map/ppermute | solution.py:402
  37.0 1.2 %collective-permute-start.11 = (f32[120,128]{1,0:T(8,128)S(1)}, f32[120,128]{1,0:T(8,128)S(1)}, u32[]{:S(2)}, u32[]{:S(2)}) collective-permute-start(f32[120,128]{1,0:T(8,128)S(1)} %get-tuple-element.114), channel_id=1, source_target_pairs={{0,24},{8,16},{16,8},{24,0},{1,25},{9,17},{17,9},{25,1},{2,26},{10... | collective-permute-start | bytes 184328 | tf_op jit(solution)/shard_map/ppermute | solution.py:402
  38.2 0.0 collective-permute-start.10
  38.2 2.2 %collective-permute-start.9 = (f32[120,128]{1,0:T(8,128)S(1)}, f32[120,128]{1,0:T(8,128)S(1)}, u32[]{:S(2)}, u32[]{:S(2)}) collective-permute-start(f32[120,128]{1,0:T(8,128)S(1)} %get-tuple-element.116), channel_id=1, source_target_pairs={{0,8},{8,0},{16,24},{24,16},{1,9},{9,1},{17,25},{25,17},{2,10},{10... | collective-permute-start | bytes 184328 | tf_op jit(solution)/shard_map/ppermute | solution.py:402
  40.4 1.0 %collective-permute-done.11 = f32[120,128]{1,0:T(8,128)S(1)} collective-permute-done((f32[120,128]{1,0:T(8,128)S(1)}, f32[120,128]{1,0:T(8,128)S(1)}, u32[]{:S(2)}, u32[]{:S(2)}) %collective-permute-start.11) | collective-permute-done | bytes 61472 | tf_op jit(solution)/shard_map/ppermute | solution.py:402
  41.4 1.5 %collective-permute-done.10 = f32[120,128]{1,0:T(8,128)S(1)} collective-permute-done((f32[120,128]{1,0:T(8,128)S(1)}, f32[120,128]{1,0:T(8,128)S(1)}, u32[]{:S(2)}, u32[]{:S(2)}) %collective-permute-start.10) | collective-permute-done | bytes 61472 | tf_op jit(solution)/shard_map/ppermute | solution.py:402
  42.9 0.2 collective-permute-done.9
  43.1 2.1 %collective-permute-start.14 = (f32[120,128]{1,0:T(8,128)S(1)}, f32[120,128]{1,0:T(8,128)S(1)}, u32[]{:S(2)}, u32[]{:S(2)}) collective-permute-start(f32[120,128]{1,0:T(8,128)S(1)} %fusion), channel_id=1, source_target_pairs={{0,96},{32,64},{64,32},{96,0},{128,224},{160,192},{192,160},{224,1... | collective-permute-start | bytes 184328 | tf_op jit(solution)/shard_map/ppermute | solution.py:402
  45.3 0.7 collective-permute-start.13
  45.9 0.9 %collective-permute-start.12 = (f32[120,128]{1,0:T(8,128)S(1)}, f32[120,128]{1,0:T(8,128)S(1)}, u32[]{:S(2)}, u32[]{:S(2)}) collective-permute-start(f32[120,128]{1,0:T(8,128)S(1)} %fusion), channel_id=1, source_target_pairs={{0,32},{32,0},{64,96},{96,64},{128,160},{160,128},{192,224},{224,1... | collective-permute-start | bytes 184328 | tf_op jit(solution)/shard_map/ppermute | solution.py:402
  46.8 1.4 %collective-permute-done.14 = f32[120,128]{1,0:T(8,128)S(1)} collective-permute-done((f32[120,128]{1,0:T(8,128)S(1)}, f32[120,128]{1,0:T(8,128)S(1)}, u32[]{:S(2)}, u32[]{:S(2)}) %collective-permute-start.14) | collective-permute-done | bytes 61472 | tf_op jit(solution)/shard_map/ppermute | solution.py:402
  48.2 2.1 %collective-permute-done.13 = f32[120,128]{1,0:T(8,128)S(1)} collective-permute-done((f32[120,128]{1,0:T(8,128)S(1)}, f32[120,128]{1,0:T(8,128)S(1)}, u32[]{:S(2)}, u32[]{:S(2)}) %collective-permute-start.13) | collective-permute-done | bytes 61472 | tf_op jit(solution)/shard_map/ppermute | solution.py:402
  50.3 0.0 collective-permute-done.12
  50.4 2.4 %collective-permute-start.15 = (f32[120,128]{1,0:T(8,128)S(1)}, f32[120,128]{1,0:T(8,128)S(1)}, u32[]{:S(2)}, u32[]{:S(2)}) collective-permute-start(f32[120,128]{1,0:T(8,128)S(1)} %add_add_fusion), channel_id=1, source_target_pairs={{0,224},{32,192},{64,160},{96,128},{128,96},{160,64},{192,32},{224... | collective-permute-start | bytes 184328 | tf_op jit(solution)/shard_map/ppermute | solution.py:402
  52.8 1.6 %shard_map.236 = (bf16[1024,128]{1,0:T(8,128)(2,1)}, bf16[2688,128]{1,0:T(8,128)(2,1)}) custom-call(f32[1344,256]{1,0:T(8,128)S(1)} %get-tuple-element.97.cot_ref, bf16[1408,256]{1,0:T(8,128)(2,1)S(1)} %get-tuple-element.98.eback_ref, f32[1024,256]{1,0:T(8,128)S(1)} %get-tuple-element.99.sums_ref, f32[1024,128]{1,0:T(8,128)S(1)} %get-tuple-element.100.part_ref, ...), custom_call_target="tpu_custom_call" | custom-call | flops 2000000000 | bytes 6000000 | tf_op jit(solution)/shard_map/pallas_call | solution.py:363
  54.4 1.0 %collective-permute-done.15 = f32[120,128]{1,0:T(8,128)S(1)} collective-permute-done((f32[120,128]{1,0:T(8,128)S(1)}, f32[120,128]{1,0:T(8,128)S(1)}, u32[]{:S(2)}, u32[]{:S(2)}) %collective-permute-start.15) | collective-permute-done | bytes 61472 | tf_op jit(solution)/shard_map/ppermute | solution.py:402
  55.4 2.7 %collective-permute-start.18 = (f32[120,128]{1,0:T(8,128)S(1)}, f32[120,128]{1,0:T(8,128)S(1)}, u32[]{:S(2)}, u32[]{:S(2)}) collective-permute-start(f32[120,128]{1,0:T(8,128)S(1)} %add.31), channel_id=1, source_target_pairs={{0,24},{8,16},{16,8},{24,0},{1,25},{9,17},{17,9},{25,1},{2,26},{10... | collective-permute-start | bytes 184328 | tf_op jit(solution)/shard_map/ppermute | solution.py:402
  58.1 0.3 collective-permute-start.17
  58.4 0.4 collective-permute-start.16
  58.8 1.0 %collective-permute-done.18 = f32[120,128]{1,0:T(8,128)S(1)} collective-permute-done((f32[120,128]{1,0:T(8,128)S(1)}, f32[120,128]{1,0:T(8,128)S(1)}, u32[]{:S(2)}, u32[]{:S(2)}) %collective-permute-start.18) | collective-permute-done | bytes 61472 | tf_op jit(solution)/shard_map/ppermute | solution.py:402
  59.8 2.9 %collective-permute-done.17 = f32[120,128]{1,0:T(8,128)S(1)} collective-permute-done((f32[120,128]{1,0:T(8,128)S(1)}, f32[120,128]{1,0:T(8,128)S(1)}, u32[]{:S(2)}, u32[]{:S(2)}) %collective-permute-start.17) | collective-permute-done | bytes 61472 | tf_op jit(solution)/shard_map/ppermute | solution.py:402
  62.7 0.0 collective-permute-done.16
  62.7 4.0 %collective-permute-start.19 = (f32[480,128]{1,0:T(8,128)S(1)}, f32[480,128]{1,0:T(8,128)S(1)}, u32[]{:S(2)}, u32[]{:S(2)}) collective-permute-start(f32[480,128]{1,0:T(8,128)S(1)} %pad_maximum_fusion.refs_0_), channel_id=1, source_target_pairs={{0,4},{4,0},{1,5},{5,1},{2,6},{6,2},{3,7},{7,3},{8,12},{12,8},{9,1... | collective-permute-start | bytes 737288 | tf_op jit(solution)/shard_map/ppermute | solution.py:402
  66.7 1.1 %collective-permute-done.19.refs_1_ = f32[480,128]{1,0:T(8,128)S(1)} collective-permute-done((f32[480,128]{1,0:T(8,128)S(1)}, f32[480,128]{1,0:T(8,128)S(1)}, u32[]{:S(2)}, u32[]{:S(2)}) %collective-permute-start.19) | collective-permute-done | bytes 245792 | tf_op jit(solution)/shard_map/ppermute | solution.py:402
  67.9 0.8 %shard_map.237 = (f32[384,128]{1,0:T(8,128)}, f32[1,128]{1,0:T(1,128)}, f32[128,128]{1,0:T(8,128)}, f32[1,128]{1,0:T(1,128)}, f32[256,128]{1,0:T(8,128)}, /*inde...) custom-call(f32[480,128]{1,0:T(8,128)S(1)} %pad_maximum_fusion.refs_0_, ...), custom_call_target="tpu_custom_call" | custom-call | flops 1000000 | bytes 1000000 | tf_op jit(solution)/shard_map/pallas_call | solution.py:363
  (15 shorter events, 0.1 us)
Async XLA Ops:
  0.6 17.4 %copy-start.2 = (bf16[256,128]{1,0:T(8,128)(2,1)S(1)}, bf16[256,128]{1,0:T(8,128)(2,1)}, u32[]{:S(2)}) copy-start(bf16[256,128]{1,0:T(8,128)(2,1)} %wn_ref.5) | copy-start | bytes 196612
  0.7 17.4 %copy-start.3 = (bf16[1024,128]{1,0:T(8,128)(2,1)S(1)}, bf16[1024,128]{1,0:T(8,128)(2,1)}, u32[]{:S(2)}) copy-start(bf16[1024,128]{1,0:T(8,128)(2,1)} %nf_ref.3) | copy-start | bytes 786436
  0.7 17.4 %copy-start.5 = (bf16[1024,128]{1,0:T(8,128)(2,1)S(1)}, bf16[1024,128]{1,0:T(8,128)(2,1)}, u32[]{:S(2)}) copy-start(bf16[1024,128]{1,0:T(8,128)(2,1)} %nc_ref.1) | copy-start | bytes 786436
  0.7 17.4 %copy-start.7 = (bf16[128,128]{1,0:T(8,128)(2,1)S(1)}, bf16[128,128]{1,0:T(8,128)(2,1)}, u32[]{:S(2)}) copy-start(bf16[128,128]{1,0:T(8,128)(2,1)} %wo_ref.2) | copy-start | bytes 98308
  0.7 17.4 %copy-start.8 = (s32[2,1344]{1,0:T(2,128)S(1)}, s32[2,1344]{1,0:T(2,128)}, u32[]{:S(2)}) copy-start(s32[2,1344]{1,0:T(2,128)} %ends_ref.1) | copy-start | bytes 32260
  0.7 17.4 %copy-start.9 = (s32[1024]{0:T(1024)S(1)}, s32[1024]{0:T(1024)}, u32[]{:S(2)}) copy-start(s32[1024]{0:T(1024)} %param.31) | copy-start | bytes 12292
  0.7 17.4 %copy-start.10 = (s32[1,4,128]{2,1,0:T(4,128)S(1)}, s32[1,4,128]{2,1,0:T(4,128)}, u32[]{:S(2)}) copy-start(s32[1,4,128]{2,1,0:T(4,128)} %param.29) | copy-start | bytes 6148
  0.7 17.4 %copy-start.11 = (s32[1,4]{1,0:T(1,128)S(1)}, s32[1,4]{1,0:T(1,128)}, u32[]{:S(2)}) copy-start(s32[1,4]{1,0:T(1,128)} %counts_ref.1) | copy-start | bytes 52
  0.7 17.4 %copy-start.12 = (f32[128]{0:T(128)S(1)}, f32[128]{0:T(128)}, u32[]{:S(2)}) copy-start(f32[128]{0:T(128)} %param.25) | copy-start | bytes 1540
  6.1 13.2 %collective-permute-start = (f32[128,128]{1,0:T(8,128)S(1)}, f32[128,128]{1,0:T(8,128)S(1)}, u32[]{:S(2)}, u32[]{:S(2)}) collective-permute-start(f32[128,128]{1,0:T(8,128)S(1)} %get-tuple-element.63), channel_id=1, source_target_pairs={{0,252},{4,8},{8,4},{12,16},{16,12},{20,24},{24,20},{28,32},{32,28... | collective-permute-start | bytes 196616 | tf_op jit(solution)/shard_map/ppermute | solution.py:395
  8.8 10.5 %collective-permute-start.1 = (f32[128,128]{1,0:T(8,128)S(1)}, f32[128,128]{1,0:T(8,128)S(1)}, u32[]{:S(2)}, u32[]{:S(2)}) collective-permute-start(f32[128,128]{1,0:T(8,128)S(1)} %get-tuple-element.64), channel_id=1, source_target_pairs={{0,64},{4,68},{8,72},{12,76},{16,80},{20,84},{24,88},{28,92},{32,9... | collective-permute-start | bytes 196616 | tf_op jit(solution)/shard_map/ppermute | solution.py:395
  11.8 7.5 %collective-permute-start.2 = (f32[128,128]{1,0:T(8,128)S(1)}, f32[128,128]{1,0:T(8,128)S(1)}, u32[]{:S(2)}, u32[]{:S(2)}) collective-permute-start(f32[128,128]{1,0:T(8,128)S(1)} %get-tuple-element.65), channel_id=1, source_target_pairs={{0,192},{4,196},{8,200},{12,204},{16,208},{20,212},{24,216},{28,22... | collective-permute-start | bytes 196616 | tf_op jit(solution)/shard_map/ppermute | solution.py:395
  16.0 3.3 %collective-permute-start.3 = (f32[128,128]{1,0:T(8,128)S(1)}, f32[128,128]{1,0:T(8,128)S(1)}, u32[]{:S(2)}, u32[]{:S(2)}) collective-permute-start(f32[128,128]{1,0:T(8,128)S(1)} %get-tuple-element.66), channel_id=1, source_target_pairs={{0,4},{4,0},{8,12},{12,8},{16,20},{20,16},{24,28},{28,24},{32,36},... | collective-permute-start | bytes 196616 | tf_op jit(solution)/shard_map/ppermute | solution.py:395
  19.3 8.5 %copy-start = (bf16[2688,128]{1,0:T(8,128)(2,1)S(1)}, bf16[2688,128]{1,0:T(8,128)(2,1)}, u32[]{:S(2)}) copy-start(bf16[2688,128]{1,0:T(8,128)(2,1)} %ef_ref.1) | copy-start | bytes 2064388
  19.3 8.5 %copy-start.1 = (bf16[2688,128]{1,0:T(8,128)(2,1)S(1)}, bf16[2688,128]{1,0:T(8,128)(2,1)}, u32[]{:S(2)}) copy-start(bf16[2688,128]{1,0:T(8,128)(2,1)} %ec_ref.1) | copy-start | bytes 2064388
  19.3 8.5 %copy-start.4 = (bf16[128,128]{1,0:T(8,128)(2,1)S(1)}, bf16[128,128]{1,0:T(8,128)(2,1)}, u32[]{:S(2)}) copy-start(bf16[128,128]{1,0:T(8,128)(2,1)} %wo_ref.3) | copy-start | bytes 98308
  20.8 8.3 %collective-permute-start.4 = (f32[128,128]{1,0:T(8,128)S(1)}, f32[128,128]{1,0:T(8,128)S(1)}, u32[]{:S(2)}, u32[]{:S(2)}) collective-permute-start(f32[128,128]{1,0:T(8,128)S(1)} %get-tuple-element.73), channel_id=1, source_target_pairs={{0,252},{4,8},{8,4},{12,16},{16,12},{20,24},{24,20},{28,32},{32,28... | collective-permute-start | bytes 196616 | tf_op jit(solution)/shard_map/ppermute | solution.py:395
  21.6 7.5 %collective-permute-start.5 = (f32[128,128]{1,0:T(8,128)S(1)}, f32[128,128]{1,0:T(8,128)S(1)}, u32[]{:S(2)}, u32[]{:S(2)}) collective-permute-start(f32[128,128]{1,0:T(8,128)S(1)} %get-tuple-element.74), channel_id=1, source_target_pairs={{0,64},{4,68},{8,72},{12,76},{16,80},{20,84},{24,88},{28,92},{32,9... | collective-permute-start | bytes 196616 | tf_op jit(solution)/shard_map/ppermute | solution.py:395
  23.0 6.1 %collective-permute-start.6 = (f32[128,128]{1,0:T(8,128)S(1)}, f32[128,128]{1,0:T(8,128)S(1)}, u32[]{:S(2)}, u32[]{:S(2)}) collective-permute-start(f32[128,128]{1,0:T(8,128)S(1)} %get-tuple-element.75), channel_id=1, source_target_pairs={{0,192},{4,196},{8,200},{12,204},{16,208},{20,212},{24,216},{28,22... | collective-permute-start | bytes 196616 | tf_op jit(solution)/shard_map/ppermute | solution.py:395
  26.0 3.1 %collective-permute-start.7 = (f32[128,128]{1,0:T(8,128)S(1)}, f32[128,128]{1,0:T(8,128)S(1)}, u32[]{:S(2)}, u32[]{:S(2)}) collective-permute-start(f32[128,128]{1,0:T(8,128)S(1)} %get-tuple-element.76), channel_id=1, source_target_pairs={{0,4},{4,0},{8,12},{12,8},{16,20},{20,16},{24,28},{28,24},{32,36},... | collective-permute-start | bytes 196616 | tf_op jit(solution)/shard_map/ppermute | solution.py:395
  32.2 20.6 %copy-start.6 = (bf16[384,128]{1,0:T(8,128)(2,1)S(1)}, bf16[384,128]{1,0:T(8,128)(2,1)}, u32[]{:S(2)}) copy-start(bf16[384,128]{1,0:T(8,128)(2,1)} %wi_ref.1) | copy-start | bytes 294916
  32.2 4.8 %collective-permute-start.8 = (f32[480,128]{1,0:T(8,128)S(1)}, f32[480,128]{1,0:T(8,128)S(1)}, u32[]{:S(2)}, u32[]{:S(2)}) collective-permute-start(f32[480,128]{1,0:T(8,128)S(1)} %get-tuple-element.94), channel_id=1, source_target_pairs={{0,4},{4,0},{1,5},{5,1},{2,6},{6,2},{3,7},{7,3},{8,12},{12,8},{9,1... | collective-permute-start | bytes 737288 | tf_op jit(solution)/shard_map/ppermute | solution.py:402
  37.0 4.4 %collective-permute-start.11 = (f32[120,128]{1,0:T(8,128)S(1)}, f32[120,128]{1,0:T(8,128)S(1)}, u32[]{:S(2)}, u32[]{:S(2)}) collective-permute-start(f32[120,128]{1,0:T(8,128)S(1)} %get-tuple-element.114), channel_id=1, source_target_pairs={{0,24},{8,16},{16,8},{24,0},{1,25},{9,17},{17,9},{25,1},{2,26},{10... | collective-permute-start | bytes 184328 | tf_op jit(solution)/shard_map/ppermute | solution.py:402
  38.2 4.7 %collective-permute-start.10 = (f32[120,128]{1,0:T(8,128)S(1)}, f32[120,128]{1,0:T(8,128)S(1)}, u32[]{:S(2)}, u32[]{:S(2)}) collective-permute-start(f32[120,128]{1,0:T(8,128)S(1)} %get-tuple-element.115), channel_id=1, source_target_pairs={{0,16},{8,24},{16,0},{24,8},{1,17},{9,25},{17,1},{25,9},{2,18},{10... | collective-permute-start | bytes 184328 | tf_op jit(solution)/shard_map/ppermute | solution.py:402
  38.2 4.9 %collective-permute-start.9 = (f32[120,128]{1,0:T(8,128)S(1)}, f32[120,128]{1,0:T(8,128)S(1)}, u32[]{:S(2)}, u32[]{:S(2)}) collective-permute-start(f32[120,128]{1,0:T(8,128)S(1)} %get-tuple-element.116), channel_id=1, source_target_pairs={{0,8},{8,0},{16,24},{24,16},{1,9},{9,1},{17,25},{25,17},{2,10},{10... | collective-permute-start | bytes 184328 | tf_op jit(solution)/shard_map/ppermute | solution.py:402
  43.1 5.0 %collective-permute-start.14 = (f32[120,128]{1,0:T(8,128)S(1)}, f32[120,128]{1,0:T(8,128)S(1)}, u32[]{:S(2)}, u32[]{:S(2)}) collective-permute-start(f32[120,128]{1,0:T(8,128)S(1)} %fusion), channel_id=1, source_target_pairs={{0,96},{32,64},{64,32},{96,0},{128,224},{160,192},{192,160},{224,1... | collective-permute-start | bytes 184328 | tf_op jit(solution)/shard_map/ppermute | solution.py:402
  45.3 5.1 %collective-permute-start.13 = (f32[120,128]{1,0:T(8,128)S(1)}, f32[120,128]{1,0:T(8,128)S(1)}, u32[]{:S(2)}, u32[]{:S(2)}) collective-permute-start(f32[120,128]{1,0:T(8,128)S(1)} %fusion), channel_id=1, source_target_pairs={{0,64},{32,96},{64,0},{96,32},{128,192},{160,224},{192,128},{224,1... | collective-permute-start | bytes 184328 | tf_op jit(solution)/shard_map/ppermute | solution.py:402
  45.9 4.4 %collective-permute-start.12 = (f32[120,128]{1,0:T(8,128)S(1)}, f32[120,128]{1,0:T(8,128)S(1)}, u32[]{:S(2)}, u32[]{:S(2)}) collective-permute-start(f32[120,128]{1,0:T(8,128)S(1)} %fusion), channel_id=1, source_target_pairs={{0,32},{32,0},{64,96},{96,64},{128,160},{160,128},{192,224},{224,1... | collective-permute-start | bytes 184328 | tf_op jit(solution)/shard_map/ppermute | solution.py:402
  50.4 5.0 %collective-permute-start.15 = (f32[120,128]{1,0:T(8,128)S(1)}, f32[120,128]{1,0:T(8,128)S(1)}, u32[]{:S(2)}, u32[]{:S(2)}) collective-permute-start(f32[120,128]{1,0:T(8,128)S(1)} %add_add_fusion), channel_id=1, source_target_pairs={{0,224},{32,192},{64,160},{96,128},{128,96},{160,64},{192,32},{224... | collective-permute-start | bytes 184328 | tf_op jit(solution)/shard_map/ppermute | solution.py:402
  55.4 4.4 %collective-permute-start.18 = (f32[120,128]{1,0:T(8,128)S(1)}, f32[120,128]{1,0:T(8,128)S(1)}, u32[]{:S(2)}, u32[]{:S(2)}) collective-permute-start(f32[120,128]{1,0:T(8,128)S(1)} %add.31), channel_id=1, source_target_pairs={{0,24},{8,16},{16,8},{24,0},{1,25},{9,17},{17,9},{25,1},{2,26},{10... | collective-permute-start | bytes 184328 | tf_op jit(solution)/shard_map/ppermute | solution.py:402
  58.1 4.6 %collective-permute-start.17 = (f32[120,128]{1,0:T(8,128)S(1)}, f32[120,128]{1,0:T(8,128)S(1)}, u32[]{:S(2)}, u32[]{:S(2)}) collective-permute-start(f32[120,128]{1,0:T(8,128)S(1)} %add.31), channel_id=1, source_target_pairs={{0,16},{8,24},{16,0},{24,8},{1,17},{9,25},{17,1},{25,9},{2,18},{10... | collective-permute-start | bytes 184328 | tf_op jit(solution)/shard_map/ppermute | solution.py:402
  58.4 4.3 %collective-permute-start.16 = (f32[120,128]{1,0:T(8,128)S(1)}, f32[120,128]{1,0:T(8,128)S(1)}, u32[]{:S(2)}, u32[]{:S(2)}) collective-permute-start(f32[120,128]{1,0:T(8,128)S(1)} %add.31), channel_id=1, source_target_pairs={{0,8},{8,0},{16,24},{24,16},{1,9},{9,1},{17,25},{25,17},{2,10},{10... | collective-permute-start | bytes 184328 | tf_op jit(solution)/shard_map/ppermute | solution.py:402
  62.7 5.1 %collective-permute-start.19 = (f32[480,128]{1,0:T(8,128)S(1)}, f32[480,128]{1,0:T(8,128)S(1)}, u32[]{:S(2)}, u32[]{:S(2)}) collective-permute-start(f32[480,128]{1,0:T(8,128)S(1)} %pad_maximum_fusion.refs_0_), channel_id=1, source_target_pairs={{0,4},{4,0},{1,5},{5,1},{2,6},{6,2},{3,7},{7,3},{8,12},{12,8},{9,1... | collective-permute-start | bytes 737288 | tf_op jit(solution)/shard_map/ppermute | solution.py:402

commit v4 on v3

--- a/solution.py
+++ b/solution.py
@@ -210,7 +210,7 @@
 
 def prepare_kernel(
     counts_ref, live_ref, ends_ref, lists_ref, mult_ref, nf_ref, nc_ref, wn_ref, bn_ref, wo_ref,
-    spread_ref, arrive_ref, linear_ref, hback_ref, cot_ref, copies_ref,
+    spread_ref, arrive_ref, linear_ref, hback_ref, cot_ref, shares_ref,
     ends_sc,
 ):
     nodes = nf_ref.shape[0]
@@ -227,21 +227,21 @@
     linear_ref[...] = dot(nf_ref[...], wn_ref[0:128, :]) + bn_ref[...]
     hback_ref[...] = dot_t(cot, wo_ref[...])
     for b in range(nodes // LANES):
-        copies_ref[b * LANES : (b + 1) * LANES, :] = as_column(mult_ref[b : b + 1, :].astype(F32))
+        shares_ref[b * LANES : (b + 1) * LANES, :] = 1.0 / as_column(mult_ref[b : b + 1, :].astype(F32))
 
 
 def node_kernel(
-    agg_ref, in0, in1, in2, in3, arrive_ref, pick_ref, linear_ref, hback_ref, copies_ref, wn_ref,
+    agg_ref, in0, in1, in2, in3, arrive_ref, pick_ref, linear_ref, hback_ref, shares_ref, wn_ref,
     cback_ref, out0, out1, out2, out3, cons_ref, hid_ref, back_ref,
 ):
-    copies = copies_ref[...]
+    shares = shares_ref[...]
     total = agg_ref[...] + incoming(arrive_ref, (in0, in1, in2, in3))
-    consistent = (total / copies).astype(BF16)
+    consistent = (total * shares).astype(BF16)
     linear = linear_ref[...] + dot(consistent, wn_ref[128:256, :])
     squashed = jax.nn.sigmoid(linear)
     slope = squashed * (1.0 + linear * (1.0 - squashed))
     back = (hback_ref[...] * slope).astype(BF16)
-    consistent_back = dot_t(back, wn_ref[128:256, :]) / copies
+    consistent_back = dot_t(back, wn_ref[128:256, :]) * shares
     cback_ref[...] = consistent_back
     outgoing(pick_ref, consistent_back, (out0, out1, out2, out3))
     cons_ref[...] = consistent
@@ -405,23 +405,26 @@
 def summed_along_y(mine, theirs):
     half = mine + swapped_with(theirs, "c", lambda s: 1 - s)
     blocks = [half[k * QUARTER : (k + 1) * QUARTER] for k in range(4)]
+    one = swapped_with(blocks[1], "y", lambda s: s ^ 1)
+    three = swapped_with(blocks[3], "y", lambda s: s ^ 3)
     two = swapped_with(blocks[2], "y", lambda s: s ^ 2)
-    three = swapped_with(blocks[3], "y", lambda s: s ^ 3)
-    one = swapped_with(blocks[1], "y", lambda s: s ^ 1)
+    one, three, two = lax.optimization_barrier((one, three, two))
     return (blocks[0] + one) + (two + three)
 
 
 def summed_along_z(total):
+    one = swapped_with(total, "z", lambda s: s ^ 1)
     three = swapped_with(total, "z", lambda s: s ^ 3)
     two = swapped_with(total, "z", lambda s: s ^ 2)
-    one = swapped_with(total, "z", lambda s: s ^ 1)
+    one, three, two = lax.optimization_barrier((one, three, two))
     return (total + one) + (two + three)
 
 
 def shared(total):
+    one = swapped_with(total, "y", lambda s: s ^ 1)
+    three = swapped_with(total, "y", lambda s: s ^ 3)
     two = swapped_with(total, "y", lambda s: s ^ 2)
-    three = swapped_with(total, "y", lambda s: s ^ 3)
-    one = swapped_with(total, "y", lambda s: s ^ 1)
+    one, three, two = lax.optimization_barrier((one, three, two))
     own = jnp.concatenate([total, one, two, three], axis=0)
     return own, swapped_with(own, "c", lambda s: 1 - s)
 
@@ -496,7 +499,7 @@
         4_000_000,
     )
     arrived = exchanged(messages)
-    spread_source, arrive, linear_part, hidden_back, node_cot, copies_wide = call(
+    spread_source, arrive, linear_part, hidden_back, node_cot, node_shares = call(
         prepare_kernel,
         [
             ((NPE, rows_height), BF16),
@@ -535,7 +538,7 @@
             pick,
             linear_part,
             hidden_back,
-            copies_wide,
+            node_shares,
             node_in_weight,
         ),
         600_000_000,

time: 68.8 us -> 68.4 us (level)
  starting transfers between devices: 38.9 us -> 37.2 us
  waiting for transfers between devices: 13.5 us -> 14.7 us
    ppermute x12, starting transfers between devices: 20.5 us -> 18.8 us  [swapped_with(): lax.ppermute(value, axis, [(s, partner(s)) for s in range(lax.axis_size(a...]
    ppermute x12, waiting for transfers between devices: 13.5 us -> 14.7 us  [swapped_with(): lax.ppermute(value, axis, [(s, partner(s)) for s in range(lax.axis_size(a...]
  transfers between devices with their start and end apart: 20 -> 20, of which waited for: 10 -> 9; matrix products, arithmetic and copies ran while one was open for 0% -> 0% of each run, Pallas kernels for 6% -> 6%
where the time goes in v4:
time: 68.4 us; the launch traced here: 68.3 us
  starting transfers between devices  37.2 us (54%)
  waiting for transfers between devices  14.7 us (21%)
  Pallas kernels  14.6 us (21%)
  between operations  1.61 us (2%)
    ppermute x12, starting transfers between devices, swapped_with(): lax.ppermute(value, axis, [(s, partner(s)) for s in range(lax.axis_size(a...  18.8 us
    ppermute x8, starting transfers between devices, swapped(): lax.ppermute(message, AXES, [(s, swap(s) % count) for s in range(count)])  18.4 us
    ppermute x12, waiting for transfers between devices, swapped_with(): lax.ppermute(value, axis, [(s, partner(s)) for s in range(lax.axis_size(a...  14.7 us
    pallas_call x7, Pallas kernels, call(): pl.pallas_call(kernel, out_shape=[jax.ShapeDtypeStruct(shape, dtype) for...  14.6 us
  transfers between devices with their start and end apart: 20, of which 9 were waited for; matrix products, arithmetic and copies ran while one was open for 0% of the time, Pallas kernels for 6%

profile of v4, /device:TPU:1, one launch (start us, length us, event | category | flops | bytes accessed | tf_op | source)
XLA Modules:
  0.0 68.3 jit_solution(15283586844205849905)
XLA Ops:
  0.6 0.0 copy-start.2
  0.7 0.0 copy-start.3
  0.7 0.0 copy-start.5
  0.7 0.0 copy-start.7
  0.7 0.0 copy-start.8
  0.7 0.0 copy-start.9
  0.7 0.0 copy-start.10
  0.7 0.0 copy-start.11
  0.7 0.0 copy-start.12
  0.7 5.3 %shard_map.231 = (f32[1024,128]{1,0:T(8,128)S(1)}, f32[128,128]{1,0:T(8,128)S(1)}, f32[128,128]{1,0:T(8,128)S(1)}, f32[128,128]{1,0:T(8,128)S(1)}, f32[128,128]{...) custom-call(s32[1,4]{1,0:T(1,128)} %counts_ref.1, ...), custom_call_target="tpu_custom_call" | custom-call | flops 2000000000 | bytes 4000000 | tf_op jit(solution)/shard_map/pallas_call | solution.py:363
  6.1 2.8 %collective-permute-start = (f32[128,128]{1,0:T(8,128)S(1)}, f32[128,128]{1,0:T(8,128)S(1)}, u32[]{:S(2)}, u32[]{:S(2)}) collective-permute-start(f32[128,128]{1,0:T(8,128)S(1)} %get-tuple-element.72), channel_id=1, source_target_pairs={{0,252},{4,8},{8,4},{12,16},{16,12},{20,24},{24,20},{28,32},{32,28... | collective-permute-start | bytes 196616 | tf_op jit(solution)/shard_map/ppermute | solution.py:395
  8.8 3.0 %collective-permute-start.1 = (f32[128,128]{1,0:T(8,128)S(1)}, f32[128,128]{1,0:T(8,128)S(1)}, u32[]{:S(2)}, u32[]{:S(2)}) collective-permute-start(f32[128,128]{1,0:T(8,128)S(1)} %get-tuple-element.73), channel_id=1, source_target_pairs={{0,64},{4,68},{8,72},{12,76},{16,80},{20,84},{24,88},{28,92},{32,9... | collective-permute-start | bytes 196616 | tf_op jit(solution)/shard_map/ppermute | solution.py:395
  11.8 4.2 %collective-permute-start.2 = (f32[128,128]{1,0:T(8,128)S(1)}, f32[128,128]{1,0:T(8,128)S(1)}, u32[]{:S(2)}, u32[]{:S(2)}) collective-permute-start(f32[128,128]{1,0:T(8,128)S(1)} %get-tuple-element.74), channel_id=1, source_target_pairs={{0,192},{4,196},{8,200},{12,204},{16,208},{20,212},{24,216},{28,22... | collective-permute-start | bytes 196616 | tf_op jit(solution)/shard_map/ppermute | solution.py:395
  16.0 1.4 %collective-permute-start.3 = (f32[128,128]{1,0:T(8,128)S(1)}, f32[128,128]{1,0:T(8,128)S(1)}, u32[]{:S(2)}, u32[]{:S(2)}) collective-permute-start(f32[128,128]{1,0:T(8,128)S(1)} %get-tuple-element.75), channel_id=1, source_target_pairs={{0,4},{4,0},{8,12},{12,8},{16,20},{20,16},{24,28},{28,24},{32,36},... | collective-permute-start | bytes 196616 | tf_op jit(solution)/shard_map/ppermute | solution.py:395
  18.0 0.0 copy-done.2
  18.1 0.0 copy-done.3
  18.1 1.2 %shard_map.232 = (bf16[512,1408]{1,0:T(8,128)(2,1)S(1)}, bf16[1024,512]{1,0:T(8,128)(2,1)S(1)}, f32[1024,128]{1,0:T(8,128)S(1)}, f32[1024,128]{1,0:T(8,128)S(1)}...) custom-call(s32[1,4]{1,0:T(1,128)S(1)} %copy-done.11, s32[1]{0:T(128)S(6)} %copy.26.live_ref, ...), custom_call_target="tpu_custom_call" | custom-call | flops 1000000000 | bytes 4000000 | tf_op jit(solution)/shard_map/pallas_call | solution.py:363
  19.3 0.0 collective-permute-done.in0
  19.3 0.0 collective-permute-done.1.in1
  19.3 0.0 collective-permute-done.2.in2
  19.3 0.0 collective-permute-done.3.in3
  19.3 0.0 copy-start
  19.3 0.0 copy-start.1
  19.4 0.0 copy-start.4
  19.4 1.4 %shard_map.233 = (f32[1024,128]{1,0:T(8,128)S(1)}, f32[128,128]{1,0:T(8,128)S(1)}, f32[128,128]{1,0:T(8,128)S(1)}, f32[128,128]{1,0:T(8,128)S(1)}, f32[128,128]{...) custom-call(f32[1024,128]{1,0:T(8,128)S(1)} %get-tuple-element.71.agg_, ...), custom_call_target="tpu_custom_call" | custom-call | flops 600000000 | bytes 4000000 | tf_op jit(solution)/shard_map/pallas_call | solution.py:363
  20.8 0.8 %collective-permute-start.4 = (f32[128,128]{1,0:T(8,128)S(1)}, f32[128,128]{1,0:T(8,128)S(1)}, u32[]{:S(2)}, u32[]{:S(2)}) collective-permute-start(f32[128,128]{1,0:T(8,128)S(1)} %get-tuple-element.82), channel_id=1, source_target_pairs={{0,252},{4,8},{8,4},{12,16},{16,12},{20,24},{24,20},{28,32},{32,28... | collective-permute-start | bytes 196616 | tf_op jit(solution)/shard_map/ppermute | solution.py:395
  21.6 1.5 %collective-permute-start.5 = (f32[128,128]{1,0:T(8,128)S(1)}, f32[128,128]{1,0:T(8,128)S(1)}, u32[]{:S(2)}, u32[]{:S(2)}) collective-permute-start(f32[128,128]{1,0:T(8,128)S(1)} %get-tuple-element.83), channel_id=1, source_target_pairs={{0,64},{4,68},{8,72},{12,76},{16,80},{20,84},{24,88},{28,92},{32,9... | collective-permute-start | bytes 196616 | tf_op jit(solution)/shard_map/ppermute | solution.py:395
  23.0 3.0 %collective-permute-start.6 = (f32[128,128]{1,0:T(8,128)S(1)}, f32[128,128]{1,0:T(8,128)S(1)}, u32[]{:S(2)}, u32[]{:S(2)}) collective-permute-start(f32[128,128]{1,0:T(8,128)S(1)} %get-tuple-element.84), channel_id=1, source_target_pairs={{0,192},{4,196},{8,200},{12,204},{16,208},{20,212},{24,216},{28,22... | collective-permute-start | bytes 196616 | tf_op jit(solution)/shard_map/ppermute | solution.py:395
  26.0 1.8 %collective-permute-start.7 = (f32[128,128]{1,0:T(8,128)S(1)}, f32[128,128]{1,0:T(8,128)S(1)}, u32[]{:S(2)}, u32[]{:S(2)}) collective-permute-start(f32[128,128]{1,0:T(8,128)S(1)} %get-tuple-element.85), channel_id=1, source_target_pairs={{0,4},{4,0},{8,12},{12,8},{16,20},{20,16},{24,28},{28,24},{32,36},... | collective-permute-start | bytes 196616 | tf_op jit(solution)/shard_map/ppermute | solution.py:395
  27.8 0.0 copy-done.1
  27.8 1.2 %shard_map.234 = (f32[1024,128]{1,0:T(8,128)S(1)}, f32[448,128]{1,0:T(8,128)S(1)}, bf16[1344,256]{1,0:T(8,128)(2,1)S(1)}, bf16[256,1408]{1,0:T(8,128)(2,1)S(1)},...) custom-call(s32[1]{0:T(128)S(6)} %copy.26.live_ref, ...), custom_call_target="tpu_custom_call" | custom-call | flops 1000000000 | bytes 4000000 | tf_op jit(solution)/shard_map/pallas_call | solution.py:363
  29.1 0.0 collective-permute-done.4.in0
  29.1 0.0 collective-permute-done.5.in1
  29.1 0.0 collective-permute-done.6.in2
  29.1 0.0 collective-permute-done.7.in3
  29.1 3.1 %shard_map.235 = (f32[1344,256]{1,0:T(8,128)S(1)}, bf16[1408,256]{1,0:T(8,128)(2,1)S(1)}, f32[1024,256]{1,0:T(8,128)S(1)}, f32[480,128]{1,0:T(8,128)S(1)}, f32[480,128]{1,0:T(8,128)S(1)}) custom-call(f32[1024,128]{1,0:T(8,128)S(1)} %get-tuple-element.81.cback_ref, f32[128,128]{1,0:T(8,128)S(1)} %collective-permute-done.4.in0, ...), custom_call_target="tpu_custom_call" | custom-call | flops 2000000000 | bytes 6000000 | tf_op jit(solution)/shard_map/pallas_call | solution.py:363
  32.2 0.0 copy-start.6
  32.2 3.6 %collective-permute-start.8 = (f32[480,128]{1,0:T(8,128)S(1)}, f32[480,128]{1,0:T(8,128)S(1)}, u32[]{:S(2)}, u32[]{:S(2)}) collective-permute-start(f32[480,128]{1,0:T(8,128)S(1)} %get-tuple-element.103), channel_id=1, source_target_pairs={{0,4},{4,0},{1,5},{5,1},{2,6},{6,2},{3,7},{7,3},{8,12},{12,8},{9,1... | collective-permute-start | bytes 737288 | tf_op jit(solution)/shard_map/ppermute | solution.py:402
  35.9 1.1 %collective-permute-done.8 = f32[480,128]{1,0:T(8,128)S(1)} collective-permute-done((f32[480,128]{1,0:T(8,128)S(1)}, f32[480,128]{1,0:T(8,128)S(1)}, u32[]{:S(2)}, u32[]{:S(2)}) %collective-permute-start.8) | collective-permute-done | bytes 245792 | tf_op jit(solution)/shard_map/ppermute | solution.py:402
  37.0 0.7 %collective-permute-start.11 = (f32[120,128]{1,0:T(8,128)S(1)}, f32[120,128]{1,0:T(8,128)S(1)}, u32[]{:S(2)}, u32[]{:S(2)}) collective-permute-start(f32[120,128]{1,0:T(8,128)S(1)} %get-tuple-element.132), channel_id=1, source_target_pairs={{0,16},{8,24},{16,0},{24,8},{1,17},{9,25},{17,1},{25,9},{2,18},{10... | collective-permute-start | bytes 184328 | tf_op jit(solution)/shard_map/ppermute | solution.py:402
  37.8 1.0 %collective-permute-start.10 = (f32[120,128]{1,0:T(8,128)S(1)}, f32[120,128]{1,0:T(8,128)S(1)}, u32[]{:S(2)}, u32[]{:S(2)}) collective-permute-start(f32[120,128]{1,0:T(8,128)S(1)} %get-tuple-element.133), channel_id=1, source_target_pairs={{0,24},{8,16},{16,8},{24,0},{1,25},{9,17},{17,9},{25,1},{2,26},{10... | collective-permute-start | bytes 184328 | tf_op jit(solution)/shard_map/ppermute | solution.py:402
  38.8 1.0 %collective-permute-start.9 = (f32[120,128]{1,0:T(8,128)S(1)}, f32[120,128]{1,0:T(8,128)S(1)}, u32[]{:S(2)}, u32[]{:S(2)}) collective-permute-start(f32[120,128]{1,0:T(8,128)S(1)} %get-tuple-element.134), channel_id=1, source_target_pairs={{0,8},{8,0},{16,24},{24,16},{1,9},{9,1},{17,25},{25,17},{2,10},{10... | collective-permute-start | bytes 184328 | tf_op jit(solution)/shard_map/ppermute | solution.py:402
  39.8 2.0 %collective-permute-done.11 = f32[120,128]{1,0:T(8,128)S(1)} collective-permute-done((f32[120,128]{1,0:T(8,128)S(1)}, f32[120,128]{1,0:T(8,128)S(1)}, u32[]{:S(2)}, u32[]{:S(2)}) %collective-permute-start.11) | collective-permute-done | bytes 61472 | tf_op jit(solution)/shard_map/ppermute | solution.py:402
  41.7 2.0 %collective-permute-done.10 = f32[120,128]{1,0:T(8,128)S(1)} collective-permute-done((f32[120,128]{1,0:T(8,128)S(1)}, f32[120,128]{1,0:T(8,128)S(1)}, u32[]{:S(2)}, u32[]{:S(2)}) %collective-permute-start.10) | collective-permute-done | bytes 61472 | tf_op jit(solution)/shard_map/ppermute | solution.py:402
  43.8 0.0 collective-permute-done.9
  43.8 1.5 %collective-permute-start.14 = (f32[120,128]{1,0:T(8,128)S(1)}, f32[120,128]{1,0:T(8,128)S(1)}, u32[]{:S(2)}, u32[]{:S(2)}) collective-permute-start(f32[120,128]{1,0:T(8,128)S(1)} %fusion), channel_id=1, source_target_pairs={{0,64},{32,96},{64,0},{96,32},{128,192},{160,224},{192,128},{224,1... | collective-permute-start | bytes 184328 | tf_op jit(solution)/shard_map/ppermute | solution.py:402
  45.2 1.2 %collective-permute-start.13 = (f32[120,128]{1,0:T(8,128)S(1)}, f32[120,128]{1,0:T(8,128)S(1)}, u32[]{:S(2)}, u32[]{:S(2)}) collective-permute-start(f32[120,128]{1,0:T(8,128)S(1)} %fusion), channel_id=1, source_target_pairs={{0,96},{32,64},{64,32},{96,0},{128,224},{160,192},{192,160},{224,1... | collective-permute-start | bytes 184328 | tf_op jit(solution)/shard_map/ppermute | solution.py:402
  46.4 0.1 collective-permute-start.12
  46.5 2.5 %collective-permute-done.14 = f32[120,128]{1,0:T(8,128)S(1)} collective-permute-done((f32[120,128]{1,0:T(8,128)S(1)}, f32[120,128]{1,0:T(8,128)S(1)}, u32[]{:S(2)}, u32[]{:S(2)}) %collective-permute-start.14) | collective-permute-done | bytes 61472 | tf_op jit(solution)/shard_map/ppermute | solution.py:402
  49.0 1.7 %collective-permute-done.13 = f32[120,128]{1,0:T(8,128)S(1)} collective-permute-done((f32[120,128]{1,0:T(8,128)S(1)}, f32[120,128]{1,0:T(8,128)S(1)}, u32[]{:S(2)}, u32[]{:S(2)}) %collective-permute-start.13) | collective-permute-done | bytes 61472 | tf_op jit(solution)/shard_map/ppermute | solution.py:402
  50.7 0.0 collective-permute-done.12
  50.7 1.7 %collective-permute-start.15 = (f32[120,128]{1,0:T(8,128)S(1)}, f32[120,128]{1,0:T(8,128)S(1)}, u32[]{:S(2)}, u32[]{:S(2)}) collective-permute-start(f32[120,128]{1,0:T(8,128)S(1)} %add_add_fusion), channel_id=1, source_target_pairs={{0,224},{32,192},{64,160},{96,128},{128,96},{160,64},{192,32},{224... | collective-permute-start | bytes 184328 | tf_op jit(solution)/shard_map/ppermute | solution.py:402
  52.4 0.0 copy-done.6
  52.4 1.6 %shard_map.236 = (bf16[1024,128]{1,0:T(8,128)(2,1)}, bf16[2688,128]{1,0:T(8,128)(2,1)}) custom-call(f32[1344,256]{1,0:T(8,128)S(1)} %get-tuple-element.112.cot_ref, bf16[1408,256]{1,0:T(8,128)(2,1)S(1)} %get-tuple-element.113.eback_ref, f32[1024,256]{1,0:T(8,128)S(1)} %get-tuple-element.114.sums_ref, f32[1024,128]{1,0:T(8,128)S(1)} %get-tuple-element.115.part_ref, ...), custom_call_target="tpu_custom_call" | custom-call | flops 2000000000 | bytes 6000000 | tf_op jit(solution)/shard_map/pallas_call | solution.py:363
  54.0 1.1 %collective-permute-done.15 = f32[120,128]{1,0:T(8,128)S(1)} collective-permute-done((f32[120,128]{1,0:T(8,128)S(1)}, f32[120,128]{1,0:T(8,128)S(1)}, u32[]{:S(2)}, u32[]{:S(2)}) %collective-permute-start.15) | collective-permute-done | bytes 61472 | tf_op jit(solution)/shard_map/ppermute | solution.py:402
  55.1 1.6 %collective-permute-start.18 = (f32[120,128]{1,0:T(8,128)S(1)}, f32[120,128]{1,0:T(8,128)S(1)}, u32[]{:S(2)}, u32[]{:S(2)}) collective-permute-start(f32[120,128]{1,0:T(8,128)S(1)} %add.31), channel_id=1, source_target_pairs={{0,16},{8,24},{16,0},{24,8},{1,17},{9,25},{17,1},{25,9},{2,18},{10... | collective-permute-start | bytes 184328 | tf_op jit(solution)/shard_map/ppermute | solution.py:402
  56.7 1.2 %collective-permute-start.17 = (f32[120,128]{1,0:T(8,128)S(1)}, f32[120,128]{1,0:T(8,128)S(1)}, u32[]{:S(2)}, u32[]{:S(2)}) collective-permute-start(f32[120,128]{1,0:T(8,128)S(1)} %add.31), channel_id=1, source_target_pairs={{0,24},{8,16},{16,8},{24,0},{1,25},{9,17},{17,9},{25,1},{2,26},{10... | collective-permute-start | bytes 184328 | tf_op jit(solution)/shard_map/ppermute | solution.py:402
  57.9 0.0 collective-permute-start.16
  57.9 1.9 %collective-permute-done.18 = f32[120,128]{1,0:T(8,128)S(1)} collective-permute-done((f32[120,128]{1,0:T(8,128)S(1)}, f32[120,128]{1,0:T(8,128)S(1)}, u32[]{:S(2)}, u32[]{:S(2)}) %collective-permute-start.18) | collective-permute-done | bytes 61472 | tf_op jit(solution)/shard_map/ppermute | solution.py:402
  59.8 1.2 %collective-permute-done.17 = f32[120,128]{1,0:T(8,128)S(1)} collective-permute-done((f32[120,128]{1,0:T(8,128)S(1)}, f32[120,128]{1,0:T(8,128)S(1)}, u32[]{:S(2)}, u32[]{:S(2)}) %collective-permute-start.17) | collective-permute-done | bytes 61472 | tf_op jit(solution)/shard_map/ppermute | solution.py:402
  61.0 0.0 collective-permute-done.16
  61.0 5.2 %collective-permute-start.19 = (f32[480,128]{1,0:T(8,128)S(1)}, f32[480,128]{1,0:T(8,128)S(1)}, u32[]{:S(2)}, u32[]{:S(2)}) collective-permute-start(f32[480,128]{1,0:T(8,128)S(1)} %pad_maximum_fusion.refs_0_), channel_id=1, source_target_pairs={{0,4},{4,0},{1,5},{5,1},{2,6},{6,2},{3,7},{7,3},{8,12},{12,8},{9,1... | collective-permute-start | bytes 737288 | tf_op jit(solution)/shard_map/ppermute | solution.py:402
  66.3 1.1 %collective-permute-done.19.refs_1_ = f32[480,128]{1,0:T(8,128)S(1)} collective-permute-done((f32[480,128]{1,0:T(8,128)S(1)}, f32[480,128]{1,0:T(8,128)S(1)}, u32[]{:S(2)}, u32[]{:S(2)}) %collective-permute-start.19) | collective-permute-done | bytes 245792 | tf_op jit(solution)/shard_map/ppermute | solution.py:402
  67.4 0.8 %shard_map.237 = (f32[384,128]{1,0:T(8,128)}, f32[1,128]{1,0:T(1,128)}, f32[128,128]{1,0:T(8,128)}, f32[1,128]{1,0:T(1,128)}, f32[256,128]{1,0:T(8,128)}, /*inde...) custom-call(f32[480,128]{1,0:T(8,128)S(1)} %pad_maximum_fusion.refs_0_, ...), custom_call_target="tpu_custom_call" | custom-call | flops 1000000 | bytes 1000000 | tf_op jit(solution)/shard_map/pallas_call | solution.py:363
  (15 shorter events, 0.1 us)
Async XLA Ops:
  0.6 17.4 %copy-start.2 = (bf16[256,128]{1,0:T(8,128)(2,1)S(1)}, bf16[256,128]{1,0:T(8,128)(2,1)}, u32[]{:S(2)}) copy-start(bf16[256,128]{1,0:T(8,128)(2,1)} %wn_ref.5) | copy-start | bytes 196612
  0.7 17.4 %copy-start.3 = (bf16[1024,128]{1,0:T(8,128)(2,1)S(1)}, bf16[1024,128]{1,0:T(8,128)(2,1)}, u32[]{:S(2)}) copy-start(bf16[1024,128]{1,0:T(8,128)(2,1)} %nf_ref.3) | copy-start | bytes 786436
  0.7 17.4 %copy-start.5 = (bf16[1024,128]{1,0:T(8,128)(2,1)S(1)}, bf16[1024,128]{1,0:T(8,128)(2,1)}, u32[]{:S(2)}) copy-start(bf16[1024,128]{1,0:T(8,128)(2,1)} %nc_ref.1) | copy-start | bytes 786436
  0.7 17.4 %copy-start.7 = (bf16[128,128]{1,0:T(8,128)(2,1)S(1)}, bf16[128,128]{1,0:T(8,128)(2,1)}, u32[]{:S(2)}) copy-start(bf16[128,128]{1,0:T(8,128)(2,1)} %wo_ref.2) | copy-start | bytes 98308
  0.7 17.4 %copy-start.8 = (s32[2,1344]{1,0:T(2,128)S(1)}, s32[2,1344]{1,0:T(2,128)}, u32[]{:S(2)}) copy-start(s32[2,1344]{1,0:T(2,128)} %ends_ref.1) | copy-start | bytes 32260
  0.7 17.4 %copy-start.9 = (s32[1024]{0:T(1024)S(1)}, s32[1024]{0:T(1024)}, u32[]{:S(2)}) copy-start(s32[1024]{0:T(1024)} %param.31) | copy-start | bytes 12292
  0.7 17.4 %copy-start.10 = (s32[1,4,128]{2,1,0:T(4,128)S(1)}, s32[1,4,128]{2,1,0:T(4,128)}, u32[]{:S(2)}) copy-start(s32[1,4,128]{2,1,0:T(4,128)} %param.29) | copy-start | bytes 6148
  0.7 17.4 %copy-start.11 = (s32[1,4]{1,0:T(1,128)S(1)}, s32[1,4]{1,0:T(1,128)}, u32[]{:S(2)}) copy-start(s32[1,4]{1,0:T(1,128)} %counts_ref.1) | copy-start | bytes 52
  0.7 17.4 %copy-start.12 = (f32[128]{0:T(128)S(1)}, f32[128]{0:T(128)}, u32[]{:S(2)}) copy-start(f32[128]{0:T(128)} %param.25) | copy-start | bytes 1540
  6.1 13.2 %collective-permute-start = (f32[128,128]{1,0:T(8,128)S(1)}, f32[128,128]{1,0:T(8,128)S(1)}, u32[]{:S(2)}, u32[]{:S(2)}) collective-permute-start(f32[128,128]{1,0:T(8,128)S(1)} %get-tuple-element.72), channel_id=1, source_target_pairs={{0,252},{4,8},{8,4},{12,16},{16,12},{20,24},{24,20},{28,32},{32,28... | collective-permute-start | bytes 196616 | tf_op jit(solution)/shard_map/ppermute | solution.py:395
  8.8 10.5 %collective-permute-start.1 = (f32[128,128]{1,0:T(8,128)S(1)}, f32[128,128]{1,0:T(8,128)S(1)}, u32[]{:S(2)}, u32[]{:S(2)}) collective-permute-start(f32[128,128]{1,0:T(8,128)S(1)} %get-tuple-element.73), channel_id=1, source_target_pairs={{0,64},{4,68},{8,72},{12,76},{16,80},{20,84},{24,88},{28,92},{32,9... | collective-permute-start | bytes 196616 | tf_op jit(solution)/shard_map/ppermute | solution.py:395
  11.8 7.5 %collective-permute-start.2 = (f32[128,128]{1,0:T(8,128)S(1)}, f32[128,128]{1,0:T(8,128)S(1)}, u32[]{:S(2)}, u32[]{:S(2)}) collective-permute-start(f32[128,128]{1,0:T(8,128)S(1)} %get-tuple-element.74), channel_id=1, source_target_pairs={{0,192},{4,196},{8,200},{12,204},{16,208},{20,212},{24,216},{28,22... | collective-permute-start | bytes 196616 | tf_op jit(solution)/shard_map/ppermute | solution.py:395
  16.0 3.3 %collective-permute-start.3 = (f32[128,128]{1,0:T(8,128)S(1)}, f32[128,128]{1,0:T(8,128)S(1)}, u32[]{:S(2)}, u32[]{:S(2)}) collective-permute-start(f32[128,128]{1,0:T(8,128)S(1)} %get-tuple-element.75), channel_id=1, source_target_pairs={{0,4},{4,0},{8,12},{12,8},{16,20},{20,16},{24,28},{28,24},{32,36},... | collective-permute-start | bytes 196616 | tf_op jit(solution)/shard_map/ppermute | solution.py:395
  19.3 8.5 %copy-start = (bf16[2688,128]{1,0:T(8,128)(2,1)S(1)}, bf16[2688,128]{1,0:T(8,128)(2,1)}, u32[]{:S(2)}) copy-start(bf16[2688,128]{1,0:T(8,128)(2,1)} %ef_ref.1) | copy-start | bytes 2064388
  19.3 8.5 %copy-start.1 = (bf16[2688,128]{1,0:T(8,128)(2,1)S(1)}, bf16[2688,128]{1,0:T(8,128)(2,1)}, u32[]{:S(2)}) copy-start(bf16[2688,128]{1,0:T(8,128)(2,1)} %ec_ref.1) | copy-start | bytes 2064388
  19.4 8.5 %copy-start.4 = (bf16[128,128]{1,0:T(8,128)(2,1)S(1)}, bf16[128,128]{1,0:T(8,128)(2,1)}, u32[]{:S(2)}) copy-start(bf16[128,128]{1,0:T(8,128)(2,1)} %wo_ref.3) | copy-start | bytes 98308
  20.8 8.3 %collective-permute-start.4 = (f32[128,128]{1,0:T(8,128)S(1)}, f32[128,128]{1,0:T(8,128)S(1)}, u32[]{:S(2)}, u32[]{:S(2)}) collective-permute-start(f32[128,128]{1,0:T(8,128)S(1)} %get-tuple-element.82), channel_id=1, source_target_pairs={{0,252},{4,8},{8,4},{12,16},{16,12},{20,24},{24,20},{28,32},{32,28... | collective-permute-start | bytes 196616 | tf_op jit(solution)/shard_map/ppermute | solution.py:395
  21.6 7.5 %collective-permute-start.5 = (f32[128,128]{1,0:T(8,128)S(1)}, f32[128,128]{1,0:T(8,128)S(1)}, u32[]{:S(2)}, u32[]{:S(2)}) collective-permute-start(f32[128,128]{1,0:T(8,128)S(1)} %get-tuple-element.83), channel_id=1, source_target_pairs={{0,64},{4,68},{8,72},{12,76},{16,80},{20,84},{24,88},{28,92},{32,9... | collective-permute-start | bytes 196616 | tf_op jit(solution)/shard_map/ppermute | solution.py:395
  23.0 6.1 %collective-permute-start.6 = (f32[128,128]{1,0:T(8,128)S(1)}, f32[128,128]{1,0:T(8,128)S(1)}, u32[]{:S(2)}, u32[]{:S(2)}) collective-permute-start(f32[128,128]{1,0:T(8,128)S(1)} %get-tuple-element.84), channel_id=1, source_target_pairs={{0,192},{4,196},{8,200},{12,204},{16,208},{20,212},{24,216},{28,22... | collective-permute-start | bytes 196616 | tf_op jit(solution)/shard_map/ppermute | solution.py:395
  26.0 3.1 %collective-permute-start.7 = (f32[128,128]{1,0:T(8,128)S(1)}, f32[128,128]{1,0:T(8,128)S(1)}, u32[]{:S(2)}, u32[]{:S(2)}) collective-permute-start(f32[128,128]{1,0:T(8,128)S(1)} %get-tuple-element.85), channel_id=1, source_target_pairs={{0,4},{4,0},{8,12},{12,8},{16,20},{20,16},{24,28},{28,24},{32,36},... | collective-permute-start | bytes 196616 | tf_op jit(solution)/shard_map/ppermute | solution.py:395
  32.2 20.2 %copy-start.6 = (bf16[384,128]{1,0:T(8,128)(2,1)S(1)}, bf16[384,128]{1,0:T(8,128)(2,1)}, u32[]{:S(2)}) copy-start(bf16[384,128]{1,0:T(8,128)(2,1)} %wi_ref.1) | copy-start | bytes 294916
  32.2 4.8 %collective-permute-start.8 = (f32[480,128]{1,0:T(8,128)S(1)}, f32[480,128]{1,0:T(8,128)S(1)}, u32[]{:S(2)}, u32[]{:S(2)}) collective-permute-start(f32[480,128]{1,0:T(8,128)S(1)} %get-tuple-element.103), channel_id=1, source_target_pairs={{0,4},{4,0},{1,5},{5,1},{2,6},{6,2},{3,7},{7,3},{8,12},{12,8},{9,1... | collective-permute-start | bytes 737288 | tf_op jit(solution)/shard_map/ppermute | solution.py:402
  37.0 4.7 %collective-permute-start.11 = (f32[120,128]{1,0:T(8,128)S(1)}, f32[120,128]{1,0:T(8,128)S(1)}, u32[]{:S(2)}, u32[]{:S(2)}) collective-permute-start(f32[120,128]{1,0:T(8,128)S(1)} %get-tuple-element.132), channel_id=1, source_target_pairs={{0,16},{8,24},{16,0},{24,8},{1,17},{9,25},{17,1},{25,9},{2,18},{10... | collective-permute-start | bytes 184328 | tf_op jit(solution)/shard_map/ppermute | solution.py:402
  37.8 6.0 %collective-permute-start.10 = (f32[120,128]{1,0:T(8,128)S(1)}, f32[120,128]{1,0:T(8,128)S(1)}, u32[]{:S(2)}, u32[]{:S(2)}) collective-permute-start(f32[120,128]{1,0:T(8,128)S(1)} %get-tuple-element.133), channel_id=1, source_target_pairs={{0,24},{8,16},{16,8},{24,0},{1,25},{9,17},{17,9},{25,1},{2,26},{10... | collective-permute-start | bytes 184328 | tf_op jit(solution)/shard_map/ppermute | solution.py:402
  38.8 5.0 %collective-permute-start.9 = (f32[120,128]{1,0:T(8,128)S(1)}, f32[120,128]{1,0:T(8,128)S(1)}, u32[]{:S(2)}, u32[]{:S(2)}) collective-permute-start(f32[120,128]{1,0:T(8,128)S(1)} %get-tuple-element.134), channel_id=1, source_target_pairs={{0,8},{8,0},{16,24},{24,16},{1,9},{9,1},{17,25},{25,17},{2,10},{10... | collective-permute-start | bytes 184328 | tf_op jit(solution)/shard_map/ppermute | solution.py:402
  43.8 5.2 %collective-permute-start.14 = (f32[120,128]{1,0:T(8,128)S(1)}, f32[120,128]{1,0:T(8,128)S(1)}, u32[]{:S(2)}, u32[]{:S(2)}) collective-permute-start(f32[120,128]{1,0:T(8,128)S(1)} %fusion), channel_id=1, source_target_pairs={{0,64},{32,96},{64,0},{96,32},{128,192},{160,224},{192,128},{224,1... | collective-permute-start | bytes 184328 | tf_op jit(solution)/shard_map/ppermute | solution.py:402
  45.2 5.5 %collective-permute-start.13 = (f32[120,128]{1,0:T(8,128)S(1)}, f32[120,128]{1,0:T(8,128)S(1)}, u32[]{:S(2)}, u32[]{:S(2)}) collective-permute-start(f32[120,128]{1,0:T(8,128)S(1)} %fusion), channel_id=1, source_target_pairs={{0,96},{32,64},{64,32},{96,0},{128,224},{160,192},{192,160},{224,1... | collective-permute-start | bytes 184328 | tf_op jit(solution)/shard_map/ppermute | solution.py:402
  46.4 4.3 %collective-permute-start.12 = (f32[120,128]{1,0:T(8,128)S(1)}, f32[120,128]{1,0:T(8,128)S(1)}, u32[]{:S(2)}, u32[]{:S(2)}) collective-permute-start(f32[120,128]{1,0:T(8,128)S(1)} %fusion), channel_id=1, source_target_pairs={{0,32},{32,0},{64,96},{96,64},{128,160},{160,128},{192,224},{224,1... | collective-permute-start | bytes 184328 | tf_op jit(solution)/shard_map/ppermute | solution.py:402
  50.7 4.4 %collective-permute-start.15 = (f32[120,128]{1,0:T(8,128)S(1)}, f32[120,128]{1,0:T(8,128)S(1)}, u32[]{:S(2)}, u32[]{:S(2)}) collective-permute-start(f32[120,128]{1,0:T(8,128)S(1)} %add_add_fusion), channel_id=1, source_target_pairs={{0,224},{32,192},{64,160},{96,128},{128,96},{160,64},{192,32},{224... | collective-permute-start | bytes 184328 | tf_op jit(solution)/shard_map/ppermute | solution.py:402
  55.1 4.7 %collective-permute-start.18 = (f32[120,128]{1,0:T(8,128)S(1)}, f32[120,128]{1,0:T(8,128)S(1)}, u32[]{:S(2)}, u32[]{:S(2)}) collective-permute-start(f32[120,128]{1,0:T(8,128)S(1)} %add.31), channel_id=1, source_target_pairs={{0,16},{8,24},{16,0},{24,8},{1,17},{9,25},{17,1},{25,9},{2,18},{10... | collective-permute-start | bytes 184328 | tf_op jit(solution)/shard_map/ppermute | solution.py:402
  56.7 4.3 %collective-permute-start.17 = (f32[120,128]{1,0:T(8,128)S(1)}, f32[120,128]{1,0:T(8,128)S(1)}, u32[]{:S(2)}, u32[]{:S(2)}) collective-permute-start(f32[120,128]{1,0:T(8,128)S(1)} %add.31), channel_id=1, source_target_pairs={{0,24},{8,16},{16,8},{24,0},{1,25},{9,17},{17,9},{25,1},{2,26},{10... | collective-permute-start | bytes 184328 | tf_op jit(solution)/shard_map/ppermute | solution.py:402
  57.9 3.1 %collective-permute-start.16 = (f32[120,128]{1,0:T(8,128)S(1)}, f32[120,128]{1,0:T(8,128)S(1)}, u32[]{:S(2)}, u32[]{:S(2)}) collective-permute-start(f32[120,128]{1,0:T(8,128)S(1)} %add.31), channel_id=1, source_target_pairs={{0,8},{8,0},{16,24},{24,16},{1,9},{9,1},{17,25},{25,17},{2,10},{10... | collective-permute-start | bytes 184328 | tf_op jit(solution)/shard_map/ppermute | solution.py:402
  61.0 6.4 %collective-permute-start.19 = (f32[480,128]{1,0:T(8,128)S(1)}, f32[480,128]{1,0:T(8,128)S(1)}, u32[]{:S(2)}, u32[]{:S(2)}) collective-permute-start(f32[480,128]{1,0:T(8,128)S(1)} %pad_maximum_fusion.refs_0_), channel_id=1, source_target_pairs={{0,4},{4,0},{1,5},{5,1},{2,6},{6,2},{3,7},{7,3},{8,12},{12,8},{9,1... | collective-permute-start | bytes 737288 | tf_op jit(solution)/shard_map/ppermute | solution.py:402

commit v5 on v4

--- a/solution.py
+++ b/solution.py
@@ -81,16 +81,14 @@
 
 
 def outgoing(table_ref, values, refs):
-    both = dot(table_ref[...], jnp.concatenate(split(values), axis=1))
+    picked = dot(table_ref[...], values.astype(BF16))
     for k, ref in enumerate(refs):
-        part = both[k * LANES : (k + 1) * LANES]
-        ref[...] = part[:, :LANES] + part[:, LANES:]
+        ref[...] = picked[k * LANES : (k + 1) * LANES]
 
 
 def incoming(table_ref, refs):
     arrived = jnp.concatenate([ref[...] for ref in refs], axis=0)
-    both = dot(table_ref[...], jnp.concatenate(split(arrived), axis=1))
-    return both[:, :LANES] + both[:, LANES:]
+    return dot(table_ref[...], arrived.astype(BF16))
 
 
 def spans(count, block):

time: 68.4 us -> 68.3 us (level)
  no operation moved by 1% of the time
where the time goes in v5:
time: 68.3 us; the launch traced here: 68.2 us
  starting transfers between devices  37.2 us (54%)
  waiting for transfers between devices  14.7 us (22%)
  Pallas kernels  14.5 us (21%)
  between operations  1.61 us (2%)
    ppermute x12, starting transfers between devices, swapped_with(): lax.ppermute(value, axis, [(s, partner(s)) for s in range(lax.axis_size(a...  18.8 us
    ppermute x8, starting transfers between devices, swapped(): lax.ppermute(message, AXES, [(s, swap(s) % count) for s in range(count)])  18.4 us
    ppermute x12, waiting for transfers between devices, swapped_with(): lax.ppermute(value, axis, [(s, partner(s)) for s in range(lax.axis_size(a...  14.7 us
    pallas_call x7, Pallas kernels, call(): pl.pallas_call(kernel, out_shape=[jax.ShapeDtypeStruct(shape, dtype) for...  14.5 us
  transfers between devices with their start and end apart: 20, of which 9 were waited for; matrix products, arithmetic and copies ran while one was open for 0% of the time, Pallas kernels for 6%

profile of v5, /device:TPU:1, one launch (start us, length us, event | category | flops | bytes accessed | tf_op | source)
XLA Modules:
  0.0 68.2 jit_solution(14701210374045999855)
XLA Ops:
  0.6 0.0 copy-start.2
  0.7 0.0 copy-start.3
  0.7 0.0 copy-start.5
  0.7 0.0 copy-start.7
  0.7 0.0 copy-start.8
  0.7 0.0 copy-start.9
  0.7 0.0 copy-start.10
  0.7 0.0 copy-start.11
  0.7 0.0 copy-start.12
  0.7 5.3 %shard_map.231 = (f32[1024,128]{1,0:T(8,128)S(1)}, f32[128,128]{1,0:T(8,128)S(1)}, f32[128,128]{1,0:T(8,128)S(1)}, f32[128,128]{1,0:T(8,128)S(1)}, f32[128,128]{...) custom-call(s32[1,4]{1,0:T(1,128)} %counts_ref.1, ...), custom_call_target="tpu_custom_call" | custom-call | flops 2000000000 | bytes 4000000 | tf_op jit(solution)/shard_map/pallas_call | solution.py:361
  6.0 2.8 %collective-permute-start = (f32[128,128]{1,0:T(8,128)S(1)}, f32[128,128]{1,0:T(8,128)S(1)}, u32[]{:S(2)}, u32[]{:S(2)}) collective-permute-start(f32[128,128]{1,0:T(8,128)S(1)} %get-tuple-element.72), channel_id=1, source_target_pairs={{0,252},{4,8},{8,4},{12,16},{16,12},{20,24},{24,20},{28,32},{32,28... | collective-permute-start | bytes 196616 | tf_op jit(solution)/shard_map/ppermute | solution.py:393
  8.8 3.0 %collective-permute-start.1 = (f32[128,128]{1,0:T(8,128)S(1)}, f32[128,128]{1,0:T(8,128)S(1)}, u32[]{:S(2)}, u32[]{:S(2)}) collective-permute-start(f32[128,128]{1,0:T(8,128)S(1)} %get-tuple-element.73), channel_id=1, source_target_pairs={{0,64},{4,68},{8,72},{12,76},{16,80},{20,84},{24,88},{28,92},{32,9... | collective-permute-start | bytes 196616 | tf_op jit(solution)/shard_map/ppermute | solution.py:393
  11.8 4.2 %collective-permute-start.2 = (f32[128,128]{1,0:T(8,128)S(1)}, f32[128,128]{1,0:T(8,128)S(1)}, u32[]{:S(2)}, u32[]{:S(2)}) collective-permute-start(f32[128,128]{1,0:T(8,128)S(1)} %get-tuple-element.74), channel_id=1, source_target_pairs={{0,192},{4,196},{8,200},{12,204},{16,208},{20,212},{24,216},{28,22... | collective-permute-start | bytes 196616 | tf_op jit(solution)/shard_map/ppermute | solution.py:393
  16.0 1.4 %collective-permute-start.3 = (f32[128,128]{1,0:T(8,128)S(1)}, f32[128,128]{1,0:T(8,128)S(1)}, u32[]{:S(2)}, u32[]{:S(2)}) collective-permute-start(f32[128,128]{1,0:T(8,128)S(1)} %get-tuple-element.75), channel_id=1, source_target_pairs={{0,4},{4,0},{8,12},{12,8},{16,20},{20,16},{24,28},{28,24},{32,36},... | collective-permute-start | bytes 196616 | tf_op jit(solution)/shard_map/ppermute | solution.py:393
  18.0 0.0 copy-done.2
  18.0 0.0 copy-done.3
  18.1 0.0 copy-done.5
  18.1 1.2 %shard_map.232 = (bf16[512,1408]{1,0:T(8,128)(2,1)S(1)}, bf16[1024,512]{1,0:T(8,128)(2,1)S(1)}, f32[1024,128]{1,0:T(8,128)S(1)}, f32[1024,128]{1,0:T(8,128)S(1)}...) custom-call(s32[1,4]{1,0:T(1,128)S(1)} %copy-done.11, s32[1]{0:T(128)S(6)} %copy.26.live_ref, ...), custom_call_target="tpu_custom_call" | custom-call | flops 1000000000 | bytes 4000000 | tf_op jit(solution)/shard_map/pallas_call | solution.py:361
  19.3 0.0 collective-permute-done.in0
  19.3 0.0 collective-permute-done.1.in1
  19.3 0.0 collective-permute-done.2.in2
  19.3 0.0 collective-permute-done.3.in3
  19.3 0.0 copy-start
  19.3 0.0 copy-start.1
  19.3 0.0 copy-start.4
  19.4 1.4 %shard_map.233 = (f32[1024,128]{1,0:T(8,128)S(1)}, f32[128,128]{1,0:T(8,128)S(1)}, f32[128,128]{1,0:T(8,128)S(1)}, f32[128,128]{1,0:T(8,128)S(1)}, f32[128,128]{...) custom-call(f32[1024,128]{1,0:T(8,128)S(1)} %get-tuple-element.71.agg_, ...), custom_call_target="tpu_custom_call" | custom-call | flops 600000000 | bytes 4000000 | tf_op jit(solution)/shard_map/pallas_call | solution.py:361
  20.8 0.8 %collective-permute-start.4 = (f32[128,128]{1,0:T(8,128)S(1)}, f32[128,128]{1,0:T(8,128)S(1)}, u32[]{:S(2)}, u32[]{:S(2)}) collective-permute-start(f32[128,128]{1,0:T(8,128)S(1)} %get-tuple-element.82), channel_id=1, source_target_pairs={{0,252},{4,8},{8,4},{12,16},{16,12},{20,24},{24,20},{28,32},{32,28... | collective-permute-start | bytes 196616 | tf_op jit(solution)/shard_map/ppermute | solution.py:393
  21.6 1.5 %collective-permute-start.5 = (f32[128,128]{1,0:T(8,128)S(1)}, f32[128,128]{1,0:T(8,128)S(1)}, u32[]{:S(2)}, u32[]{:S(2)}) collective-permute-start(f32[128,128]{1,0:T(8,128)S(1)} %get-tuple-element.83), channel_id=1, source_target_pairs={{0,64},{4,68},{8,72},{12,76},{16,80},{20,84},{24,88},{28,92},{32,9... | collective-permute-start | bytes 196616 | tf_op jit(solution)/shard_map/ppermute | solution.py:393
  23.0 3.0 %collective-permute-start.6 = (f32[128,128]{1,0:T(8,128)S(1)}, f32[128,128]{1,0:T(8,128)S(1)}, u32[]{:S(2)}, u32[]{:S(2)}) collective-permute-start(f32[128,128]{1,0:T(8,128)S(1)} %get-tuple-element.84), channel_id=1, source_target_pairs={{0,192},{4,196},{8,200},{12,204},{16,208},{20,212},{24,216},{28,22... | collective-permute-start | bytes 196616 | tf_op jit(solution)/shard_map/ppermute | solution.py:393
  26.0 1.8 %collective-permute-start.7 = (f32[128,128]{1,0:T(8,128)S(1)}, f32[128,128]{1,0:T(8,128)S(1)}, u32[]{:S(2)}, u32[]{:S(2)}) collective-permute-start(f32[128,128]{1,0:T(8,128)S(1)} %get-tuple-element.85), channel_id=1, source_target_pairs={{0,4},{4,0},{8,12},{12,8},{16,20},{20,16},{24,28},{28,24},{32,36},... | collective-permute-start | bytes 196616 | tf_op jit(solution)/shard_map/ppermute | solution.py:393
  27.8 0.0 copy-done.4
  27.8 1.2 %shard_map.234 = (f32[1024,128]{1,0:T(8,128)S(1)}, f32[448,128]{1,0:T(8,128)S(1)}, bf16[1344,256]{1,0:T(8,128)(2,1)S(1)}, bf16[256,1408]{1,0:T(8,128)(2,1)S(1)},...) custom-call(s32[1]{0:T(128)S(6)} %copy.26.live_ref, ...), custom_call_target="tpu_custom_call" | custom-call | flops 1000000000 | bytes 4000000 | tf_op jit(solution)/shard_map/pallas_call | solution.py:361
  29.1 0.0 collective-permute-done.4.in0
  29.1 0.0 collective-permute-done.5.in1
  29.1 0.0 collective-permute-done.6.in2
  29.1 0.0 collective-permute-done.7.in3
  29.1 3.0 %shard_map.235 = (f32[1344,256]{1,0:T(8,128)S(1)}, bf16[1408,256]{1,0:T(8,128)(2,1)S(1)}, f32[1024,256]{1,0:T(8,128)S(1)}, f32[480,128]{1,0:T(8,128)S(1)}, f32[480,128]{1,0:T(8,128)S(1)}) custom-call(f32[1024,128]{1,0:T(8,128)S(1)} %get-tuple-element.81.cback_ref, f32[128,128]{1,0:T(8,128)S(1)} %collective-permute-done.4.in0, ...), custom_call_target="tpu_custom_call" | custom-call | flops 2000000000 | bytes 6000000 | tf_op jit(solution)/shard_map/pallas_call | solution.py:361
  32.1 0.0 copy-start.6
  32.1 3.6 %collective-permute-start.8 = (f32[480,128]{1,0:T(8,128)S(1)}, f32[480,128]{1,0:T(8,128)S(1)}, u32[]{:S(2)}, u32[]{:S(2)}) collective-permute-start(f32[480,128]{1,0:T(8,128)S(1)} %get-tuple-element.103), channel_id=1, source_target_pairs={{0,4},{4,0},{1,5},{5,1},{2,6},{6,2},{3,7},{7,3},{8,12},{12,8},{9,1... | collective-permute-start | bytes 737288 | tf_op jit(solution)/shard_map/ppermute | solution.py:400
  35.8 1.1 %collective-permute-done.8 = f32[480,128]{1,0:T(8,128)S(1)} collective-permute-done((f32[480,128]{1,0:T(8,128)S(1)}, f32[480,128]{1,0:T(8,128)S(1)}, u32[]{:S(2)}, u32[]{:S(2)}) %collective-permute-start.8) | collective-permute-done | bytes 245792 | tf_op jit(solution)/shard_map/ppermute | solution.py:400
  37.0 0.7 %collective-permute-start.11 = (f32[120,128]{1,0:T(8,128)S(1)}, f32[120,128]{1,0:T(8,128)S(1)}, u32[]{:S(2)}, u32[]{:S(2)}) collective-permute-start(f32[120,128]{1,0:T(8,128)S(1)} %get-tuple-element.132), channel_id=1, source_target_pairs={{0,16},{8,24},{16,0},{24,8},{1,17},{9,25},{17,1},{25,9},{2,18},{10... | collective-permute-start | bytes 184328 | tf_op jit(solution)/shard_map/ppermute | solution.py:400
  37.7 1.0 %collective-permute-start.10 = (f32[120,128]{1,0:T(8,128)S(1)}, f32[120,128]{1,0:T(8,128)S(1)}, u32[]{:S(2)}, u32[]{:S(2)}) collective-permute-start(f32[120,128]{1,0:T(8,128)S(1)} %get-tuple-element.133), channel_id=1, source_target_pairs={{0,24},{8,16},{16,8},{24,0},{1,25},{9,17},{17,9},{25,1},{2,26},{10... | collective-permute-start | bytes 184328 | tf_op jit(solution)/shard_map/ppermute | solution.py:400
  38.7 1.0 %collective-permute-start.9 = (f32[120,128]{1,0:T(8,128)S(1)}, f32[120,128]{1,0:T(8,128)S(1)}, u32[]{:S(2)}, u32[]{:S(2)}) collective-permute-start(f32[120,128]{1,0:T(8,128)S(1)} %get-tuple-element.134), channel_id=1, source_target_pairs={{0,8},{8,0},{16,24},{24,16},{1,9},{9,1},{17,25},{25,17},{2,10},{10... | collective-permute-start | bytes 184328 | tf_op jit(solution)/shard_map/ppermute | solution.py:400
  39.7 2.0 %collective-permute-done.11 = f32[120,128]{1,0:T(8,128)S(1)} collective-permute-done((f32[120,128]{1,0:T(8,128)S(1)}, f32[120,128]{1,0:T(8,128)S(1)}, u32[]{:S(2)}, u32[]{:S(2)}) %collective-permute-start.11) | collective-permute-done | bytes 61472 | tf_op jit(solution)/shard_map/ppermute | solution.py:400
  41.7 2.0 %collective-permute-done.10 = f32[120,128]{1,0:T(8,128)S(1)} collective-permute-done((f32[120,128]{1,0:T(8,128)S(1)}, f32[120,128]{1,0:T(8,128)S(1)}, u32[]{:S(2)}, u32[]{:S(2)}) %collective-permute-start.10) | collective-permute-done | bytes 61472 | tf_op jit(solution)/shard_map/ppermute | solution.py:400
  43.7 0.0 collective-permute-done.9
  43.7 1.5 %collective-permute-start.14 = (f32[120,128]{1,0:T(8,128)S(1)}, f32[120,128]{1,0:T(8,128)S(1)}, u32[]{:S(2)}, u32[]{:S(2)}) collective-permute-start(f32[120,128]{1,0:T(8,128)S(1)} %fusion), channel_id=1, source_target_pairs={{0,64},{32,96},{64,0},{96,32},{128,192},{160,224},{192,128},{224,1... | collective-permute-start | bytes 184328 | tf_op jit(solution)/shard_map/ppermute | solution.py:400
  45.2 1.2 %collective-permute-start.13 = (f32[120,128]{1,0:T(8,128)S(1)}, f32[120,128]{1,0:T(8,128)S(1)}, u32[]{:S(2)}, u32[]{:S(2)}) collective-permute-start(f32[120,128]{1,0:T(8,128)S(1)} %fusion), channel_id=1, source_target_pairs={{0,96},{32,64},{64,32},{96,0},{128,224},{160,192},{192,160},{224,1... | collective-permute-start | bytes 184328 | tf_op jit(solution)/shard_map/ppermute | solution.py:400
  46.3 0.1 collective-permute-start.12
  46.4 2.5 %collective-permute-done.14 = f32[120,128]{1,0:T(8,128)S(1)} collective-permute-done((f32[120,128]{1,0:T(8,128)S(1)}, f32[120,128]{1,0:T(8,128)S(1)}, u32[]{:S(2)}, u32[]{:S(2)}) %collective-permute-start.14) | collective-permute-done | bytes 61472 | tf_op jit(solution)/shard_map/ppermute | solution.py:400
  48.9 1.7 %collective-permute-done.13 = f32[120,128]{1,0:T(8,128)S(1)} collective-permute-done((f32[120,128]{1,0:T(8,128)S(1)}, f32[120,128]{1,0:T(8,128)S(1)}, u32[]{:S(2)}, u32[]{:S(2)}) %collective-permute-start.13) | collective-permute-done | bytes 61472 | tf_op jit(solution)/shard_map/ppermute | solution.py:400
  50.6 0.0 collective-permute-done.12
  50.7 1.7 %collective-permute-start.15 = (f32[120,128]{1,0:T(8,128)S(1)}, f32[120,128]{1,0:T(8,128)S(1)}, u32[]{:S(2)}, u32[]{:S(2)}) collective-permute-start(f32[120,128]{1,0:T(8,128)S(1)} %add_add_fusion), channel_id=1, source_target_pairs={{0,224},{32,192},{64,160},{96,128},{128,96},{160,64},{192,32},{224... | collective-permute-start | bytes 184328 | tf_op jit(solution)/shard_map/ppermute | solution.py:400
  52.3 1.6 %shard_map.236 = (bf16[1024,128]{1,0:T(8,128)(2,1)}, bf16[2688,128]{1,0:T(8,128)(2,1)}) custom-call(f32[1344,256]{1,0:T(8,128)S(1)} %get-tuple-element.112.cot_ref, bf16[1408,256]{1,0:T(8,128)(2,1)S(1)} %get-tuple-element.113.eback_ref, f32[1024,256]{1,0:T(8,128)S(1)} %get-tuple-element.114.sums_ref, f32[1024,128]{1,0:T(8,128)S(1)} %get-tuple-element.115.part_ref, ...), custom_call_target="tpu_custom_call" | custom-call | flops 2000000000 | bytes 6000000 | tf_op jit(solution)/shard_map/pallas_call | solution.py:361
  53.9 1.1 %collective-permute-done.15 = f32[120,128]{1,0:T(8,128)S(1)} collective-permute-done((f32[120,128]{1,0:T(8,128)S(1)}, f32[120,128]{1,0:T(8,128)S(1)}, u32[]{:S(2)}, u32[]{:S(2)}) %collective-permute-start.15) | collective-permute-done | bytes 61472 | tf_op jit(solution)/shard_map/ppermute | solution.py:400
  55.0 1.6 %collective-permute-start.18 = (f32[120,128]{1,0:T(8,128)S(1)}, f32[120,128]{1,0:T(8,128)S(1)}, u32[]{:S(2)}, u32[]{:S(2)}) collective-permute-start(f32[120,128]{1,0:T(8,128)S(1)} %add.31), channel_id=1, source_target_pairs={{0,16},{8,24},{16,0},{24,8},{1,17},{9,25},{17,1},{25,9},{2,18},{10... | collective-permute-start | bytes 184328 | tf_op jit(solution)/shard_map/ppermute | solution.py:400
  56.7 1.2 %collective-permute-start.17 = (f32[120,128]{1,0:T(8,128)S(1)}, f32[120,128]{1,0:T(8,128)S(1)}, u32[]{:S(2)}, u32[]{:S(2)}) collective-permute-start(f32[120,128]{1,0:T(8,128)S(1)} %add.31), channel_id=1, source_target_pairs={{0,24},{8,16},{16,8},{24,0},{1,25},{9,17},{17,9},{25,1},{2,26},{10... | collective-permute-start | bytes 184328 | tf_op jit(solution)/shard_map/ppermute | solution.py:400
  57.8 0.0 collective-permute-start.16
  57.8 1.9 %collective-permute-done.18 = f32[120,128]{1,0:T(8,128)S(1)} collective-permute-done((f32[120,128]{1,0:T(8,128)S(1)}, f32[120,128]{1,0:T(8,128)S(1)}, u32[]{:S(2)}, u32[]{:S(2)}) %collective-permute-start.18) | collective-permute-done | bytes 61472 | tf_op jit(solution)/shard_map/ppermute | solution.py:400
  59.7 1.2 %collective-permute-done.17 = f32[120,128]{1,0:T(8,128)S(1)} collective-permute-done((f32[120,128]{1,0:T(8,128)S(1)}, f32[120,128]{1,0:T(8,128)S(1)}, u32[]{:S(2)}, u32[]{:S(2)}) %collective-permute-start.17) | collective-permute-done | bytes 61472 | tf_op jit(solution)/shard_map/ppermute | solution.py:400
  61.0 0.0 collective-permute-done.16
  61.0 5.2 %collective-permute-start.19 = (f32[480,128]{1,0:T(8,128)S(1)}, f32[480,128]{1,0:T(8,128)S(1)}, u32[]{:S(2)}, u32[]{:S(2)}) collective-permute-start(f32[480,128]{1,0:T(8,128)S(1)} %pad_maximum_fusion.refs_0_), channel_id=1, source_target_pairs={{0,4},{4,0},{1,5},{5,1},{2,6},{6,2},{3,7},{7,3},{8,12},{12,8},{9,1... | collective-permute-start | bytes 737288 | tf_op jit(solution)/shard_map/ppermute | solution.py:400
  66.2 1.1 %collective-permute-done.19.refs_1_ = f32[480,128]{1,0:T(8,128)S(1)} collective-permute-done((f32[480,128]{1,0:T(8,128)S(1)}, f32[480,128]{1,0:T(8,128)S(1)}, u32[]{:S(2)}, u32[]{:S(2)}) %collective-permute-start.19) | collective-permute-done | bytes 245792 | tf_op jit(solution)/shard_map/ppermute | solution.py:400
  67.3 0.8 %shard_map.237 = (f32[384,128]{1,0:T(8,128)}, f32[1,128]{1,0:T(1,128)}, f32[128,128]{1,0:T(8,128)}, f32[1,128]{1,0:T(1,128)}, f32[256,128]{1,0:T(8,128)}, /*inde...) custom-call(f32[480,128]{1,0:T(8,128)S(1)} %pad_maximum_fusion.refs_0_, ...), custom_call_target="tpu_custom_call" | custom-call | flops 1000000 | bytes 1000000 | tf_op jit(solution)/shard_map/pallas_call | solution.py:361
  (15 shorter events, 0.1 us)
Async XLA Ops:
  0.6 17.4 %copy-start.2 = (bf16[256,128]{1,0:T(8,128)(2,1)S(1)}, bf16[256,128]{1,0:T(8,128)(2,1)}, u32[]{:S(2)}) copy-start(bf16[256,128]{1,0:T(8,128)(2,1)} %wn_ref.5) | copy-start | bytes 196612
  0.7 17.4 %copy-start.3 = (bf16[1024,128]{1,0:T(8,128)(2,1)S(1)}, bf16[1024,128]{1,0:T(8,128)(2,1)}, u32[]{:S(2)}) copy-start(bf16[1024,128]{1,0:T(8,128)(2,1)} %nf_ref.3) | copy-start | bytes 786436
  0.7 17.4 %copy-start.5 = (bf16[1024,128]{1,0:T(8,128)(2,1)S(1)}, bf16[1024,128]{1,0:T(8,128)(2,1)}, u32[]{:S(2)}) copy-start(bf16[1024,128]{1,0:T(8,128)(2,1)} %nc_ref.1) | copy-start | bytes 786436
  0.7 17.4 %copy-start.7 = (bf16[128,128]{1,0:T(8,128)(2,1)S(1)}, bf16[128,128]{1,0:T(8,128)(2,1)}, u32[]{:S(2)}) copy-start(bf16[128,128]{1,0:T(8,128)(2,1)} %wo_ref.2) | copy-start | bytes 98308
  0.7 17.4 %copy-start.8 = (s32[2,1344]{1,0:T(2,128)S(1)}, s32[2,1344]{1,0:T(2,128)}, u32[]{:S(2)}) copy-start(s32[2,1344]{1,0:T(2,128)} %ends_ref.1) | copy-start | bytes 32260
  0.7 17.4 %copy-start.9 = (s32[1024]{0:T(1024)S(1)}, s32[1024]{0:T(1024)}, u32[]{:S(2)}) copy-start(s32[1024]{0:T(1024)} %param.31) | copy-start | bytes 12292
  0.7 17.4 %copy-start.10 = (s32[1,4,128]{2,1,0:T(4,128)S(1)}, s32[1,4,128]{2,1,0:T(4,128)}, u32[]{:S(2)}) copy-start(s32[1,4,128]{2,1,0:T(4,128)} %param.29) | copy-start | bytes 6148
  0.7 17.4 %copy-start.11 = (s32[1,4]{1,0:T(1,128)S(1)}, s32[1,4]{1,0:T(1,128)}, u32[]{:S(2)}) copy-start(s32[1,4]{1,0:T(1,128)} %counts_ref.1) | copy-start | bytes 52
  0.7 17.4 %copy-start.12 = (f32[128]{0:T(128)S(1)}, f32[128]{0:T(128)}, u32[]{:S(2)}) copy-start(f32[128]{0:T(128)} %param.25) | copy-start | bytes 1540
  6.0 13.2 %collective-permute-start = (f32[128,128]{1,0:T(8,128)S(1)}, f32[128,128]{1,0:T(8,128)S(1)}, u32[]{:S(2)}, u32[]{:S(2)}) collective-permute-start(f32[128,128]{1,0:T(8,128)S(1)} %get-tuple-element.72), channel_id=1, source_target_pairs={{0,252},{4,8},{8,4},{12,16},{16,12},{20,24},{24,20},{28,32},{32,28... | collective-permute-start | bytes 196616 | tf_op jit(solution)/shard_map/ppermute | solution.py:393
  8.8 10.5 %collective-permute-start.1 = (f32[128,128]{1,0:T(8,128)S(1)}, f32[128,128]{1,0:T(8,128)S(1)}, u32[]{:S(2)}, u32[]{:S(2)}) collective-permute-start(f32[128,128]{1,0:T(8,128)S(1)} %get-tuple-element.73), channel_id=1, source_target_pairs={{0,64},{4,68},{8,72},{12,76},{16,80},{20,84},{24,88},{28,92},{32,9... | collective-permute-start | bytes 196616 | tf_op jit(solution)/shard_map/ppermute | solution.py:393
  11.8 7.5 %collective-permute-start.2 = (f32[128,128]{1,0:T(8,128)S(1)}, f32[128,128]{1,0:T(8,128)S(1)}, u32[]{:S(2)}, u32[]{:S(2)}) collective-permute-start(f32[128,128]{1,0:T(8,128)S(1)} %get-tuple-element.74), channel_id=1, source_target_pairs={{0,192},{4,196},{8,200},{12,204},{16,208},{20,212},{24,216},{28,22... | collective-permute-start | bytes 196616 | tf_op jit(solution)/shard_map/ppermute | solution.py:393
  16.0 3.3 %collective-permute-start.3 = (f32[128,128]{1,0:T(8,128)S(1)}, f32[128,128]{1,0:T(8,128)S(1)}, u32[]{:S(2)}, u32[]{:S(2)}) collective-permute-start(f32[128,128]{1,0:T(8,128)S(1)} %get-tuple-element.75), channel_id=1, source_target_pairs={{0,4},{4,0},{8,12},{12,8},{16,20},{20,16},{24,28},{28,24},{32,36},... | collective-permute-start | bytes 196616 | tf_op jit(solution)/shard_map/ppermute | solution.py:393
  19.3 8.5 %copy-start = (bf16[2688,128]{1,0:T(8,128)(2,1)S(1)}, bf16[2688,128]{1,0:T(8,128)(2,1)}, u32[]{:S(2)}) copy-start(bf16[2688,128]{1,0:T(8,128)(2,1)} %ef_ref.1) | copy-start | bytes 2064388
  19.3 8.5 %copy-start.1 = (bf16[2688,128]{1,0:T(8,128)(2,1)S(1)}, bf16[2688,128]{1,0:T(8,128)(2,1)}, u32[]{:S(2)}) copy-start(bf16[2688,128]{1,0:T(8,128)(2,1)} %ec_ref.1) | copy-start | bytes 2064388
  19.3 8.5 %copy-start.4 = (bf16[128,128]{1,0:T(8,128)(2,1)S(1)}, bf16[128,128]{1,0:T(8,128)(2,1)}, u32[]{:S(2)}) copy-start(bf16[128,128]{1,0:T(8,128)(2,1)} %wo_ref.3) | copy-start | bytes 98308
  20.8 8.3 %collective-permute-start.4 = (f32[128,128]{1,0:T(8,128)S(1)}, f32[128,128]{1,0:T(8,128)S(1)}, u32[]{:S(2)}, u32[]{:S(2)}) collective-permute-start(f32[128,128]{1,0:T(8,128)S(1)} %get-tuple-element.82), channel_id=1, source_target_pairs={{0,252},{4,8},{8,4},{12,16},{16,12},{20,24},{24,20},{28,32},{32,28... | collective-permute-start | bytes 196616 | tf_op jit(solution)/shard_map/ppermute | solution.py:393
  21.6 7.5 %collective-permute-start.5 = (f32[128,128]{1,0:T(8,128)S(1)}, f32[128,128]{1,0:T(8,128)S(1)}, u32[]{:S(2)}, u32[]{:S(2)}) collective-permute-start(f32[128,128]{1,0:T(8,128)S(1)} %get-tuple-element.83), channel_id=1, source_target_pairs={{0,64},{4,68},{8,72},{12,76},{16,80},{20,84},{24,88},{28,92},{32,9... | collective-permute-start | bytes 196616 | tf_op jit(solution)/shard_map/ppermute | solution.py:393
  23.0 6.1 %collective-permute-start.6 = (f32[128,128]{1,0:T(8,128)S(1)}, f32[128,128]{1,0:T(8,128)S(1)}, u32[]{:S(2)}, u32[]{:S(2)}) collective-permute-start(f32[128,128]{1,0:T(8,128)S(1)} %get-tuple-element.84), channel_id=1, source_target_pairs={{0,192},{4,196},{8,200},{12,204},{16,208},{20,212},{24,216},{28,22... | collective-permute-start | bytes 196616 | tf_op jit(solution)/shard_map/ppermute | solution.py:393
  26.0 3.1 %collective-permute-start.7 = (f32[128,128]{1,0:T(8,128)S(1)}, f32[128,128]{1,0:T(8,128)S(1)}, u32[]{:S(2)}, u32[]{:S(2)}) collective-permute-start(f32[128,128]{1,0:T(8,128)S(1)} %get-tuple-element.85), channel_id=1, source_target_pairs={{0,4},{4,0},{8,12},{12,8},{16,20},{20,16},{24,28},{28,24},{32,36},... | collective-permute-start | bytes 196616 | tf_op jit(solution)/shard_map/ppermute | solution.py:393
  32.1 20.2 %copy-start.6 = (bf16[384,128]{1,0:T(8,128)(2,1)S(1)}, bf16[384,128]{1,0:T(8,128)(2,1)}, u32[]{:S(2)}) copy-start(bf16[384,128]{1,0:T(8,128)(2,1)} %wi_ref.1) | copy-start | bytes 294916
  32.1 4.8 %collective-permute-start.8 = (f32[480,128]{1,0:T(8,128)S(1)}, f32[480,128]{1,0:T(8,128)S(1)}, u32[]{:S(2)}, u32[]{:S(2)}) collective-permute-start(f32[480,128]{1,0:T(8,128)S(1)} %get-tuple-element.103), channel_id=1, source_target_pairs={{0,4},{4,0},{1,5},{5,1},{2,6},{6,2},{3,7},{7,3},{8,12},{12,8},{9,1... | collective-permute-start | bytes 737288 | tf_op jit(solution)/shard_map/ppermute | solution.py:400
  37.0 4.7 %collective-permute-start.11 = (f32[120,128]{1,0:T(8,128)S(1)}, f32[120,128]{1,0:T(8,128)S(1)}, u32[]{:S(2)}, u32[]{:S(2)}) collective-permute-start(f32[120,128]{1,0:T(8,128)S(1)} %get-tuple-element.132), channel_id=1, source_target_pairs={{0,16},{8,24},{16,0},{24,8},{1,17},{9,25},{17,1},{25,9},{2,18},{10... | collective-permute-start | bytes 184328 | tf_op jit(solution)/shard_map/ppermute | solution.py:400
  37.7 6.0 %collective-permute-start.10 = (f32[120,128]{1,0:T(8,128)S(1)}, f32[120,128]{1,0:T(8,128)S(1)}, u32[]{:S(2)}, u32[]{:S(2)}) collective-permute-start(f32[120,128]{1,0:T(8,128)S(1)} %get-tuple-element.133), channel_id=1, source_target_pairs={{0,24},{8,16},{16,8},{24,0},{1,25},{9,17},{17,9},{25,1},{2,26},{10... | collective-permute-start | bytes 184328 | tf_op jit(solution)/shard_map/ppermute | solution.py:400
  38.7 5.0 %collective-permute-start.9 = (f32[120,128]{1,0:T(8,128)S(1)}, f32[120,128]{1,0:T(8,128)S(1)}, u32[]{:S(2)}, u32[]{:S(2)}) collective-permute-start(f32[120,128]{1,0:T(8,128)S(1)} %get-tuple-element.134), channel_id=1, source_target_pairs={{0,8},{8,0},{16,24},{24,16},{1,9},{9,1},{17,25},{25,17},{2,10},{10... | collective-permute-start | bytes 184328 | tf_op jit(solution)/shard_map/ppermute | solution.py:400
  43.7 5.2 %collective-permute-start.14 = (f32[120,128]{1,0:T(8,128)S(1)}, f32[120,128]{1,0:T(8,128)S(1)}, u32[]{:S(2)}, u32[]{:S(2)}) collective-permute-start(f32[120,128]{1,0:T(8,128)S(1)} %fusion), channel_id=1, source_target_pairs={{0,64},{32,96},{64,0},{96,32},{128,192},{160,224},{192,128},{224,1... | collective-permute-start | bytes 184328 | tf_op jit(solution)/shard_map/ppermute | solution.py:400
  45.2 5.5 %collective-permute-start.13 = (f32[120,128]{1,0:T(8,128)S(1)}, f32[120,128]{1,0:T(8,128)S(1)}, u32[]{:S(2)}, u32[]{:S(2)}) collective-permute-start(f32[120,128]{1,0:T(8,128)S(1)} %fusion), channel_id=1, source_target_pairs={{0,96},{32,64},{64,32},{96,0},{128,224},{160,192},{192,160},{224,1... | collective-permute-start | bytes 184328 | tf_op jit(solution)/shard_map/ppermute | solution.py:400
  46.3 4.3 %collective-permute-start.12 = (f32[120,128]{1,0:T(8,128)S(1)}, f32[120,128]{1,0:T(8,128)S(1)}, u32[]{:S(2)}, u32[]{:S(2)}) collective-permute-start(f32[120,128]{1,0:T(8,128)S(1)} %fusion), channel_id=1, source_target_pairs={{0,32},{32,0},{64,96},{96,64},{128,160},{160,128},{192,224},{224,1... | collective-permute-start | bytes 184328 | tf_op jit(solution)/shard_map/ppermute | solution.py:400
  50.7 4.4 %collective-permute-start.15 = (f32[120,128]{1,0:T(8,128)S(1)}, f32[120,128]{1,0:T(8,128)S(1)}, u32[]{:S(2)}, u32[]{:S(2)}) collective-permute-start(f32[120,128]{1,0:T(8,128)S(1)} %add_add_fusion), channel_id=1, source_target_pairs={{0,224},{32,192},{64,160},{96,128},{128,96},{160,64},{192,32},{224... | collective-permute-start | bytes 184328 | tf_op jit(solution)/shard_map/ppermute | solution.py:400
  55.0 4.7 %collective-permute-start.18 = (f32[120,128]{1,0:T(8,128)S(1)}, f32[120,128]{1,0:T(8,128)S(1)}, u32[]{:S(2)}, u32[]{:S(2)}) collective-permute-start(f32[120,128]{1,0:T(8,128)S(1)} %add.31), channel_id=1, source_target_pairs={{0,16},{8,24},{16,0},{24,8},{1,17},{9,25},{17,1},{25,9},{2,18},{10... | collective-permute-start | bytes 184328 | tf_op jit(solution)/shard_map/ppermute | solution.py:400
  56.7 4.3 %collective-permute-start.17 = (f32[120,128]{1,0:T(8,128)S(1)}, f32[120,128]{1,0:T(8,128)S(1)}, u32[]{:S(2)}, u32[]{:S(2)}) collective-permute-start(f32[120,128]{1,0:T(8,128)S(1)} %add.31), channel_id=1, source_target_pairs={{0,24},{8,16},{16,8},{24,0},{1,25},{9,17},{17,9},{25,1},{2,26},{10... | collective-permute-start | bytes 184328 | tf_op jit(solution)/shard_map/ppermute | solution.py:400
  57.8 3.1 %collective-permute-start.16 = (f32[120,128]{1,0:T(8,128)S(1)}, f32[120,128]{1,0:T(8,128)S(1)}, u32[]{:S(2)}, u32[]{:S(2)}) collective-permute-start(f32[120,128]{1,0:T(8,128)S(1)} %add.31), channel_id=1, source_target_pairs={{0,8},{8,0},{16,24},{24,16},{1,9},{9,1},{17,25},{25,17},{2,10},{10... | collective-permute-start | bytes 184328 | tf_op jit(solution)/shard_map/ppermute | solution.py:400
  61.0 6.4 %collective-permute-start.19 = (f32[480,128]{1,0:T(8,128)S(1)}, f32[480,128]{1,0:T(8,128)S(1)}, u32[]{:S(2)}, u32[]{:S(2)}) collective-permute-start(f32[480,128]{1,0:T(8,128)S(1)} %pad_maximum_fusion.refs_0_), channel_id=1, source_target_pairs={{0,4},{4,0},{1,5},{5,1},{2,6},{6,2},{3,7},{7,3},{8,12},{12,8},{9,1... | collective-permute-start | bytes 737288 | tf_op jit(solution)/shard_map/ppermute | solution.py:400
